TPU v7x, 32 devices: a whole 2x2x4 slice. The times are simulated.
32 devices in a mesh: grp: 2 (over x), ep: 8 (over z, y), sub: 2 (over core).
Axes of the slice: x: 2, y: 2, z: 4, core: 2. Of those that a mesh axis runs over, the one named last changes fastest.
Arguments:
- queries: bfloat16 [320, 16, 128], P(('grp', 'ep'), 'sub'), parts along dimension 0
- cache_keys: bfloat16 [320, 2, 384, 128], P(('grp', 'ep'), 'sub'), parts along dimension 0, may hold values from -6 to 6
- cache_values: bfloat16 [320, 2, 384, 128], P(('grp', 'ep'), 'sub'), parts along dimension 0, may hold values from -6 to 6
- new_keys: bfloat16 [320, 2, 128], P(('grp', 'ep'), 'sub'), parts along dimension 0
- new_values: bfloat16 [320, 2, 128], P(('grp', 'ep'), 'sub'), parts along dimension 0, may hold values from -6 to 6
- lengths: int32 [320], P(('grp', 'ep')), parts along dimension 0, may hold values from 1 to 384, as said below
- out_proj: bfloat16 [2048, 2048], P('sub'), may hold values from -1.5 to 1.5
- residual: bfloat16 [320, 2048], P(('grp', 'ep', 'sub')), parts along dimension 0, may hold values from -6 to 6
- norm_gain: float32 [2048], replicated, may hold values from 0.25 to 1.75
- gate_proj: bfloat16 [64, 2048, 768], P(('ep', 'sub')), may hold values from -0.125 to 0.125
- up_proj: bfloat16 [64, 2048, 768], P(('ep', 'sub')), may hold values from -0.125 to 0.125
- down_proj: bfloat16 [64, 768, 2048], P(('ep', 'sub')), may hold values from -0.21875 to 0.21875
- routing: int32 [320, 8], P(('grp', 'ep', 'sub')), parts along dimension 0, may hold values from 0 to 63, all different within a row; in each aligned block of 10 rows (0 to 9, 10 to 19, ...) at most 3 rows name the same one
- route_weights: float32 [320, 8], P(('grp', 'ep', 'sub')), parts along dimension 0, may hold values from 0.05 to 1
Outputs:
- layer_out: bfloat16 [320, 2048], P(('grp', 'ep', 'sub')), parts along dimension 0
There are 2 independent parts, one for each index of `grp`. A program takes and returns all parts, laid end to end along the dimension named above; an argument that names none is the same for every part. Nothing has to cross between parts.
Inputs may be any that keep to these rules, and one draw needn't show every extreme that they name: Slots 0 to lengths - 1 of a request are live; some request has exactly 384. `routing`: each request names 8 different experts; among the 10 requests of one device no expert is named by more than 3, and some device reaches 3.
All inputs are finite; a program needn't handle non-finite values.
Results may differ from a plain program's by a relative error of at most 0.007.
Values may be sent and summed in bfloat16 or wider, within the bound.
No kernel may reach another device: no remote copies, remote signals or barrier semaphores. Data moves between devices by JAX's collectives and lax.ppermute only.
A program may use at most 128 MiB of HBM per device.

v0:
```python
import math

import jax
import jax.numpy as jnp
from jax import lax
from jax.sharding import PartitionSpec as P

EXPERTS = 64
MOST = 3


def per_device(
    queries,
    cache_keys,
    cache_values,
    new_keys,
    new_values,
    lengths,
    out_proj,
    residual,
    norm_gain,
    gate_proj,
    up_proj,
    down_proj,
    routing,
    route_weights,
):
    rows_ep, local_heads, head_dim = queries.shape
    local_kv = cache_keys.shape[1]
    window = cache_keys.shape[2]
    group_size = local_heads // local_kv
    score_scale = 1.0 / math.sqrt(head_dim)
    grouped = queries.reshape(rows_ep, local_kv, group_size, head_dim)
    scores = (
        jnp.einsum("bgqd,bgjd->bgqj", grouped, cache_keys, preferred_element_type=jnp.float32)
        * score_scale
    )
    own_score = (
        jnp.einsum("bgqd,bgd->bgq", grouped, new_keys, preferred_element_type=jnp.float32)
        * score_scale
    )
    valid_mask = lax.broadcasted_iota(jnp.int32, (rows_ep, window), 1) < lengths[:, None]
    scores = jnp.where(valid_mask[:, None, None, :], scores, -1e30)
    top_score = jnp.maximum(jnp.max(scores, -1), own_score)
    weights = jnp.exp(scores - top_score[..., None])
    own_weight = jnp.exp(own_score - top_score)
    denominator = jnp.sum(weights, -1) + own_weight
    mixture = jnp.einsum(
        "bgqj,bgjd->bgqd",
        weights.astype(jnp.bfloat16),
        cache_values,
        preferred_element_type=jnp.float32,
    )
    mixture = mixture + jnp.einsum(
        "bgq,bgd->bgqd",
        own_weight.astype(jnp.bfloat16),
        new_values,
        preferred_element_type=jnp.float32,
    )
    head_out = (
        (mixture / denominator[..., None])
        .reshape(rows_ep, local_heads * head_dim)
        .astype(jnp.bfloat16)
    )
    width = residual.shape[1]
    attended = lax.psum_scatter(
        jnp.dot(head_out, out_proj, preferred_element_type=jnp.float32),
        "sub",
        scatter_dimension=0,
        tiled=True,
    )
    stream = residual.astype(jnp.float32) + attended
    normed = (
        stream * lax.rsqrt(jnp.mean(stream * stream, -1, keepdims=True) + 1e-06) * norm_gain
    ).astype(jnp.bfloat16)
    experts_local = gate_proj.shape[0]
    devices_all = lax.axis_size("ep") * lax.axis_size("sub")
    expert_ids = lax.broadcasted_iota(jnp.int32, (1, 1, EXPERTS), 2)
    expert_hits = jnp.sum((routing[:, :, None] == expert_ids).astype(jnp.int32), 1)
    earlier_hits = jnp.cumsum(expert_hits, 0) - expert_hits
    slot_rank = jnp.take_along_axis(earlier_hits, routing, 1)
    slot_index = routing * MOST + slot_rank
    slot_ids = lax.broadcasted_iota(jnp.int32, (EXPERTS * MOST, 1, 1), 0)
    placing = jnp.sum((slot_index[None, :, :] == slot_ids).astype(jnp.bfloat16), 2)
    outgoing = jnp.dot(placing, normed, preferred_element_type=jnp.float32).astype(jnp.bfloat16)
    outgoing = outgoing.reshape(devices_all, experts_local, MOST, width)
    arriving = lax.all_to_all(outgoing, ("ep", "sub"), split_axis=0, concat_axis=0, tiled=True)
    gate_val = jnp.einsum("sekd,edf->sekf", arriving, gate_proj, preferred_element_type=jnp.float32)
    up_val = jnp.einsum("sekd,edf->sekf", arriving, up_proj, preferred_element_type=jnp.float32)
    hidden = (jax.nn.silu(gate_val) * up_val).astype(jnp.bfloat16)
    answered = jnp.einsum(
        "sekf,efd->sekd", hidden, down_proj, preferred_element_type=jnp.float32
    ).astype(jnp.bfloat16)
    returned = lax.all_to_all(answered, ("ep", "sub"), split_axis=0, concat_axis=0, tiled=True)
    returned = returned.reshape(EXPERTS * MOST, width)
    picked_rows = returned[slot_index].astype(jnp.float32)
    expert_sum = jnp.sum(route_weights[:, :, None] * picked_rows, 1)
    return (stream + expert_sum).astype(jnp.bfloat16)


def solution(mesh):
    return jax.shard_map(
        per_device,
        mesh=mesh,
        in_specs=(
            P(("grp", "ep"), "sub", None),
            P(("grp", "ep"), "sub", None, None),
            P(("grp", "ep"), "sub", None, None),
            P(("grp", "ep"), "sub", None),
            P(("grp", "ep"), "sub", None),
            P(("grp", "ep")),
            P("sub", None),
            P(("grp", "ep", "sub"), None),
            P(),
            P(("ep", "sub"), None, None),
            P(("ep", "sub"), None, None),
            P(("ep", "sub"), None, None),
            P(("grp", "ep", "sub"), None),
            P(("grp", "ep", "sub"), None),
        ),
        out_specs=P(("grp", "ep", "sub"), None),
        check_vma=False,
    )
```

profile of v0, /device:TPU:0, one launch (start us, length us, event | category | flops | bytes accessed | tf_op | source)
XLA Modules:
  0.0 100.9 jit_solution(5853337740614725218)
XLA Ops:
  0.0 0.9 iota_compare_fusion.2
  0.9 1.3 %fusion.60 = f32[20,1,8]{2,1,0:T(1,128)S(1)} fusion(bf16[20,8,128]{2,1,0:T(8,128)(2,1)} %param.14, bf16[20,128,1]{1,0,2:T(8,128)(2,1)} %bitcast.98), kind=kOutput, calls=%fused_computation.49 | convolution fusion | flops 40960 | bytes 46720 | tf_op jit(solution)/shard_map/bgqd,bgd->bgq/dot_general | solution.py:39
  2.2 1.6 %fusion.65 = (f32[20,8]{1,0:T(8,128)S(1)}, f32[20,8,384]{2,1,0:T(8,128)S(1)}) fusion(bf16[20,8,128]{2,1,0:T(8,128)(2,1)} %param.14, bf16[20,1,384,128]{3,2,1,0:T(8,128)(2,1)S(1)} %copy-done, pred[20,384]{1,0:T(8,128)(4,1)S(1)} %iota_compare_fusion.2), kind=kOutput, calls=%fused_computation.60 | convolution fusion | flops 15912800 | bytes 2261120 | tf_op jit(solution)/shard_map/bgqd,bgjd->bgqj/dot_general | solution.py:35
  3.9 0.2 fusion.51
  4.1 0.7 bitcast_convert_fusion
  4.8 2.0 %fusion.41 = bf16[20,8,128]{2,1,0:T(8,128)(2,1)S(1)} fusion(bf16[20,1,384,128]{3,2,1,0:T(8,128)(2,1)} %param.16, f32[20,8,384]{2,1,0:T(8,128)S(1)} %get-tuple-element.10, f32[20,8]{1,0:T(8,128)S(1)} %fusion.59, f32[20,8]{1,0:T(8,128)S(1)} %get-tuple-element.8, f32[20,128]{1,0:T(8,128)S(1)} %bitcast_convert_fusion, f32[20,8]{1,0:T(8,128)S(1)} %get-tuple-element.7), kind=kOutput, calls=%fused_computation.23 | convolution fusion | flops 15933440 | bytes 2264960 | tf_op jit(solution)/shard_map/bgqj,bgjd->bgqd/dot_general | solution.py:48
  6.9 0.7 fusion.66
  7.6 3.4 %fusion = f32[16,2048]{1,0:T(8,128)S(1)} fusion(f32[20,2048]{1,0:T(8,128)S(1)} %fusion.66), kind=kCustom, calls=%all-reduce-scatter | all-reduce-scatter fusion | flops 65537 | bytes 295424
  11.0 2.1 %collective-permute-start = (f32[6,2048]{1,0:T(8,128)S(1)}, f32[6,2048]{1,0:T(8,128)S(1)}, u32[]{:S(2)}, u32[]{:S(2)}) collective-permute-start(f32[6,2048]{1,0:T(8,128)S(1)} %slice.4), channel_id=1, source_target_pairs={{0,1},{2,3},{4,5},{6,7},{8,9},{10,11},{12,13},{14,15},{16,17},{18,... | collective-permute-start | bytes 147464
  13.1 0.1 copy.51
  13.2 0.1 convert_reduce_fusion
  13.5 1.7 %gather_fusion.1 = s32[80]{0:T(128)S(1)} fusion(s32[10,64]{1,0:T(8,128)S(1)} %sub.19, s32[80]{0:T(128)S(1)} %reshape.117), kind=kCustom, calls=%fused_computation.1 | custom fusion | bytes 1280 | tf_op jit(solution)/shard_map/jit(take_along_axis)/gather | solution.py:81
  15.4 0.1 copy.54
  15.5 0.1 fusion.58
  15.6 0.6 dynamic-slice.4
  16.8 0.2 concatenate.3
  17.1 0.1 multiply_reduce_fusion
  17.2 0.5 copy-done.2
  17.7 1.3 %convolution_convert_fusion = bf16[192,2048]{1,0:T(8,128)(2,1)} fusion(bf16[192,10]{0,1:T(8,128)(2,1)S(1)} %fusion.58, f32[2048]{0:T(1024)S(1)} %copy-done.7, f32[10]{0:T(128)S(1)} %add_rsqrt_fusion, f32[22,2048]{1,0:T(8,128)S(1)} %concatenate.3, u32[]{:S(6)} %subtract, bf16[10,2048]{1,0:T(8,128)(2,1)S(1)} %copy-done.4), kind=kOutput, calls=%fused_computation.9 | convolution fusion | flops 8359936 | bytes 999940 | tf_op jit(solution)/shard_map/dot_general | solution.py:85
  19.0 2.4 %reshape.106 = bf16[16,4,3,2048]{3,2,1,0:T(4,128)(2,1)S(1)} reshape(bf16[192,2048]{1,0:T(8,128)(2,1)} %convolution_convert_fusion) | data formatting | bytes 1572864 | tf_op jit(solution)/shard_map/reshape | solution.py:86
  21.5 0.8 copy.55
  22.3 27.2 %all_to_all.10 = bf16[16,4,3,2048]{3,1,2,0:T(4,128)(2,1)S(1)} all-to-all(bf16[16,4,3,2048]{3,1,2,0:T(4,128)(2,1)S(1)} %copy.55), channel_id=1, replica_groups=mesh['grp'=2,'ep'=8,'sub'=2] {'ep','sub'}, dimensions={0} | all-to-all | bytes 1572864 | tf_op jit(solution)/shard_map/all_to_all | solution.py:87
  49.5 8.0 %fusion.17 = f32[16,4,3,768]{3,0,2,1:T(8,128)} fusion(bf16[4,2048,768]{2,1,0:T(8,128)(2,1)} %param.23, bf16[16,4,3,2048]{3,1,2,0:T(4,128)(2,1)S(1)} %all_to_all.10), kind=kOutput, calls=%fused_computation.15 | convolution fusion | flops 603979776 | bytes 13959168 | tf_op jit(solution)/shard_map/sekd,edf->sekf/dot_general | solution.py:88
  57.5 13.3 %fusion.10 = bf16[16,4,3,2048]{3,0,2,1:T(8,128)(2,1)S(1)} fusion(bf16[4,768,2048]{2,1,0:T(8,128)(2,1)} %param.25, bf16[4,2048,768]{2,1,0:T(8,128)(2,1)} %param.24, bf16[16,4,3,2048]{3,1,2,0:T(4,128)(2,1)S(1)} %all_to_all.10, f32[16,4,3,768]{3,0,2,1:T(8,128)} %fusion.17), kind=kOutput, calls=%fused_computation.10 | convolution fusion | flops 1209237504 | bytes 27328512 | tf_op jit(solution)/shard_map/sekf,efd->sekd/dot_general | solution.py:91
  70.8 1.5 %copy.58 = bf16[16,4,3,2048]{3,1,2,0:T(4,128)(2,1)} copy(bf16[16,4,3,2048]{3,0,2,1:T(8,128)(2,1)S(1)} %fusion.10) | data formatting | bytes 1572864 | tf_op jit(solution)/shard_map/convert_element_type | solution.py:93
  72.3 4.1 %all-to-all-start.1 = ((bf16[16,4,3,2048]{3,1,2,0:T(4,128)(2,1)}), bf16[16,4,3,2048]{3,1,2,0:T(4,128)(2,1)S(1)}, u32[]{:S(2)}, u32[]{:S(2)}) async-start(bf16[16,4,3,2048]{3,1,2,0:T(4,128)(2,1)} %copy.58), calls=%async_computation.1 | async-start | bytes 1572864 | tf_op jit(solution)/shard_map/all_to_all | solution.py:94
  76.6 18.4 %all-to-all-done.1 = bf16[16,4,3,2048]{3,1,2,0:T(4,128)(2,1)S(1)} async-done(((bf16[16,4,3,2048]{3,1,2,0:T(4,128)(2,1)}), bf16[16,4,3,2048]{3,1,2,0:T(4,128)(2,1)S(1)}, u32[]{:S(2)}, u32[]{:S(2)}) %all-to-all-start.1) | async-done | bytes 786464 | tf_op jit(solution)/shard_map/all_to_all | solution.py:94
  95.0 1.7 %copy.59 = bf16[16,4,3,2048]{3,2,1,0:T(4,128)(2,1)} copy(bf16[16,4,3,2048]{3,1,2,0:T(4,128)(2,1)S(1)} %all-to-all-done.1) | data formatting | bytes 1572864 | tf_op jit(solution)/shard_map/all_to_all | solution.py:94
  96.7 2.4 %reshape.107 = bf16[192,2048]{1,0:T(8,128)(2,1)S(1)} reshape(bf16[16,4,3,2048]{3,2,1,0:T(4,128)(2,1)} %copy.59) | data formatting | bytes 1572864 | tf_op jit(solution)/shard_map/reshape | solution.py:95
  99.1 0.8 gather_fusion
  99.9 0.3 fusion.46
  100.2 0.7 add_convert_fusion
  (38 shorter events, 0.7 us)
Async XLA Ops:
  0.0 2.2 %copy-start = (bf16[20,1,384,128]{3,2,1,0:T(8,128)(2,1)S(1)}, bf16[20,1,384,128]{3,2,1,0:T(8,128)(2,1)}, u32[]{:S(2)}) copy-start(bf16[20,1,384,128]{3,2,1,0:T(8,128)(2,1)} %param.15) | copy-start | bytes 5898244
  0.0 6.9 %copy-start.1 = (bf16[1024,2048]{1,0:T(8,128)(2,1)S(1)}, bf16[1024,2048]{1,0:T(8,128)(2,1)}, u32[]{:S(2)}) copy-start(bf16[1024,2048]{1,0:T(8,128)(2,1)} %param.20) | copy-start | bytes 12582916
  3.9 9.2 %copy-start.6 = (s32[10,8]{0,1:T(8,128)S(1)}, s32[10,8]{0,1:T(8,128)}, u32[]{:S(2)}) copy-start(s32[10,8]{0,1:T(8,128)} %param.26) | copy-start | bytes 964
  11.0 5.8 %collective-permute-start = (f32[6,2048]{1,0:T(8,128)S(1)}, f32[6,2048]{1,0:T(8,128)S(1)}, u32[]{:S(2)}, u32[]{:S(2)}) collective-permute-start(f32[6,2048]{1,0:T(8,128)S(1)} %slice.4), channel_id=1, source_target_pairs={{0,1},{2,3},{4,5},{6,7},{8,9},{10,11},{12,13},{14,15},{16,17},{18,... | collective-permute-start | bytes 147464
  13.5 2.1 %copy-start.9 = (u32[32]{0:T(128)S(1)}, u32[32]{0:T(128)}, u32[]{:S(2)}) copy-start(u32[32]{0:T(128)} %constant.71) | copy-start | bytes 388
  13.5 3.6 %copy-start.4 = (bf16[10,2048]{1,0:T(8,128)(2,1)S(1)}, bf16[10,2048]{1,0:T(8,128)(2,1)}, u32[]{:S(2)}) copy-start(bf16[10,2048]{1,0:T(8,128)(2,1)} %param.21) | copy-start | bytes 122884
  13.5 4.2 %copy-start.7 = (f32[2048]{0:T(1024)S(1)}, f32[2048]{0:T(1024)}, u32[]{:S(2)}) copy-start(f32[2048]{0:T(1024)} %param.22) | copy-start | bytes 24580
  17.1 0.7 copy-start.2
  57.5 19.0 %copy-start.8 = (f32[10,8]{0,1:T(8,128)S(1)}, f32[10,8]{0,1:T(8,128)}, u32[]{:S(2)}) copy-start(f32[10,8]{0,1:T(8,128)} %param.27) | copy-start | bytes 964
  72.3 27.9 %copy-start.3 = (f32[22,2048]{1,0:T(8,128)S(1)}, f32[22,2048]{1,0:T(8,128)}, u32[]{:S(2)}) copy-start(f32[22,2048]{1,0:T(8,128)} %copy-done.2) | copy-start | bytes 540676
  72.3 28.0 %copy-start.5 = (bf16[10,2048]{1,0:T(8,128)(2,1)S(1)}, bf16[10,2048]{1,0:T(8,128)(2,1)}, u32[]{:S(2)}) copy-start(bf16[10,2048]{1,0:T(8,128)(2,1)} %param.21) | copy-start | bytes 122884
  72.3 22.7 %all-to-all-start.1 = ((bf16[16,4,3,2048]{3,1,2,0:T(4,128)(2,1)}), bf16[16,4,3,2048]{3,1,2,0:T(4,128)(2,1)S(1)}, u32[]{:S(2)}, u32[]{:S(2)}) async-start(bf16[16,4,3,2048]{3,1,2,0:T(4,128)(2,1)} %copy.58), calls=%async_computation.1 | async-start | bytes 1572864 | tf_op jit(solution)/shard_map/all_to_all | solution.py:94
where the time goes:
time: 102 us; the launch traced here: 101 us
  blocking collectives  30.6 us (30%)
  matrix products  28.3 us (28%)
  waiting for transfers between devices  18.4 us (18%)
  local copies, waits for them, and re-layouts  13.4 us (13%)
  starting transfers between devices  6.12 us (6%)
  other arithmetic  3.18 us (3%)
    all_to_all x1, blocking collectives, per_device(): lax.all_to_all(outgoing, ('ep', 'sub'), split_axis=0, concat_axis=0, tile...  27.2 us
    all_to_all x1, waiting for transfers between devices, per_device(): lax.all_to_all(answered, ('ep', 'sub'), split_axis=0, concat_axis=0, tile...  18.4 us
    dot_general x1, matrix products, per_device(): jnp.einsum('sekf,efd->sekd', hidden, down_proj, preferred_element_type=jn...  13.3 us
    dot_general x1, matrix products, per_device(): jnp.einsum('sekd,edf->sekf', arriving, gate_proj, preferred_element_type=...  8 us
    all_to_all x1, starting transfers between devices, per_device(): lax.all_to_all(answered, ('ep', 'sub'), split_axis=0, concat_axis=0, tile...  4.06 us
    unnamed x1, blocking collectives  3.44 us
    reshape x2, local copies, waits for them, and re-layouts, per_device(): outgoing = outgoing.reshape(devices_all, experts_local, MOST, width)  3.25 us
    reshape x1, local copies, waits for them, and re-layouts, per_device(): returned = returned.reshape(EXPERTS * MOST, width)  2.4 us
  transfers between devices with their start and end apart: 2, of which 1 were waited for; matrix products, arithmetic and copies ran while one was open for 3% of the time, Pallas kernels for 0%

commit v1 on v0

v1 whole, which is shorter than its diff:
```python
import functools
import math

import jax
import jax.numpy as jnp
from jax import lax
from jax.experimental import pallas as pl
from jax.experimental.pallas import tpu as pltpu
from jax.sharding import PartitionSpec as P

F32 = jnp.float32
BF16 = jnp.bfloat16
LANES = 128
SUBL = 8

VMEM = pl.BlockSpec(memory_space=pltpu.VMEM)
SMEM = pl.BlockSpec(memory_space=pltpu.SMEM)
HBM = pl.BlockSpec(memory_space=pltpu.HBM)


def dot(a, b):
    return jnp.dot(a, b, preferred_element_type=F32)


def onehot(shape, rows_to_cols):
    r = lax.broadcasted_iota(jnp.int32, shape, 0)
    c = lax.broadcasted_iota(jnp.int32, shape, 1)
    return jnp.where(rows_to_cols(r, c), 1.0, 0.0).astype(BF16)


def attention_kernel(
    n_chunks, sub_ref, len_hbm, q_hbm, nk_hbm, nv_hbm, res_hbm, k_hbm, v_hbm, wo_hbm,
    out_ref, len_ref, q_ref, nk_ref, nv_ref, res_ref, kbuf, vbuf, wobuf, sc_ref, w_ref, mix_ref,
    ho_ref, ssem, ksem, vsem, wsem,
):
    rows, heads, hd = q_ref.shape
    win = kbuf.shape[1]
    per = rows // n_chunks
    scale = 1.0 / math.sqrt(hd)
    half = wobuf.shape[0] // 2
    kcp = [
        pltpu.make_async_copy(k_hbm.at[pl.ds(c * per, per), 0], kbuf.at[pl.ds(c * per, per)], ksem.at[c])
        for c in range(n_chunks)
    ]
    vcp = [
        pltpu.make_async_copy(v_hbm.at[pl.ds(c * per, per), 0], vbuf.at[pl.ds(c * per, per)], vsem.at[c])
        for c in range(n_chunks)
    ]
    wcp = [
        pltpu.make_async_copy(wo_hbm.at[pl.ds(c * half, half)], wobuf.at[pl.ds(c * half, half)], wsem.at[c])
        for c in range(2)
    ]
    small = [
        pltpu.make_async_copy(src, dst, ssem.at[i])
        for i, (src, dst) in enumerate(
            ((q_hbm, q_ref), (len_hbm, len_ref), (nk_hbm, nk_ref), (nv_hbm, nv_ref), (res_hbm, res_ref))
        )
    ]
    for cp in small + kcp + vcp + wcp:
        cp.start()
    for cp in small:
        cp.wait()

    q = q_ref[...].astype(F32)
    own = jnp.sum(q * nk_ref[...].astype(F32)[:, None, :], -1, keepdims=True) * scale
    new_v = nv_ref[...].astype(F32)
    slot = lax.broadcasted_iota(jnp.int32, (heads, win), 1)
    for c in range(n_chunks):
        kcp[c].wait()
        for b in range(c * per, (c + 1) * per):
            s = lax.dot_general(q_ref[b], kbuf[b], (((1,), (1,)), ((), ())), preferred_element_type=F32)
            sc_ref[b] = jnp.where(slot < len_ref[b], s * scale, -1e30)
    for c in range(n_chunks):
        r = pl.ds(c * per, per)
        sc = sc_ref[r]
        own_c = own[c * per : (c + 1) * per]
        top = jnp.maximum(jnp.max(sc, -1, keepdims=True), own_c)
        w = jnp.exp(sc - top)
        ow = jnp.exp(own_c - top)
        den = jnp.sum(w, -1, keepdims=True) + ow
        w_ref[r] = w.astype(BF16)
        owv = ow.astype(BF16).astype(F32) * new_v[c * per : (c + 1) * per, None, :]
        vcp[c].wait()
        for b in range(c * per, (c + 1) * per):
            i = b - c * per
            mix_ref[pl.ds(b * heads, heads)] = (dot(w_ref[b], vbuf[b]) + owv[i]) / den[i]

    dev_rows = rows // 2
    tail = dev_rows - SUBL
    order = [(0, SUBL), (dev_rows, SUBL), (SUBL, tail), (dev_rows + SUBL, tail)]
    for h in range(heads):
        at = 0
        for first, n in order:
            piece = mix_ref[pl.ds(first * heads + h, n, stride=heads), :]
            ho_ref[pl.ds(at, n), pl.ds(h * hd, hd)] = piece
            at += n
    ho = ho_ref[...].astype(BF16)
    wcp[0].wait()
    acc = dot(ho[:, :half], wobuf[:half])
    wcp[1].wait()
    out_ref[...] = acc + dot(ho[:, half:], wobuf[half:])
    sub = sub_ref[0]
    res = res_ref[...].astype(F32)

    @pl.when(sub == 0)
    def _():
        out_ref[pl.ds(0, SUBL)] += res[:SUBL]
        out_ref[pl.ds(2 * SUBL, tail)] += res[SUBL:]

    @pl.when(sub == 1)
    def _():
        out_ref[pl.ds(SUBL, SUBL)] += res[:SUBL]
        out_ref[pl.ds(2 * SUBL + tail, tail)] += res[SUBL:]


def norm_kernel(experts, sub_ref, a_ref, b_ref, gain_ref, route_ref, rw_ref, pay_ref, stream_ref, nrm_ref):
    rows, width = a_ref.shape
    dev_rows = rows // 2
    tail = dev_rows - SUBL
    cols = width // 2
    chunks = 2 * SUBL // (2 * tail)
    cw = cols // chunks
    s0 = sub_ref[0] == 0
    stream = a_ref[...] + b_ref[...]
    mean = jnp.mean(stream * stream, -1, keepdims=True)
    normed = stream * lax.rsqrt(mean + 1e-06) * gain_ref[...]
    nrm_ref[...] = jnp.where(s0, normed[:, :cols], normed[:, cols:])
    main = nrm_ref[pl.ds(0, 2 * SUBL)]
    rest = nrm_ref[pl.ds(2 * SUBL, 2 * tail)]
    folded = jnp.concatenate([rest[:, c * cw : (c + 1) * cw] for c in range(chunks)], 0)
    pay_ref[:, pl.ds(0, cols)] = main.astype(BF16)
    pay_ref[:, pl.ds(cols, cw)] = folded.astype(BF16)
    stream_ref[pl.ds(0, SUBL)] = jnp.where(s0, stream[:SUBL], stream[SUBL : 2 * SUBL])
    stream_ref[pl.ds(SUBL, tail)] = jnp.where(
        s0, stream[2 * SUBL : 2 * SUBL + tail], stream[2 * SUBL + tail :]
    )
    lane = lax.broadcasted_iota(jnp.int32, (dev_rows, 2 * experts), 1)
    which = jnp.where(lane < experts, lane, lane - experts)
    route, rw = route_ref[...], rw_ref[...]
    dense = jnp.zeros((dev_rows, 2 * experts), F32)
    for k in range(route.shape[1]):
        dense += jnp.where(route[:, k : k + 1] == which, rw[:, k : k + 1], 0.0)
    high = dense.astype(BF16).astype(F32)
    pair = jnp.where(lane < experts, high, dense - high)
    pad = jnp.zeros((SUBL - tail, 2 * experts), F32)
    first = jnp.concatenate([pair[:SUBL], pair[SUBL:], pad], 0)
    second = jnp.concatenate([pair[SUBL:], pad, pair[:SUBL]], 0)
    pay_ref[:, pl.ds(cols + cw, 2 * experts)] = jnp.where(s0, first, second).astype(BF16)


def unpack_tokens(x_ref, piece_ref, cols, chunks):
    blocks, br, _ = piece_ref.shape
    tail = br // chunks
    cw = cols // chunks
    x_ref[pl.ds(0, blocks * br)] = piece_ref[:, :, pl.ds(0, cols)].reshape(blocks * br, cols)
    folded = piece_ref[:, :, pl.ds(cols, cw)].reshape(blocks * br, cw)
    for c in range(chunks):
        pick = onehot(
            (blocks * tail, blocks * br),
            lambda r, q: q == (r // tail) * br + c * tail + r % tail,
        )
        x_ref[pl.ds(blocks * br, blocks * tail), pl.ds(c * cw, cw)] = dot(pick, folded).astype(BF16)


def load_kernel(n_src, spans, *refs):
    srcs, outs, sem = refs[:n_src], refs[n_src + 1 : -1], refs[-1]
    copies = [
        pltpu.make_async_copy(srcs[i].at[pl.ds(first, n)], outs[j], sem.at[j])
        for j, (i, first, n) in enumerate(spans)
    ]
    for cp in copies:
        cp.start()
    for cp in copies:
        cp.wait()


def first_half_kernel(
    chunks, sub_ref, piece_ref, ga_ref, gb_ref, ua_ref, up_hbm, g_ref, u_ref, ub_ref, x_ref, sem
):
    n, width, _ = ga_ref.shape
    cols = width // 2
    rest = [pltpu.make_async_copy(up_hbm.at[n + e], ub_ref.at[e], sem.at[e]) for e in range(n)]
    for cp in rest:
        cp.start()
    unpack_tokens(x_ref, piece_ref, cols, chunks)
    at = pl.ds(pl.multiple_of(sub_ref[0] * cols, cols), cols)
    for e in range(n):
        g_ref[e] = dot(x_ref[...], ga_ref[e, at, :])
        u_ref[e] = dot(x_ref[...], ua_ref[e, at, :])
        g_ref[n + e] = dot(x_ref[...], gb_ref[e, at, :])
    for e in range(n):
        rest[e].wait()
        u_ref[n + e] = dot(x_ref[...], ub_ref[e, at, :])


def second_half_kernel(
    chunks, sub_ref, ep_ref, own_ref, oth_ref, g_ref, u_ref, ga_ref, gb_ref, ua_ref, ub_ref, down_hbm,
    keep_ref, send_ref, x_ref, acc_ref, comb_ref, hid_ref, down_ref, sem,
):
    n, _, width = down_ref.shape
    downs = [pltpu.make_async_copy(down_hbm.at[e], down_ref.at[e], sem.at[e]) for e in range(n)]
    for cp in downs:
        cp.start()
    cols = width // 2
    blocks, br, wide = oth_ref.shape
    cw = cols // chunks
    experts = (wide - cols - cw) // 2
    tail = br // chunks
    sub = sub_ref[0]
    s0 = sub == 0
    unpack_tokens(x_ref, oth_ref, cols, chunks)
    at = pl.ds(pl.multiple_of((1 - sub) * cols, cols), cols)

    mine = own_ref[:, :, pl.ds(cols + cw, 2 * experts)]
    other = oth_ref[:, :, pl.ds(cols + cw, 2 * experts)]
    c0 = jnp.where(s0, mine, other)
    c1 = jnp.where(s0, other, mine)
    row = lax.broadcasted_iota(jnp.int32, c0.shape, 1)
    comb_ref[pl.ds(0, blocks * br)] = (
        jnp.where(row < SUBL, c0, c1).astype(F32).reshape(blocks * br, 2 * experts)
    )
    ht = tail // 2
    shape = (blocks * tail, blocks * br)
    pick0 = onehot(shape, lambda r, q: (r % tail < ht) & (q == (r // tail) * br + SUBL + r % tail))
    pick1 = onehot(shape, lambda r, q: (r % tail >= ht) & (q == (r // tail) * br + r % tail - ht))
    comb_ref[pl.ds(blocks * br, blocks * tail)] = dot(
        pick0, c0.reshape(blocks * br, 2 * experts)
    ) + dot(pick1, c1.reshape(blocks * br, 2 * experts))
    lane = lax.broadcasted_iota(jnp.int32, comb_ref.shape, 1)
    first_expert = (2 * ep_ref[0] + sub) * n
    comb = comb_ref[...]
    part = n // 2
    for e in range(n):
        gate_ref, up_ref, i = (ga_ref, ua_ref, e) if e < part else (gb_ref, ub_ref, e - part)
        gate = g_ref[e] + dot(x_ref[...], gate_ref[i, at, :])
        up = u_ref[e] + dot(x_ref[...], up_ref[i, at, :])
        hid_ref[e] = (gate / (1.0 + jnp.exp(-gate)) * up).astype(BF16)
    for e in range(n):
        mine_e = (lane == first_expert + e) | (lane == first_expert + e + experts)
        weight = jnp.sum(jnp.where(mine_e, comb, 0.0), -1, keepdims=True)
        downs[e].wait()
        y = dot(hid_ref[e], down_ref[e]).astype(BF16).astype(F32) * weight
        acc_ref[...] = y if e == 0 else acc_ref[...] + y

    ow = width // (SUBL // ht)
    main = acc_ref[pl.ds(0, blocks * br)].reshape(blocks, 2, SUBL, width)
    m0, m1 = main[:, 0], main[:, 1]
    keep_ref[:, :, pl.ds(0, width)] = jnp.where(s0, m0, m1)
    send_ref[:, :, pl.ds(0, width)] = jnp.where(s0, m1, m0).astype(BF16)
    rest = acc_ref[pl.ds(blocks * br, blocks * tail)].astype(BF16)
    for ref, side in ((keep_ref, sub), (send_ref, 1 - sub)):
        total = jnp.zeros((blocks * SUBL, ow), F32)
        for c in range(SUBL // ht):
            pick = onehot(
                (blocks * SUBL, blocks * tail),
                lambda r, q: ((r % SUBL) // ht == c) & (q == (r // SUBL) * tail + ht * side + r % ht),
            )
            total += dot(pick, rest[:, c * ow : (c + 1) * ow])
        ref[:, :, pl.ds(width, ow)] = total.reshape(blocks, SUBL, ow).astype(ref.dtype)


def finish_kernel(stream_ref, a_ref, b_ref, out_ref):
    dev_rows, width = stream_ref.shape
    tail = dev_rows - SUBL
    chunks = SUBL // tail
    ow = width // chunks
    total = a_ref[...] + b_ref[...].astype(F32)
    out_ref[pl.ds(0, SUBL)] = (stream_ref[pl.ds(0, SUBL)] + total[:, :width]).astype(BF16)
    rest = jnp.concatenate([total[c * tail : (c + 1) * tail, width:] for c in range(chunks)], 1)
    out_ref[pl.ds(SUBL, tail)] = (stream_ref[pl.ds(SUBL, tail)] + rest).astype(BF16)


def params(mib):
    return pltpu.CompilerParams(vmem_limit_bytes=mib << 20)


def per_device(
    queries, cache_keys, cache_values, new_keys, new_values, lengths, out_proj, residual,
    norm_gain, gate_proj, up_proj, down_proj, routing, route_weights,
):
    queries, cache_keys, cache_values, lengths, out_proj, residual, gate_proj, up_proj, down_proj = (
        pltpu.with_memory_space_constraint(x, pltpu.HBM)
        for x in (
            queries, cache_keys, cache_values, lengths, out_proj, residual, gate_proj, up_proj, down_proj
        )
    )
    rows, heads, hd = queries.shape
    win = cache_keys.shape[2]
    width = residual.shape[1]
    dev_rows = residual.shape[0]
    n_ep = lax.axis_size("ep")
    n_exp = gate_proj.shape[0]
    ff = gate_proj.shape[2]
    experts = n_exp * n_ep * lax.axis_size("sub")
    tail = dev_rows - SUBL
    cols = width // 2
    chunks = SUBL // tail
    cw = cols // chunks
    br = 2 * SUBL
    n_chunks = 4
    tokens = n_ep * rows
    sub = lax.axis_index("sub").astype(jnp.int32).reshape(1)
    ep = lax.axis_index("ep").astype(jnp.int32).reshape(1)
    swap = [(0, 1), (1, 0)]

    def to(x, m):
        return lax.ppermute(x, "ep", [(i, i ^ m) for i in range(n_ep)])

    partial = pl.pallas_call(
        functools.partial(attention_kernel, n_chunks),
        in_specs=[SMEM] + [HBM] * 8,
        out_specs=VMEM,
        out_shape=jax.ShapeDtypeStruct((rows, width), F32),
        scratch_shapes=[
            pltpu.SMEM((rows,), jnp.int32),
            pltpu.VMEM(queries.shape, BF16),
            pltpu.VMEM((rows, hd), BF16),
            pltpu.VMEM((rows, hd), BF16),
            pltpu.VMEM(residual.shape, BF16),
            pltpu.VMEM((rows, win, hd), BF16),
            pltpu.VMEM((rows, win, hd), BF16),
            pltpu.VMEM(out_proj.shape, BF16),
            pltpu.VMEM((rows, heads, win), F32),
            pltpu.VMEM((rows, heads, win), BF16),
            pltpu.VMEM((rows * heads, hd), F32),
            pltpu.VMEM((rows, heads * hd), F32),
            pltpu.SemaphoreType.DMA((5,)),
            pltpu.SemaphoreType.DMA((n_chunks,)),
            pltpu.SemaphoreType.DMA((n_chunks,)),
            pltpu.SemaphoreType.DMA((2,)),
        ],
        compiler_params=params(14),
        name="attention",
    )(
        sub, lengths, queries, new_keys.reshape(rows, hd), new_values.reshape(rows, hd), residual,
        cache_keys, cache_values, out_proj,
    )

    from_sibling = lax.ppermute(partial, "sub", swap)
    payload, stream = pl.pallas_call(
        functools.partial(norm_kernel, experts),
        in_specs=[SMEM] + [VMEM] * 5,
        out_specs=(VMEM, VMEM),
        out_shape=(
            jax.ShapeDtypeStruct((br, cols + cw + 2 * experts), BF16),
            jax.ShapeDtypeStruct((dev_rows, width), F32),
        ),
        scratch_shapes=[pltpu.VMEM((rows, cols), F32)],
        compiler_params=params(6),
        name="norm",
    )(sub, partial, from_sibling, norm_gain.reshape(1, width), routing, route_weights)

    part = n_exp // 2
    part_shape = pltpu.VMEM((part, width, ff), BF16)

    def load(srcs, spans, after, name):
        return pl.pallas_call(
            functools.partial(load_kernel, len(srcs), spans),
            in_specs=[HBM] * (len(srcs) + 1),
            out_specs=(VMEM,) * len(spans),
            out_shape=(part_shape,) * len(spans),
            scratch_shapes=[pltpu.SemaphoreType.DMA((len(spans),))],
            compiler_params=params(1),
            cost_estimate=pl.CostEstimate(
                flops=0, transcendentals=0, bytes_accessed=len(spans) * part * width * ff * 2
            ),
            name=name,
        )(*srcs, after)

    pieces = payload[None]
    far = []
    m = n_ep // 2
    while m >= 4:
        far.append(m)
        pieces = jnp.concatenate([pieces, to(pieces, m)], 0)
        m //= 2
    near = list(range(1, min(4, n_ep)))
    (gate_a,) = load((gate_proj,), ((0, 0, part),), payload, "load_first")
    gate_b, up_a = load((gate_proj, up_proj), ((0, part, part), (1, 0, part)), pieces, "load_second")
    pieces = jnp.concatenate([pieces] + [to(pieces, m) for m in near], 0)
    others = lax.ppermute(pieces, "sub", swap)

    half_shape = jax.ShapeDtypeStruct((n_exp, tokens, ff), F32)
    gate_half, up_half, up_b = pl.pallas_call(
        functools.partial(first_half_kernel, chunks),
        in_specs=[SMEM, VMEM, VMEM, VMEM, VMEM, HBM],
        out_specs=(VMEM,) * 3,
        out_shape=(half_shape, half_shape, part_shape),
        scratch_shapes=[pltpu.VMEM((tokens, cols), BF16), pltpu.SemaphoreType.DMA((part,))],
        compiler_params=params(4),
        name="experts_first",
    )(sub, pieces, gate_a, gate_b, up_a, up_proj)

    ow = width // chunks
    keep, send = pl.pallas_call(
        functools.partial(second_half_kernel, chunks),
        in_specs=[SMEM, SMEM] + [VMEM] * 8 + [HBM],
        out_specs=(VMEM, VMEM),
        out_shape=(
            jax.ShapeDtypeStruct((n_ep, SUBL, width + ow), F32),
            jax.ShapeDtypeStruct((n_ep, SUBL, width + ow), BF16),
        ),
        scratch_shapes=[
            pltpu.VMEM((tokens, cols), BF16),
            pltpu.VMEM((tokens, width), F32),
            pltpu.VMEM((tokens, 2 * experts), F32),
            pltpu.VMEM((n_exp, tokens, ff), BF16),
            pltpu.VMEM(down_proj.shape, BF16),
            pltpu.SemaphoreType.DMA((n_exp,)),
        ],
        compiler_params=params(20),
        name="experts_second",
    )(sub, ep, pieces, others, gate_half, up_half, gate_a, gate_b, up_a, up_b, down_proj)

    sums = keep + lax.ppermute(send, "sub", swap).astype(F32)
    size = n_ep // (len(near) + 1)
    arrived = [to(sums[i * size : (i + 1) * size].astype(BF16), m) for i, m in enumerate(near, 1)]
    sums = sums[:size]
    for x in arrived:
        sums = sums + x.astype(F32)
    last = None
    for m in reversed(far):
        size //= 2
        if last is not None:
            sums = sums + last.astype(F32)
        last = to(sums[size:].astype(BF16), m)
        sums = sums[:size]
    if last is None:
        last = jnp.zeros(sums.shape, BF16)

    return pl.pallas_call(
        finish_kernel,
        in_specs=[VMEM] * 3,
        out_specs=VMEM,
        out_shape=jax.ShapeDtypeStruct((dev_rows, width), BF16),
        compiler_params=params(4),
        name="finish",
    )(stream, sums[0], last[0])


def solution(mesh):
    return jax.shard_map(
        per_device,
        mesh=mesh,
        in_specs=(
            P(("grp", "ep"), "sub", None),
            P(("grp", "ep"), "sub", None, None),
            P(("grp", "ep"), "sub", None, None),
            P(("grp", "ep"), "sub", None),
            P(("grp", "ep"), "sub", None),
            P(("grp", "ep")),
            P("sub", None),
            P(("grp", "ep", "sub"), None),
            P(),
            P(("ep", "sub"), None, None),
            P(("ep", "sub"), None, None),
            P(("ep", "sub"), None, None),
            P(("grp", "ep", "sub"), None),
            P(("grp", "ep", "sub"), None),
        ),
        out_specs=P(("grp", "ep", "sub"), None),
        check_vma=False,
    )
```

time: 102 us -> 61.9 us (0.61)
  blocking collectives: 30.6 us -> 0 us
  matrix products: 28.3 us -> 0 us
  Pallas kernels: 0 us -> 26.5 us
  starting transfers between devices: 6.12 us -> 15.1 us
  local copies, waits for them, and re-layouts: 13.4 us -> 4.44 us
  waiting for transfers between devices: 18.4 us -> 15.3 us
  other arithmetic: 3.18 us -> 0.12 us
    dot_general x7 -> x0, matrix products: 28.3 us -> none  [the longest x1 13.3 us: per_device(): jnp.einsum('sekf,efd->sekd', hidden, down_proj, preferred_element_type=jn...]
    all_to_all x1 -> x0, blocking collectives: 27.2 us -> none  [per_device(): lax.all_to_all(outgoing, ('ep', 'sub'), split_axis=0, concat_axis=0, tile...]
    pallas_call x0 -> x7, Pallas kernels: none -> 26.5 us  [the longest x2 7.42 us: load(): pl.pallas_call(functools.partial(load_kernel, len(srcs), spans), in_specs...]
    all_to_all x1 -> x0, waiting for transfers between devices: 18.4 us -> none  [per_device(): lax.all_to_all(answered, ('ep', 'sub'), split_axis=0, concat_axis=0, tile...]
    ppermute x0 -> x11, waiting for transfers between devices: none -> 15.3 us  [the longest x8 13.2 us: to(): return lax.ppermute(x, 'ep', [(i, i ^ m) for i in range(n_ep)])]
    ppermute x0 -> x11, starting transfers between devices: none -> 15.1 us  [the longest x8 13.9 us: to(): return lax.ppermute(x, 'ep', [(i, i ^ m) for i in range(n_ep)])]
    reshape x3 -> x0, local copies, waits for them, and re-layouts: 5.66 us -> none  [the longest x2 3.25 us: per_device(): outgoing = outgoing.reshape(devices_all, experts_local, MOST, width)]
    all_to_all x1 -> x0, starting transfers between devices: 4.06 us -> none  [per_device(): lax.all_to_all(answered, ('ep', 'sub'), split_axis=0, concat_axis=0, tile...]
  transfers between devices with their start and end apart: 2 -> 11, of which waited for: 1 -> 8; matrix products, arithmetic and copies ran while one was open for 3% -> 0% of each run, Pallas kernels for 0% -> 21%
where the time goes in v1:
time: 61.9 us; the launch traced here: 61.6 us
  Pallas kernels  26.5 us (43%)
  waiting for transfers between devices  15.3 us (25%)
  starting transfers between devices  15.1 us (24%)
  local copies, waits for them, and re-layouts  4.44 us (7%)
    ppermute x8, starting transfers between devices, to(): return lax.ppermute(x, 'ep', [(i, i ^ m) for i in range(n_ep)])  13.9 us
    ppermute x8, waiting for transfers between devices, to(): return lax.ppermute(x, 'ep', [(i, i ^ m) for i in range(n_ep)])  13.2 us
    pallas_call x2, Pallas kernels, load(): pl.pallas_call(functools.partial(load_kernel, len(srcs), spans), in_specs...  7.42 us
    pallas_call x1, Pallas kernels, per_device(): pl.pallas_call(functools.partial(second_half_kernel, chunks), in_specs=[S...  6.99 us
    pallas_call x1, Pallas kernels, per_device(): pl.pallas_call(functools.partial(first_half_kernel, chunks), in_specs=[SM...  5.64 us
    pallas_call x1, Pallas kernels, per_device(): pl.pallas_call(functools.partial(attention_kernel, n_chunks), in_specs=[S...  5.6 us
    unnamed x20, local copies, waits for them, and re-layouts  4.4 us
    ppermute x1, waiting for transfers between devices, per_device(): sums = keep + lax.ppermute(send, 'sub', swap).astype(F32)  1.26 us
  transfers between devices with their start and end apart: 11, of which 8 were waited for; matrix products, arithmetic and copies ran while one was open for 0% of the time, Pallas kernels for 21%

profile of v1, /device:TPU:0, one launch (start us, length us, event | category | flops | bytes accessed | tf_op | source)
XLA Modules:
  0.0 61.6 jit_solution(14339733631328033967)
XLA Ops:
  0.0 0.7 %copy-done.3 = bf16[20,1,128]{2,0,1:T(8,128)(2,1)S(1)} copy-done((bf16[20,1,128]{2,0,1:T(8,128)(2,1)S(1)}, bf16[20,1,128]{2,0,1:T(8,128)(2,1)}, u32[]{:S(2)}) %copy-start.3) | copy-done | bytes 5144
  0.7 0.7 %copy-done.4 = bf16[20,1,128]{2,0,1:T(8,128)(2,1)S(1)} copy-done((bf16[20,1,128]{2,0,1:T(8,128)(2,1)S(1)}, bf16[20,1,128]{2,0,1:T(8,128)(2,1)}, u32[]{:S(2)}) %copy-start.4) | copy-done | bytes 5144
  1.4 5.6 %attention.1.a_ref = f32[20,2048]{1,0:T(8,128)S(1)} custom-call(s32[1]{0:T(128)} %bitcast.sub_ref, s32[20]{0:T(128)} %len_hbm.1, bf16[20,8,128]{2,1,0:T(8,128)(2,1)} %q_hbm.1, bf16[20,128]{1,0:T(8,128)(2,1)S(1)} %bitcast.14, bf16[20,128]{1,0:T(8,128)(2,1)S(1)} %bitcast.15, bf16[10,2048]{1,0:T(8,128)(2,1)} %res_hbm.1, bf16[20,1,384,128]{3,2,1,0:T(8,128)(2,1)} %k_hbm.1, ...), custom_call_target="tpu_custom_call" | custom-call | tf_op jit(solution)/shard_map/attention/pallas_call | solution.py:309
  7.0 0.6 collective-permute-start
  7.6 0.1 copy.15.route_ref
  7.7 0.1 copy.16.rw_ref
  7.7 0.9 %collective-permute-done.b_ref = f32[20,2048]{1,0:T(8,128)S(1)} collective-permute-done((f32[20,2048]{1,0:T(8,128)S(1)}, f32[20,2048]{1,0:T(8,128)S(1)}, u32[]{:S(2)}, u32[]{:S(2)}) %collective-permute-start) | collective-permute-done | bytes 163872 | tf_op jit(solution)/shard_map/ppermute | solution.py:339
  8.7 0.2 norm.1
  8.8 4.0 %collective-permute-start.1 = (bf16[1,16,1408]{2,1,0:T(8,128)(2,1)S(1)}, bf16[1,16,1408]{2,1,0:T(8,128)(2,1)S(1)}, u32[]{:S(2)}, u32[]{:S(2)}) collective-permute-start(bf16[1,16,1408]{2,1,0:T(8,128)(2,1)S(1)} %bitcast.10), channel_id=1, source_target_pairs={{0,8},{2,10},{4,12},{6,14},{8,0},{10,2},{12,4},{14,6},{1,9},{3,11}... | collective-permute-start | bytes 135176 | tf_op jit(solution)/shard_map/ppermute | solution.py:307
  12.8 2.0 %collective-permute-done.1 = bf16[1,16,1408]{2,1,0:T(8,128)(2,1)S(1)} collective-permute-done((bf16[1,16,1408]{2,1,0:T(8,128)(2,1)S(1)}, bf16[1,16,1408]{2,1,0:T(8,128)(2,1)S(1)}, u32[]{:S(2)}, u32[]{:S(2)}) %collective-permute-start.1) | collective-permute-done | bytes 45088 | tf_op jit(solution)/shard_map/ppermute | solution.py:307
  14.9 2.9 %collective-permute-start.4 = (bf16[2,16,1408]{2,1,0:T(8,128)(2,1)S(1)}, bf16[2,16,1408]{2,1,0:T(8,128)(2,1)S(1)}, u32[]{:S(2)}, u32[]{:S(2)}) collective-permute-start(bf16[2,16,1408]{2,1,0:T(8,128)(2,1)S(1)} %pad_maximum_fusion.refs_2_), channel_id=1, source_target_pairs={{0,6},{2,4},{4,2},{6,0},{8,14},{10,12},{12,10},{14,8},{1,7},{3,5},... | collective-permute-start | bytes 270344 | tf_op jit(solution)/shard_map/ppermute | solution.py:307
  17.8 0.9 %collective-permute-start.3 = (bf16[2,16,1408]{2,1,0:T(8,128)(2,1)S(1)}, bf16[2,16,1408]{2,1,0:T(8,128)(2,1)S(1)}, u32[]{:S(2)}, u32[]{:S(2)}) collective-permute-start(bf16[2,16,1408]{2,1,0:T(8,128)(2,1)S(1)} %pad_maximum_fusion.refs_2_), channel_id=1, source_target_pairs={{0,4},{2,6},{4,0},{6,2},{8,12},{10,14},{12,8},{14,10},{1,5},{3,7},... | collective-permute-start | bytes 270344 | tf_op jit(solution)/shard_map/ppermute | solution.py:307
  18.7 0.0 collective-permute-start.2
  18.7 4.5 %collective-permute-done.2 = bf16[2,16,1408]{2,1,0:T(8,128)(2,1)S(1)} collective-permute-done((bf16[2,16,1408]{2,1,0:T(8,128)(2,1)S(1)}, bf16[2,16,1408]{2,1,0:T(8,128)(2,1)S(1)}, u32[]{:S(2)}, u32[]{:S(2)}) %collective-permute-start.2) | collective-permute-done | bytes 90144 | tf_op jit(solution)/shard_map/ppermute | solution.py:307
  23.3 0.1 collective-permute-start.5
  23.4 2.8 %load_first.1.ga_ref = bf16[2,2048,768]{2,1,0:T(8,128)(2,1)S(1)} custom-call(bf16[4,2048,768]{2,1,0:T(8,128)(2,1)} %refs_0_.3, bf16[16,1408]{1,0:T(8,128)(2,1)S(1)} %get-tuple-element.15.refs_1_), custom_call_target="tpu_custom_call" | custom-call | bytes 6291456 | tf_op jit(solution)/shard_map/load_first/pallas_call | solution.py:357
  26.2 4.6 %load_second.1 = (bf16[2,2048,768]{2,1,0:T(8,128)(2,1)S(1)}, bf16[2,2048,768]{2,1,0:T(8,128)(2,1)S(1)}) custom-call(bf16[4,2048,768]{2,1,0:T(8,128)(2,1)} %refs_0_.3, bf16[4,2048,768]{2,1,0:T(8,128)(2,1)} %up_hbm.1, bf16[2,16,1408]{2,1,0:T(8,128)(2,1)S(1)} %pad_maximum_fusion.refs_2_), custom_call_target="tpu_custom_call" | custom-call | bytes 12582912 | tf_op jit(solution)/shard_map/load_second/pallas_call | solution.py:357
  30.9 5.6 %experts_first.1 = (f32[4,160,768]{2,1,0:T(8,128)S(1)}, f32[4,160,768]{2,1,0:T(8,128)S(1)}, bf16[2,2048,768]{2,1,0:T(8,128)(2,1)S(1)}) custom-call(s32[1]{0:T(128)} %bitcast.sub_ref, bf16[8,16,1408]{2,1,0:T(8,128)(2,1)S(1)} %constant_dynamic-update-slice_fusion.piece_ref.own_ref, bf16[2,2048,768]{2,1,0:T(8,128)(2,1)S(1)} %load_first.1.ga_ref, ...), custom_call_target="tpu_custom_call" | custom-call | tf_op jit(solution)/shard_map/experts_first/pallas_call | solution.py:384
  36.5 2.8 %copy-done.1 = bf16[2,2048,768]{2,1,0:T(8,128)(2,1)S(1)} copy-done((bf16[2,2048,768]{2,1,0:T(8,128)(2,1)S(1)}, bf16[2,2048,768]{2,1,0:T(8,128)(2,1)}, u32[]{:S(2)}) %copy-start.1) | copy-done | bytes 6291480
  39.3 7.0 %experts_second.1 = (f32[8,8,2560]{2,1,0:T(8,128)S(1)}, bf16[8,8,2560]{2,1,0:T(8,128)(2,1)S(1)}) custom-call(s32[1]{0:T(128)} %bitcast.sub_ref, s32[1]{0:T(128)} %bitcast.4.ep_ref, bf16[8,16,1408]{2,1,0:T(8,128)(2,1)S(1)} %constant_dynamic-update-slice_fusion.piece_ref.own_ref, bf16[8,16,1408]{2,1,0:T(8,128)(2,1)S(1)} %collective-permute-done.5.oth_ref, ...), custom_call_target="tpu_custom_call" | custom-call | tf_op jit(solution)/shard_map/experts_second/pallas_call | solution.py:395
  46.3 0.6 collective-permute-start.6
  46.9 1.3 %collective-permute-done.6 = bf16[8,8,2560]{2,1,0:T(8,128)(2,1)S(1)} collective-permute-done((bf16[8,8,2560]{2,1,0:T(8,128)(2,1)S(1)}, bf16[8,8,2560]{2,1,0:T(8,128)(2,1)S(1)}, u32[]{:S(2)}, u32[]{:S(2)}) %collective-permute-start.6) | collective-permute-done | bytes 327712 | tf_op jit(solution)/shard_map/ppermute | solution.py:415
  48.1 0.1 fusion.2
  48.2 0.4 collective-permute-start.7
  48.7 2.2 %collective-permute-start.9 = (bf16[2,8,2560]{2,1,0:T(8,128)(2,1)S(1)}, bf16[2,8,2560]{2,1,0:T(8,128)(2,1)S(1)}, u32[]{:S(2)}, u32[]{:S(2)}) collective-permute-start(bf16[2,8,2560]{2,1,0:T(8,128)(2,1)S(1)} %get-tuple-element.26), channel_id=1, source_target_pairs={{0,6},{2,4},{4,2},{6,0},{8,14},{10,12},{12,10},{14,8},{1,7},{3,5},... | collective-permute-start | bytes 245768 | tf_op jit(solution)/shard_map/ppermute | solution.py:307
  50.9 0.9 %collective-permute-start.8 = (bf16[2,8,2560]{2,1,0:T(8,128)(2,1)S(1)}, bf16[2,8,2560]{2,1,0:T(8,128)(2,1)S(1)}, u32[]{:S(2)}, u32[]{:S(2)}) collective-permute-start(bf16[2,8,2560]{2,1,0:T(8,128)(2,1)S(1)} %get-tuple-element.27), channel_id=1, source_target_pairs={{0,4},{2,6},{4,0},{6,2},{8,12},{10,14},{12,8},{14,10},{1,5},{3,7},... | collective-permute-start | bytes 245768 | tf_op jit(solution)/shard_map/ppermute | solution.py:307
  51.8 2.9 %collective-permute-done.7 = bf16[2,8,2560]{2,1,0:T(8,128)(2,1)S(1)} collective-permute-done((bf16[2,8,2560]{2,1,0:T(8,128)(2,1)S(1)}, bf16[2,8,2560]{2,1,0:T(8,128)(2,1)S(1)}, u32[]{:S(2)}, u32[]{:S(2)}) %collective-permute-start.7) | collective-permute-done | bytes 81952 | tf_op jit(solution)/shard_map/ppermute | solution.py:307
  54.7 0.2 collective-permute-done.9
  54.9 1.1 %collective-permute-done.8 = bf16[2,8,2560]{2,1,0:T(8,128)(2,1)S(1)} collective-permute-done((bf16[2,8,2560]{2,1,0:T(8,128)(2,1)S(1)}, bf16[2,8,2560]{2,1,0:T(8,128)(2,1)S(1)}, u32[]{:S(2)}, u32[]{:S(2)}) %collective-permute-start.8) | collective-permute-done | bytes 81952 | tf_op jit(solution)/shard_map/ppermute | solution.py:307
  56.0 2.5 %collective-permute-start.10 = (bf16[1,8,2560]{2,1,0:T(8,128)(2,1)S(1)}, bf16[1,8,2560]{2,1,0:T(8,128)(2,1)S(1)}, u32[]{:S(2)}, u32[]{:S(2)}) collective-permute-start(bf16[1,8,2560]{2,1,0:T(8,128)(2,1)S(1)} %slice.41), channel_id=1, source_target_pairs={{0,8},{2,10},{4,12},{6,14},{8,0},{10,2},{12,4},{14,6},{1,9},{3,11}... | collective-permute-start | bytes 122888 | tf_op jit(solution)/shard_map/ppermute | solution.py:307
  58.5 2.5 %collective-permute-done.10 = bf16[1,8,2560]{2,1,0:T(8,128)(2,1)S(1)} collective-permute-done((bf16[1,8,2560]{2,1,0:T(8,128)(2,1)S(1)}, bf16[1,8,2560]{2,1,0:T(8,128)(2,1)S(1)}, u32[]{:S(2)}, u32[]{:S(2)}) %collective-permute-start.10) | collective-permute-done | bytes 40992 | tf_op jit(solution)/shard_map/ppermute | solution.py:307
  61.0 0.7 %finish.1 = bf16[10,2048]{1,0:T(8,128)(2,1)} custom-call(f32[10,2048]{1,0:T(8,128)S(1)} %get-tuple-element.14.stream_ref, f32[8,2560]{1,0:T(8,128)S(1)} %slice_bitcast_fusion.a_ref, bf16[8,2560]{1,0:T(8,128)(2,1)S(1)} %bitcast.12), custom_call_target="tpu_custom_call" | custom-call | tf_op jit(solution)/shard_map/finish/pallas_call | solution.py:431
  (24 shorter events, 0.2 us)
Async XLA Ops:
  0.0 8.6 %copy-start.2 = (f32[2048]{0:T(1024)S(1)}, f32[2048]{0:T(1024)}, u32[]{:S(2)}) copy-start(f32[2048]{0:T(1024)} %param.22) | copy-start | bytes 24580
  0.0 0.7 %copy-start.3 = (bf16[20,1,128]{2,0,1:T(8,128)(2,1)S(1)}, bf16[20,1,128]{2,0,1:T(8,128)(2,1)}, u32[]{:S(2)}) copy-start(bf16[20,1,128]{2,0,1:T(8,128)(2,1)} %param.17) | copy-start | bytes 15364
  0.7 0.7 %copy-start.4 = (bf16[20,1,128]{2,0,1:T(8,128)(2,1)S(1)}, bf16[20,1,128]{2,0,1:T(8,128)(2,1)}, u32[]{:S(2)}) copy-start(bf16[20,1,128]{2,0,1:T(8,128)(2,1)} %param.18) | copy-start | bytes 15364
  1.4 6.2 %copy-start.5 = (s32[10,8]{0,1:T(8,128)S(1)}, s32[10,8]{0,1:T(8,128)}, u32[]{:S(2)}) copy-start(s32[10,8]{0,1:T(8,128)} %param.26) | copy-start | bytes 964
  1.4 6.3 %copy-start.6 = (f32[10,8]{0,1:T(8,128)S(1)}, f32[10,8]{0,1:T(8,128)}, u32[]{:S(2)}) copy-start(f32[10,8]{0,1:T(8,128)} %param.27) | copy-start | bytes 964
  7.0 1.6 %collective-permute-start = (f32[20,2048]{1,0:T(8,128)S(1)}, f32[20,2048]{1,0:T(8,128)S(1)}, u32[]{:S(2)}, u32[]{:S(2)}) collective-permute-start(f32[20,2048]{1,0:T(8,128)S(1)} %attention.1.a_ref), channel_id=1, source_target_pairs={{0,1},{1,0},{2,3},{3,2},{4,5},{5,4},{6,7},{7,6},{8,9},{9,8},{10,11... | collective-permute-start | bytes 491528 | tf_op jit(solution)/shard_map/ppermute | solution.py:339
  8.8 6.0 %collective-permute-start.1 = (bf16[1,16,1408]{2,1,0:T(8,128)(2,1)S(1)}, bf16[1,16,1408]{2,1,0:T(8,128)(2,1)S(1)}, u32[]{:S(2)}, u32[]{:S(2)}) collective-permute-start(bf16[1,16,1408]{2,1,0:T(8,128)(2,1)S(1)} %bitcast.10), channel_id=1, source_target_pairs={{0,8},{2,10},{4,12},{6,14},{8,0},{10,2},{12,4},{14,6},{1,9},{3,11}... | collective-permute-start | bytes 135176 | tf_op jit(solution)/shard_map/ppermute | solution.py:307
  14.9 8.4 %collective-permute-start.4 = (bf16[2,16,1408]{2,1,0:T(8,128)(2,1)S(1)}, bf16[2,16,1408]{2,1,0:T(8,128)(2,1)S(1)}, u32[]{:S(2)}, u32[]{:S(2)}) collective-permute-start(bf16[2,16,1408]{2,1,0:T(8,128)(2,1)S(1)} %pad_maximum_fusion.refs_2_), channel_id=1, source_target_pairs={{0,6},{2,4},{4,2},{6,0},{8,14},{10,12},{12,10},{14,8},{1,7},{3,5},... | collective-permute-start | bytes 270344 | tf_op jit(solution)/shard_map/ppermute | solution.py:307
  17.8 5.5 %collective-permute-start.3 = (bf16[2,16,1408]{2,1,0:T(8,128)(2,1)S(1)}, bf16[2,16,1408]{2,1,0:T(8,128)(2,1)S(1)}, u32[]{:S(2)}, u32[]{:S(2)}) collective-permute-start(bf16[2,16,1408]{2,1,0:T(8,128)(2,1)S(1)} %pad_maximum_fusion.refs_2_), channel_id=1, source_target_pairs={{0,4},{2,6},{4,0},{6,2},{8,12},{10,14},{12,8},{14,10},{1,5},{3,7},... | collective-permute-start | bytes 270344 | tf_op jit(solution)/shard_map/ppermute | solution.py:307
  18.7 4.5 %collective-permute-start.2 = (bf16[2,16,1408]{2,1,0:T(8,128)(2,1)S(1)}, bf16[2,16,1408]{2,1,0:T(8,128)(2,1)S(1)}, u32[]{:S(2)}, u32[]{:S(2)}) collective-permute-start(bf16[2,16,1408]{2,1,0:T(8,128)(2,1)S(1)} %pad_maximum_fusion.refs_2_), channel_id=1, source_target_pairs={{0,2},{2,0},{4,6},{6,4},{8,10},{10,8},{12,14},{14,12},{1,3},{3,1},... | collective-permute-start | bytes 270344 | tf_op jit(solution)/shard_map/ppermute | solution.py:307
  23.3 13.2 %collective-permute-start.5 = (bf16[8,16,1408]{2,1,0:T(8,128)(2,1)S(1)}, bf16[8,16,1408]{2,1,0:T(8,128)(2,1)S(1)}, u32[]{:S(2)}, u32[]{:S(2)}) collective-permute-start(bf16[8,16,1408]{2,1,0:T(8,128)(2,1)S(1)} %constant_dynamic-update-slice_fusion.piece_ref.own_ref), channel_id=1, source_target_pairs={{0,1},{1,0},{2,3},{3,2},{4,5},{5,4},{6,7},{7,6},{8,9},{9,8},{10,11... | collective-permute-start | bytes 1081352 | tf_op jit(solution)/shard_map/ppermute | solution.py:381
  30.9 5.7 %copy-start = (bf16[2,2048,768]{2,1,0:T(8,128)(2,1)}, bf16[2,2048,768]{2,1,0:T(8,128)(2,1)S(1)}, u32[]{:S(2)}) copy-start(bf16[2,2048,768]{2,1,0:T(8,128)(2,1)S(1)} %get-tuple-element.17.ua_ref) | copy-start | bytes 18874372
  36.5 2.8 %copy-start.1 = (bf16[2,2048,768]{2,1,0:T(8,128)(2,1)S(1)}, bf16[2,2048,768]{2,1,0:T(8,128)(2,1)}, u32[]{:S(2)}) copy-start(bf16[2,2048,768]{2,1,0:T(8,128)(2,1)} %copy-done) | copy-start | bytes 18874372
  46.3 1.8 %collective-permute-start.6 = (bf16[8,8,2560]{2,1,0:T(8,128)(2,1)S(1)}, bf16[8,8,2560]{2,1,0:T(8,128)(2,1)S(1)}, u32[]{:S(2)}, u32[]{:S(2)}) collective-permute-start(bf16[8,8,2560]{2,1,0:T(8,128)(2,1)S(1)} %get-tuple-element.22), channel_id=1, source_target_pairs={{0,1},{1,0},{2,3},{3,2},{4,5},{5,4},{6,7},{7,6},{8,9},{9,8},{10,11... | collective-permute-start | bytes 983048 | tf_op jit(solution)/shard_map/ppermute | solution.py:415
  48.2 6.5 %collective-permute-start.7 = (bf16[2,8,2560]{2,1,0:T(8,128)(2,1)S(1)}, bf16[2,8,2560]{2,1,0:T(8,128)(2,1)S(1)}, u32[]{:S(2)}, u32[]{:S(2)}) collective-permute-start(bf16[2,8,2560]{2,1,0:T(8,128)(2,1)S(1)} %get-tuple-element.25), channel_id=1, source_target_pairs={{0,2},{2,0},{4,6},{6,4},{8,10},{10,8},{12,14},{14,12},{1,3},{3,1},... | collective-permute-start | bytes 245768 | tf_op jit(solution)/shard_map/ppermute | solution.py:307
  48.7 6.2 %collective-permute-start.9 = (bf16[2,8,2560]{2,1,0:T(8,128)(2,1)S(1)}, bf16[2,8,2560]{2,1,0:T(8,128)(2,1)S(1)}, u32[]{:S(2)}, u32[]{:S(2)}) collective-permute-start(bf16[2,8,2560]{2,1,0:T(8,128)(2,1)S(1)} %get-tuple-element.26), channel_id=1, source_target_pairs={{0,6},{2,4},{4,2},{6,0},{8,14},{10,12},{12,10},{14,8},{1,7},{3,5},... | collective-permute-start | bytes 245768 | tf_op jit(solution)/shard_map/ppermute | solution.py:307
  50.9 5.1 %collective-permute-start.8 = (bf16[2,8,2560]{2,1,0:T(8,128)(2,1)S(1)}, bf16[2,8,2560]{2,1,0:T(8,128)(2,1)S(1)}, u32[]{:S(2)}, u32[]{:S(2)}) collective-permute-start(bf16[2,8,2560]{2,1,0:T(8,128)(2,1)S(1)} %get-tuple-element.27), channel_id=1, source_target_pairs={{0,4},{2,6},{4,0},{6,2},{8,12},{10,14},{12,8},{14,10},{1,5},{3,7},... | collective-permute-start | bytes 245768 | tf_op jit(solution)/shard_map/ppermute | solution.py:307
  56.0 5.0 %collective-permute-start.10 = (bf16[1,8,2560]{2,1,0:T(8,128)(2,1)S(1)}, bf16[1,8,2560]{2,1,0:T(8,128)(2,1)S(1)}, u32[]{:S(2)}, u32[]{:S(2)}) collective-permute-start(bf16[1,8,2560]{2,1,0:T(8,128)(2,1)S(1)} %slice.41), channel_id=1, source_target_pairs={{0,8},{2,10},{4,12},{6,14},{8,0},{10,2},{12,4},{14,6},{1,9},{3,11}... | collective-permute-start | bytes 122888 | tf_op jit(solution)/shard_map/ppermute | solution.py:307

commit v2 on v1

--- a/solution.py
+++ b/solution.py
@@ -8,9 +8,9 @@
 from jax.experimental.pallas import tpu as pltpu
 from jax.sharding import PartitionSpec as P
 
+
 F32 = jnp.float32
 BF16 = jnp.bfloat16
-LANES = 128
 SUBL = 8
 
 VMEM = pl.BlockSpec(memory_space=pltpu.VMEM)
@@ -29,7 +29,7 @@
 
 
 def attention_kernel(
-    n_chunks, sub_ref, len_hbm, q_hbm, nk_hbm, nv_hbm, res_hbm, k_hbm, v_hbm, wo_hbm,
+    n_chunks, place_ref, len_hbm, q_hbm, nk_hbm, nv_hbm, res_hbm, k_hbm, v_hbm, wo_hbm,
     out_ref, len_ref, q_ref, nk_ref, nv_ref, res_ref, kbuf, vbuf, wobuf, sc_ref, w_ref, mix_ref,
     ho_ref, ssem, ksem, vsem, wsem,
 ):
@@ -99,7 +99,7 @@
     acc = dot(ho[:, :half], wobuf[:half])
     wcp[1].wait()
     out_ref[...] = acc + dot(ho[:, half:], wobuf[half:])
-    sub = sub_ref[0]
+    sub = place_ref[0]
     res = res_ref[...].astype(F32)
 
     @pl.when(sub == 0)
@@ -113,14 +113,14 @@
         out_ref[pl.ds(2 * SUBL + tail, tail)] += res[SUBL:]
 
 
-def norm_kernel(experts, sub_ref, a_ref, b_ref, gain_ref, route_ref, rw_ref, pay_ref, stream_ref, nrm_ref):
+def norm_kernel(experts, place_ref, a_ref, b_ref, gain_ref, route_ref, rw_ref, pay_ref, stream_ref, nrm_ref):
     rows, width = a_ref.shape
     dev_rows = rows // 2
     tail = dev_rows - SUBL
     cols = width // 2
     chunks = 2 * SUBL // (2 * tail)
     cw = cols // chunks
-    s0 = sub_ref[0] == 0
+    s0 = place_ref[0] == 0
     stream = a_ref[...] + b_ref[...]
     mean = jnp.mean(stream * stream, -1, keepdims=True)
     normed = stream * lax.rsqrt(mean + 1e-06) * gain_ref[...]
@@ -175,7 +175,7 @@
 
 
 def first_half_kernel(
-    chunks, sub_ref, piece_ref, ga_ref, gb_ref, ua_ref, up_hbm, g_ref, u_ref, ub_ref, x_ref, sem
+    chunks, place_ref, piece_ref, ga_ref, gb_ref, ua_ref, up_hbm, g_ref, u_ref, ub_ref, x_ref, sem
 ):
     n, width, _ = ga_ref.shape
     cols = width // 2
@@ -183,7 +183,7 @@
     for cp in rest:
         cp.start()
     unpack_tokens(x_ref, piece_ref, cols, chunks)
-    at = pl.ds(pl.multiple_of(sub_ref[0] * cols, cols), cols)
+    at = pl.ds(pl.multiple_of(place_ref[0] * cols, cols), cols)
     for e in range(n):
         g_ref[e] = dot(x_ref[...], ga_ref[e, at, :])
         u_ref[e] = dot(x_ref[...], ua_ref[e, at, :])
@@ -194,7 +194,7 @@
 
 
 def second_half_kernel(
-    chunks, sub_ref, ep_ref, own_ref, oth_ref, g_ref, u_ref, ga_ref, gb_ref, ua_ref, ub_ref, down_hbm,
+    chunks, place_ref, own_ref, oth_ref, g_ref, u_ref, ga_ref, gb_ref, ua_ref, ub_ref, down_hbm,
     keep_ref, send_ref, x_ref, acc_ref, comb_ref, hid_ref, down_ref, sem,
 ):
     n, _, width = down_ref.shape
@@ -206,7 +206,7 @@
     cw = cols // chunks
     experts = (wide - cols - cw) // 2
     tail = br // chunks
-    sub = sub_ref[0]
+    sub = place_ref[0]
     s0 = sub == 0
     unpack_tokens(x_ref, oth_ref, cols, chunks)
     at = pl.ds(pl.multiple_of((1 - sub) * cols, cols), cols)
@@ -227,7 +227,7 @@
         pick0, c0.reshape(blocks * br, 2 * experts)
     ) + dot(pick1, c1.reshape(blocks * br, 2 * experts))
     lane = lax.broadcasted_iota(jnp.int32, comb_ref.shape, 1)
-    first_expert = (2 * ep_ref[0] + sub) * n
+    first_expert = (2 * place_ref[1] + sub) * n
     comb = comb_ref[...]
     part = n // 2
     for e in range(n):
@@ -263,7 +263,6 @@
     dev_rows, width = stream_ref.shape
     tail = dev_rows - SUBL
     chunks = SUBL // tail
-    ow = width // chunks
     total = a_ref[...] + b_ref[...].astype(F32)
     out_ref[pl.ds(0, SUBL)] = (stream_ref[pl.ds(0, SUBL)] + total[:, :width]).astype(BF16)
     rest = jnp.concatenate([total[c * tail : (c + 1) * tail, width:] for c in range(chunks)], 1)
@@ -274,17 +273,13 @@
     return pltpu.CompilerParams(vmem_limit_bytes=mib << 20)
 
 
-def per_device(
+def layer(
     queries, cache_keys, cache_values, new_keys, new_values, lengths, out_proj, residual,
     norm_gain, gate_proj, up_proj, down_proj, routing, route_weights,
 ):
-    queries, cache_keys, cache_values, lengths, out_proj, residual, gate_proj, up_proj, down_proj = (
-        pltpu.with_memory_space_constraint(x, pltpu.HBM)
-        for x in (
-            queries, cache_keys, cache_values, lengths, out_proj, residual, gate_proj, up_proj, down_proj
-        )
-    )
     rows, heads, hd = queries.shape
+    in_hbm = functools.partial(pltpu.with_memory_space_constraint, memory_space=pltpu.HBM)
+    gate_proj, up_proj, down_proj = map(in_hbm, (gate_proj, up_proj, down_proj))
     win = cache_keys.shape[2]
     width = residual.shape[1]
     dev_rows = residual.shape[0]
@@ -299,8 +294,7 @@
     br = 2 * SUBL
     n_chunks = 4
     tokens = n_ep * rows
-    sub = lax.axis_index("sub").astype(jnp.int32).reshape(1)
-    ep = lax.axis_index("ep").astype(jnp.int32).reshape(1)
+    place = jnp.stack([lax.axis_index("sub"), lax.axis_index("ep")]).astype(jnp.int32)
     swap = [(0, 1), (1, 0)]
 
     def to(x, m):
@@ -332,8 +326,14 @@
         compiler_params=params(14),
         name="attention",
     )(
-        sub, lengths, queries, new_keys.reshape(rows, hd), new_values.reshape(rows, hd), residual,
-        cache_keys, cache_values, out_proj,
+        place,
+        *map(
+            in_hbm,
+            (
+                lengths, queries, new_keys.reshape(rows, hd), new_values.reshape(rows, hd), residual,
+                cache_keys, cache_values, out_proj,
+            ),
+        ),
     )
 
     from_sibling = lax.ppermute(partial, "sub", swap)
@@ -348,23 +348,19 @@
         scratch_shapes=[pltpu.VMEM((rows, cols), F32)],
         compiler_params=params(6),
         name="norm",
-    )(sub, partial, from_sibling, norm_gain.reshape(1, width), routing, route_weights)
+    )(place, partial, from_sibling, norm_gain.reshape(1, width), routing, route_weights)
 
     part = n_exp // 2
     part_shape = pltpu.VMEM((part, width, ff), BF16)
 
-    def load(srcs, spans, after, name):
+    def load(srcs, spans, after):
         return pl.pallas_call(
             functools.partial(load_kernel, len(srcs), spans),
             in_specs=[HBM] * (len(srcs) + 1),
             out_specs=(VMEM,) * len(spans),
             out_shape=(part_shape,) * len(spans),
             scratch_shapes=[pltpu.SemaphoreType.DMA((len(spans),))],
-            compiler_params=params(1),
-            cost_estimate=pl.CostEstimate(
-                flops=0, transcendentals=0, bytes_accessed=len(spans) * part * width * ff * 2
-            ),
-            name=name,
+            compiler_params=params(17),
         )(*srcs, after)
 
     pieces = payload[None]
@@ -372,12 +368,16 @@
     m = n_ep // 2
     while m >= 4:
         far.append(m)
-        pieces = jnp.concatenate([pieces, to(pieces, m)], 0)
+        got = to(pieces, m)
+        pieces = jnp.concatenate([pieces, got], 0)
         m //= 2
     near = list(range(1, min(4, n_ep)))
-    (gate_a,) = load((gate_proj,), ((0, 0, part),), payload, "load_first")
-    gate_b, up_a = load((gate_proj, up_proj), ((0, part, part), (1, 0, part)), pieces, "load_second")
-    pieces = jnp.concatenate([pieces] + [to(pieces, m) for m in near], 0)
+    (gate_a,) = load((gate_proj,), ((0, 0, part),), payload)
+    gate_b, up_a = load((gate_proj, up_proj), ((0, part, part), (1, 0, part)), pieces)
+    got = []
+    for m in near:
+        got.append(to(pieces, m))
+    pieces = jnp.concatenate([pieces] + got, 0)
     others = lax.ppermute(pieces, "sub", swap)
 
     half_shape = jax.ShapeDtypeStruct((n_exp, tokens, ff), F32)
@@ -387,14 +387,14 @@
         out_specs=(VMEM,) * 3,
         out_shape=(half_shape, half_shape, part_shape),
         scratch_shapes=[pltpu.VMEM((tokens, cols), BF16), pltpu.SemaphoreType.DMA((part,))],
-        compiler_params=params(4),
+        compiler_params=params(17),
         name="experts_first",
-    )(sub, pieces, gate_a, gate_b, up_a, up_proj)
+    )(place, pieces, gate_a, gate_b, up_a, up_proj)
 
     ow = width // chunks
     keep, send = pl.pallas_call(
         functools.partial(second_half_kernel, chunks),
-        in_specs=[SMEM, SMEM] + [VMEM] * 8 + [HBM],
+        in_specs=[SMEM] + [VMEM] * 8 + [HBM],
         out_specs=(VMEM, VMEM),
         out_shape=(
             jax.ShapeDtypeStruct((n_ep, SUBL, width + ow), F32),
@@ -408,9 +408,9 @@
             pltpu.VMEM(down_proj.shape, BF16),
             pltpu.SemaphoreType.DMA((n_exp,)),
         ],
-        compiler_params=params(20),
+        compiler_params=params(17),
         name="experts_second",
-    )(sub, ep, pieces, others, gate_half, up_half, gate_a, gate_b, up_a, up_b, down_proj)
+    )(place, pieces, others, gate_half, up_half, gate_a, gate_b, up_a, up_b, down_proj)
 
     sums = keep + lax.ppermute(send, "sub", swap).astype(F32)
     size = n_ep // (len(near) + 1)
@@ -439,8 +439,12 @@
 
 
 def solution(mesh):
+    return build(mesh)
+
+
+def build(mesh):
     return jax.shard_map(
-        per_device,
+        layer,
         mesh=mesh,
         in_specs=(
             P(("grp", "ep"), "sub", None),

time: 61.9 us -> 57.5 us (0.929)
  local copies, waits for them, and re-layouts: 4.44 us -> 0.27 us
    unnamed x20 -> x12, local copies, waits for them, and re-layouts: 4.4 us -> 0.22 us
  transfers between devices with their start and end apart: 11 -> 11, of which waited for: 8 -> 8; matrix products, arithmetic and copies ran while one was open for 0% -> 0% of each run, Pallas kernels for 21% -> 20%
where the time goes in v2:
time: 57.5 us; the launch traced here: 57.4 us
  Pallas kernels  26.3 us (46%)
  waiting for transfers between devices  15.3 us (27%)
  starting transfers between devices  15.1 us (26%)
    ppermute x8, starting transfers between devices, to(): return lax.ppermute(x, 'ep', [(i, i ^ m) for i in range(n_ep)])  13.9 us
    ppermute x8, waiting for transfers between devices, to(): return lax.ppermute(x, 'ep', [(i, i ^ m) for i in range(n_ep)])  13.2 us
    pallas_call x1, Pallas kernels, layer(): pl.pallas_call(functools.partial(second_half_kernel, chunks), in_specs=[S...  7.47 us
    pallas_call x2, Pallas kernels, load(): pl.pallas_call(functools.partial(load_kernel, len(srcs), spans), in_specs...  7.42 us
    pallas_call x1, Pallas kernels, layer(): pl.pallas_call(functools.partial(attention_kernel, n_chunks), in_specs=[S...  6.14 us
    pallas_call x1, Pallas kernels, layer(): pl.pallas_call(functools.partial(first_half_kernel, chunks), in_specs=[SM...  3.92 us
    ppermute x1, waiting for transfers between devices, layer(): sums = keep + lax.ppermute(send, 'sub', swap).astype(F32)  1.26 us
  transfers between devices with their start and end apart: 11, of which 8 were waited for; matrix products, arithmetic and copies ran while one was open for 0% of the time, Pallas kernels for 20%

profile of v2, /device:TPU:0, one launch (start us, length us, event | category | flops | bytes accessed | tf_op | source)
XLA Modules:
  0.0 57.4 jit_solution(10767786096833848293)
XLA Ops:
  0.0 0.1 pad_add_fusion.place_ref
  0.1 6.1 %attention.1.a_ref = f32[20,2048]{1,0:T(8,128)S(1)} custom-call(s32[2]{0:T(128)S(1)} %pad_add_fusion.place_ref, s32[20]{0:T(128)} %len_hbm.1, bf16[20,8,128]{2,1,0:T(8,128)(2,1)} %q_hbm.1, bf16[20,128]{1,0:T(8,128)(2,1)} %bitcast.14, bf16[20,128]{1,0:T(8,128)(2,1)} %bitcast.15, bf16[10,2048]{1,0:T(8,128)(2,1)} %res_hbm.1, bf16[20,1,384,128]{3,2,1,0:T(8,128)(2,1)} %k_hbm.1, ...), custom_call_target="tpu_custom_call" | custom-call | tf_op jit(solution)/shard_map/attention/pallas_call | solution.py:303
  6.2 0.6 collective-permute-start
  6.8 0.1 copy.15.route_ref
  6.9 0.1 copy.16.rw_ref
  7.0 0.9 %collective-permute-done.b_ref = f32[20,2048]{1,0:T(8,128)S(1)} collective-permute-done((f32[20,2048]{1,0:T(8,128)S(1)}, f32[20,2048]{1,0:T(8,128)S(1)}, u32[]{:S(2)}, u32[]{:S(2)}) %collective-permute-start) | collective-permute-done | bytes 163872 | tf_op jit(solution)/shard_map/ppermute | solution.py:339
  7.9 0.7 %norm.1 = (bf16[16,1408]{1,0:T(8,128)(2,1)S(1)}, f32[10,2048]{1,0:T(8,128)S(1)}) custom-call(s32[2]{0:T(128)S(1)} %pad_add_fusion.place_ref, f32[20,2048]{1,0:T(8,128)S(1)} %attention.1.a_ref, f32[20,2048]{1,0:T(8,128)S(1)} %collective-permute-done.b_ref, f32[1,2048]{1,0:T(1,128)S(1)} %bitcast.13, s32[10,8]{1,0:T(8,128)S(1)} %copy.15.route_ref, ...), custom_call_target="tpu_custom_call" | custom-call | tf_op jit(solution)/shard_map/norm/pallas_call | solution.py:340
  8.6 4.0 %collective-permute-start.1 = (bf16[1,16,1408]{2,1,0:T(8,128)(2,1)S(1)}, bf16[1,16,1408]{2,1,0:T(8,128)(2,1)S(1)}, u32[]{:S(2)}, u32[]{:S(2)}) collective-permute-start(bf16[1,16,1408]{2,1,0:T(8,128)(2,1)S(1)} %bitcast.10), channel_id=1, source_target_pairs={{0,8},{2,10},{4,12},{6,14},{8,0},{10,2},{12,4},{14,6},{1,9},{3,11}... | collective-permute-start | bytes 135176 | tf_op jit(solution)/shard_map/ppermute | solution.py:301
  12.6 2.0 %collective-permute-done.1 = bf16[1,16,1408]{2,1,0:T(8,128)(2,1)S(1)} collective-permute-done((bf16[1,16,1408]{2,1,0:T(8,128)(2,1)S(1)}, bf16[1,16,1408]{2,1,0:T(8,128)(2,1)S(1)}, u32[]{:S(2)}, u32[]{:S(2)}) %collective-permute-start.1) | collective-permute-done | bytes 45088 | tf_op jit(solution)/shard_map/ppermute | solution.py:301
  14.6 2.9 %collective-permute-start.4 = (bf16[2,16,1408]{2,1,0:T(8,128)(2,1)S(1)}, bf16[2,16,1408]{2,1,0:T(8,128)(2,1)S(1)}, u32[]{:S(2)}, u32[]{:S(2)}) collective-permute-start(bf16[2,16,1408]{2,1,0:T(8,128)(2,1)S(1)} %pad_maximum_fusion.refs_2_), channel_id=1, source_target_pairs={{0,6},{2,4},{4,2},{6,0},{8,14},{10,12},{12,10},{14,8},{1,7},{3,5},... | collective-permute-start | bytes 270344 | tf_op jit(solution)/shard_map/ppermute | solution.py:301
  17.6 0.9 %collective-permute-start.3 = (bf16[2,16,1408]{2,1,0:T(8,128)(2,1)S(1)}, bf16[2,16,1408]{2,1,0:T(8,128)(2,1)S(1)}, u32[]{:S(2)}, u32[]{:S(2)}) collective-permute-start(bf16[2,16,1408]{2,1,0:T(8,128)(2,1)S(1)} %pad_maximum_fusion.refs_2_), channel_id=1, source_target_pairs={{0,4},{2,6},{4,0},{6,2},{8,12},{10,14},{12,8},{14,10},{1,5},{3,7},... | collective-permute-start | bytes 270344 | tf_op jit(solution)/shard_map/ppermute | solution.py:301
  18.5 0.0 collective-permute-start.2
  18.5 4.5 %collective-permute-done.2 = bf16[2,16,1408]{2,1,0:T(8,128)(2,1)S(1)} collective-permute-done((bf16[2,16,1408]{2,1,0:T(8,128)(2,1)S(1)}, bf16[2,16,1408]{2,1,0:T(8,128)(2,1)S(1)}, u32[]{:S(2)}, u32[]{:S(2)}) %collective-permute-start.2) | collective-permute-done | bytes 90144 | tf_op jit(solution)/shard_map/ppermute | solution.py:301
  23.0 0.0 collective-permute-done.3
  23.1 0.1 collective-permute-start.5
  23.2 2.8 %shard_map.136.ga_ref = bf16[2,2048,768]{2,1,0:T(8,128)(2,1)S(1)} custom-call(bf16[4,2048,768]{2,1,0:T(8,128)(2,1)} %refs_0_.3, bf16[16,1408]{1,0:T(8,128)(2,1)S(1)} %get-tuple-element.15.refs_1_), custom_call_target="tpu_custom_call" | custom-call | tf_op jit(solution)/shard_map/pallas_call | solution.py:357
  26.0 4.6 %shard_map.137 = (bf16[2,2048,768]{2,1,0:T(8,128)(2,1)S(1)}, bf16[2,2048,768]{2,1,0:T(8,128)(2,1)S(1)}) custom-call(bf16[4,2048,768]{2,1,0:T(8,128)(2,1)} %refs_0_.3, bf16[4,2048,768]{2,1,0:T(8,128)(2,1)} %up_hbm.1, bf16[2,16,1408]{2,1,0:T(8,128)(2,1)S(1)} %pad_maximum_fusion.refs_2_), custom_call_target="tpu_custom_call" | custom-call | tf_op jit(solution)/shard_map/pallas_call | solution.py:357
  30.6 3.9 %experts_first.1 = (f32[4,160,768]{2,1,0:T(8,128)S(1)}, f32[4,160,768]{2,1,0:T(8,128)S(1)}, bf16[2,2048,768]{2,1,0:T(8,128)(2,1)S(1)}) custom-call(s32[2]{0:T(128)S(1)} %pad_add_fusion.place_ref, bf16[8,16,1408]{2,1,0:T(8,128)(2,1)S(1)} %constant_dynamic-update-slice_fusion.piece_ref.own_ref, bf16[2,2048,768]{2,1,0:T(8,128)(2,1)S(1)} %shard_map.136.ga_ref, ...), custom_call_target="tpu_custom_call" | custom-call | tf_op jit(solution)/shard_map/experts_first/pallas_call | solution.py:384
  34.5 0.0 collective-permute-done.5.oth_ref
  34.6 7.5 %experts_second.1 = (f32[8,8,2560]{2,1,0:T(8,128)S(1)}, bf16[8,8,2560]{2,1,0:T(8,128)(2,1)S(1)}) custom-call(s32[2]{0:T(128)S(1)} %pad_add_fusion.place_ref, bf16[8,16,1408]{2,1,0:T(8,128)(2,1)S(1)} %constant_dynamic-update-slice_fusion.piece_ref.own_ref, bf16[8,16,1408]{2,1,0:T(8,128)(2,1)S(1)} %collective-permute-done.5.oth_ref, ...), custom_call_target="tpu_custom_call" | custom-call | tf_op jit(solution)/shard_map/experts_second/pallas_call | solution.py:395
  42.0 0.6 collective-permute-start.6
  42.6 1.3 %collective-permute-done.6 = bf16[8,8,2560]{2,1,0:T(8,128)(2,1)S(1)} collective-permute-done((bf16[8,8,2560]{2,1,0:T(8,128)(2,1)S(1)}, bf16[8,8,2560]{2,1,0:T(8,128)(2,1)S(1)}, u32[]{:S(2)}, u32[]{:S(2)}) %collective-permute-start.6) | collective-permute-done | bytes 327712 | tf_op jit(solution)/shard_map/ppermute | solution.py:415
  43.8 0.1 fusion.2
  44.0 0.5 collective-permute-start.7
  44.4 2.1 %collective-permute-start.9 = (bf16[2,8,2560]{2,1,0:T(8,128)(2,1)S(1)}, bf16[2,8,2560]{2,1,0:T(8,128)(2,1)S(1)}, u32[]{:S(2)}, u32[]{:S(2)}) collective-permute-start(bf16[2,8,2560]{2,1,0:T(8,128)(2,1)S(1)} %get-tuple-element.26), channel_id=1, source_target_pairs={{0,6},{2,4},{4,2},{6,0},{8,14},{10,12},{12,10},{14,8},{1,7},{3,5},... | collective-permute-start | bytes 245768 | tf_op jit(solution)/shard_map/ppermute | solution.py:301
  46.6 0.9 %collective-permute-start.8 = (bf16[2,8,2560]{2,1,0:T(8,128)(2,1)S(1)}, bf16[2,8,2560]{2,1,0:T(8,128)(2,1)S(1)}, u32[]{:S(2)}, u32[]{:S(2)}) collective-permute-start(bf16[2,8,2560]{2,1,0:T(8,128)(2,1)S(1)} %get-tuple-element.27), channel_id=1, source_target_pairs={{0,4},{2,6},{4,0},{6,2},{8,12},{10,14},{12,8},{14,10},{1,5},{3,7},... | collective-permute-start | bytes 245768 | tf_op jit(solution)/shard_map/ppermute | solution.py:301
  47.5 2.9 %collective-permute-done.7 = bf16[2,8,2560]{2,1,0:T(8,128)(2,1)S(1)} collective-permute-done((bf16[2,8,2560]{2,1,0:T(8,128)(2,1)S(1)}, bf16[2,8,2560]{2,1,0:T(8,128)(2,1)S(1)}, u32[]{:S(2)}, u32[]{:S(2)}) %collective-permute-start.7) | collective-permute-done | bytes 81952 | tf_op jit(solution)/shard_map/ppermute | solution.py:301
  50.4 0.2 collective-permute-done.9
  50.6 1.1 %collective-permute-done.8 = bf16[2,8,2560]{2,1,0:T(8,128)(2,1)S(1)} collective-permute-done((bf16[2,8,2560]{2,1,0:T(8,128)(2,1)S(1)}, bf16[2,8,2560]{2,1,0:T(8,128)(2,1)S(1)}, u32[]{:S(2)}, u32[]{:S(2)}) %collective-permute-start.8) | collective-permute-done | bytes 81952 | tf_op jit(solution)/shard_map/ppermute | solution.py:301
  51.7 2.5 %collective-permute-start.10 = (bf16[1,8,2560]{2,1,0:T(8,128)(2,1)S(1)}, bf16[1,8,2560]{2,1,0:T(8,128)(2,1)S(1)}, u32[]{:S(2)}, u32[]{:S(2)}) collective-permute-start(bf16[1,8,2560]{2,1,0:T(8,128)(2,1)S(1)} %slice.41), channel_id=1, source_target_pairs={{0,8},{2,10},{4,12},{6,14},{8,0},{10,2},{12,4},{14,6},{1,9},{3,11}... | collective-permute-start | bytes 122888 | tf_op jit(solution)/shard_map/ppermute | solution.py:301
  54.3 2.5 %collective-permute-done.10 = bf16[1,8,2560]{2,1,0:T(8,128)(2,1)S(1)} collective-permute-done((bf16[1,8,2560]{2,1,0:T(8,128)(2,1)S(1)}, bf16[1,8,2560]{2,1,0:T(8,128)(2,1)S(1)}, u32[]{:S(2)}, u32[]{:S(2)}) %collective-permute-start.10) | collective-permute-done | bytes 40992 | tf_op jit(solution)/shard_map/ppermute | solution.py:301
  56.7 0.6 %finish.1 = bf16[10,2048]{1,0:T(8,128)(2,1)} custom-call(f32[10,2048]{1,0:T(8,128)S(1)} %get-tuple-element.14.stream_ref, f32[8,2560]{1,0:T(8,128)S(1)} %slice_bitcast_fusion.a_ref, bf16[8,2560]{1,0:T(8,128)(2,1)S(1)} %bitcast.12), custom_call_target="tpu_custom_call" | custom-call | tf_op jit(solution)/shard_map/finish/pallas_call | solution.py:431
  (17 shorter events, 0.2 us)
Async XLA Ops:
  0.0 6.8 %copy-start.1 = (s32[10,8]{0,1:T(8,128)S(1)}, s32[10,8]{0,1:T(8,128)}, u32[]{:S(2)}) copy-start(s32[10,8]{0,1:T(8,128)} %param.26) | copy-start | bytes 964
  0.0 6.9 %copy-start.2 = (f32[10,8]{0,1:T(8,128)S(1)}, f32[10,8]{0,1:T(8,128)}, u32[]{:S(2)}) copy-start(f32[10,8]{0,1:T(8,128)} %param.27) | copy-start | bytes 964
  0.0 7.9 %copy-start = (f32[2048]{0:T(1024)S(1)}, f32[2048]{0:T(1024)}, u32[]{:S(2)}) copy-start(f32[2048]{0:T(1024)} %param.22) | copy-start | bytes 24580
  6.2 1.6 %collective-permute-start = (f32[20,2048]{1,0:T(8,128)S(1)}, f32[20,2048]{1,0:T(8,128)S(1)}, u32[]{:S(2)}, u32[]{:S(2)}) collective-permute-start(f32[20,2048]{1,0:T(8,128)S(1)} %attention.1.a_ref), channel_id=1, source_target_pairs={{0,1},{1,0},{2,3},{3,2},{4,5},{5,4},{6,7},{7,6},{8,9},{9,8},{10,11... | collective-permute-start | bytes 491528 | tf_op jit(solution)/shard_map/ppermute | solution.py:339
  8.6 6.0 %collective-permute-start.1 = (bf16[1,16,1408]{2,1,0:T(8,128)(2,1)S(1)}, bf16[1,16,1408]{2,1,0:T(8,128)(2,1)S(1)}, u32[]{:S(2)}, u32[]{:S(2)}) collective-permute-start(bf16[1,16,1408]{2,1,0:T(8,128)(2,1)S(1)} %bitcast.10), channel_id=1, source_target_pairs={{0,8},{2,10},{4,12},{6,14},{8,0},{10,2},{12,4},{14,6},{1,9},{3,11}... | collective-permute-start | bytes 135176 | tf_op jit(solution)/shard_map/ppermute | solution.py:301
  14.6 8.4 %collective-permute-start.4 = (bf16[2,16,1408]{2,1,0:T(8,128)(2,1)S(1)}, bf16[2,16,1408]{2,1,0:T(8,128)(2,1)S(1)}, u32[]{:S(2)}, u32[]{:S(2)}) collective-permute-start(bf16[2,16,1408]{2,1,0:T(8,128)(2,1)S(1)} %pad_maximum_fusion.refs_2_), channel_id=1, source_target_pairs={{0,6},{2,4},{4,2},{6,0},{8,14},{10,12},{12,10},{14,8},{1,7},{3,5},... | collective-permute-start | bytes 270344 | tf_op jit(solution)/shard_map/ppermute | solution.py:301
  17.6 5.5 %collective-permute-start.3 = (bf16[2,16,1408]{2,1,0:T(8,128)(2,1)S(1)}, bf16[2,16,1408]{2,1,0:T(8,128)(2,1)S(1)}, u32[]{:S(2)}, u32[]{:S(2)}) collective-permute-start(bf16[2,16,1408]{2,1,0:T(8,128)(2,1)S(1)} %pad_maximum_fusion.refs_2_), channel_id=1, source_target_pairs={{0,4},{2,6},{4,0},{6,2},{8,12},{10,14},{12,8},{14,10},{1,5},{3,7},... | collective-permute-start | bytes 270344 | tf_op jit(solution)/shard_map/ppermute | solution.py:301
  18.5 4.5 %collective-permute-start.2 = (bf16[2,16,1408]{2,1,0:T(8,128)(2,1)S(1)}, bf16[2,16,1408]{2,1,0:T(8,128)(2,1)S(1)}, u32[]{:S(2)}, u32[]{:S(2)}) collective-permute-start(bf16[2,16,1408]{2,1,0:T(8,128)(2,1)S(1)} %pad_maximum_fusion.refs_2_), channel_id=1, source_target_pairs={{0,2},{2,0},{4,6},{6,4},{8,10},{10,8},{12,14},{14,12},{1,3},{3,1},... | collective-permute-start | bytes 270344 | tf_op jit(solution)/shard_map/ppermute | solution.py:301
  23.1 11.5 %collective-permute-start.5 = (bf16[8,16,1408]{2,1,0:T(8,128)(2,1)S(1)}, bf16[8,16,1408]{2,1,0:T(8,128)(2,1)S(1)}, u32[]{:S(2)}, u32[]{:S(2)}) collective-permute-start(bf16[8,16,1408]{2,1,0:T(8,128)(2,1)S(1)} %constant_dynamic-update-slice_fusion.piece_ref.own_ref), channel_id=1, source_target_pairs={{0,1},{1,0},{2,3},{3,2},{4,5},{5,4},{6,7},{7,6},{8,9},{9,8},{10,11... | collective-permute-start | bytes 1081352 | tf_op jit(solution)/shard_map/ppermute | solution.py:381
  42.0 1.8 %collective-permute-start.6 = (bf16[8,8,2560]{2,1,0:T(8,128)(2,1)S(1)}, bf16[8,8,2560]{2,1,0:T(8,128)(2,1)S(1)}, u32[]{:S(2)}, u32[]{:S(2)}) collective-permute-start(bf16[8,8,2560]{2,1,0:T(8,128)(2,1)S(1)} %get-tuple-element.22), channel_id=1, source_target_pairs={{0,1},{1,0},{2,3},{3,2},{4,5},{5,4},{6,7},{7,6},{8,9},{9,8},{10,11... | collective-permute-start | bytes 983048 | tf_op jit(solution)/shard_map/ppermute | solution.py:415
  44.0 6.4 %collective-permute-start.7 = (bf16[2,8,2560]{2,1,0:T(8,128)(2,1)S(1)}, bf16[2,8,2560]{2,1,0:T(8,128)(2,1)S(1)}, u32[]{:S(2)}, u32[]{:S(2)}) collective-permute-start(bf16[2,8,2560]{2,1,0:T(8,128)(2,1)S(1)} %get-tuple-element.25), channel_id=1, source_target_pairs={{0,2},{2,0},{4,6},{6,4},{8,10},{10,8},{12,14},{14,12},{1,3},{3,1},... | collective-permute-start | bytes 245768 | tf_op jit(solution)/shard_map/ppermute | solution.py:301
  44.4 6.2 %collective-permute-start.9 = (bf16[2,8,2560]{2,1,0:T(8,128)(2,1)S(1)}, bf16[2,8,2560]{2,1,0:T(8,128)(2,1)S(1)}, u32[]{:S(2)}, u32[]{:S(2)}) collective-permute-start(bf16[2,8,2560]{2,1,0:T(8,128)(2,1)S(1)} %get-tuple-element.26), channel_id=1, source_target_pairs={{0,6},{2,4},{4,2},{6,0},{8,14},{10,12},{12,10},{14,8},{1,7},{3,5},... | collective-permute-start | bytes 245768 | tf_op jit(solution)/shard_map/ppermute | solution.py:301
  46.6 5.1 %collective-permute-start.8 = (bf16[2,8,2560]{2,1,0:T(8,128)(2,1)S(1)}, bf16[2,8,2560]{2,1,0:T(8,128)(2,1)S(1)}, u32[]{:S(2)}, u32[]{:S(2)}) collective-permute-start(bf16[2,8,2560]{2,1,0:T(8,128)(2,1)S(1)} %get-tuple-element.27), channel_id=1, source_target_pairs={{0,4},{2,6},{4,0},{6,2},{8,12},{10,14},{12,8},{14,10},{1,5},{3,7},... | collective-permute-start | bytes 245768 | tf_op jit(solution)/shard_map/ppermute | solution.py:301
  51.7 5.0 %collective-permute-start.10 = (bf16[1,8,2560]{2,1,0:T(8,128)(2,1)S(1)}, bf16[1,8,2560]{2,1,0:T(8,128)(2,1)S(1)}, u32[]{:S(2)}, u32[]{:S(2)}) collective-permute-start(bf16[1,8,2560]{2,1,0:T(8,128)(2,1)S(1)} %slice.41), channel_id=1, source_target_pairs={{0,8},{2,10},{4,12},{6,14},{8,0},{10,2},{12,4},{14,6},{1,9},{3,11}... | collective-permute-start | bytes 122888 | tf_op jit(solution)/shard_map/ppermute | solution.py:301

commit v3 on v2

--- a/solution.py
+++ b/solution.py
@@ -29,7 +29,7 @@
 
 
 def attention_kernel(
-    n_chunks, place_ref, len_hbm, q_hbm, nk_hbm, nv_hbm, res_hbm, k_hbm, v_hbm, wo_hbm,
+    n_chunks, len_hbm, q_hbm, nk_hbm, nv_hbm, res_hbm, k_hbm, v_hbm, wo_hbm,
     out_ref, len_ref, q_ref, nk_ref, nv_ref, res_ref, kbuf, vbuf, wobuf, sc_ref, w_ref, mix_ref,
     ho_ref, ssem, ksem, vsem, wsem,
 ):
@@ -99,7 +99,7 @@
     acc = dot(ho[:, :half], wobuf[:half])
     wcp[1].wait()
     out_ref[...] = acc + dot(ho[:, half:], wobuf[half:])
-    sub = place_ref[0]
+    sub = lax.axis_index("sub")
     res = res_ref[...].astype(F32)
 
     @pl.when(sub == 0)
@@ -113,14 +113,14 @@
         out_ref[pl.ds(2 * SUBL + tail, tail)] += res[SUBL:]
 
 
-def norm_kernel(experts, place_ref, a_ref, b_ref, gain_ref, route_ref, rw_ref, pay_ref, stream_ref, nrm_ref):
+def norm_kernel(experts, a_ref, b_ref, gain_ref, route_ref, rw_ref, _g, _u, _d, pay_ref, stream_ref, nrm_ref):
     rows, width = a_ref.shape
     dev_rows = rows // 2
     tail = dev_rows - SUBL
     cols = width // 2
     chunks = 2 * SUBL // (2 * tail)
     cw = cols // chunks
-    s0 = place_ref[0] == 0
+    s0 = lax.axis_index("sub") == 0
     stream = a_ref[...] + b_ref[...]
     mean = jnp.mean(stream * stream, -1, keepdims=True)
     normed = stream * lax.rsqrt(mean + 1e-06) * gain_ref[...]
@@ -148,6 +148,25 @@
     pay_ref[:, pl.ds(cols + cw, 2 * experts)] = jnp.where(s0, first, second).astype(BF16)
 
 
+def join_kernel(*refs):
+    out_ref, at = refs[-1], 0
+    for ref in refs[:-1]:
+        n = ref.shape[0]
+        out_ref[pl.ds(at, n)] = ref[...]
+        at += n
+
+
+def join(arrays):
+    rows = sum(x.shape[0] for x in arrays)
+    return pl.pallas_call(
+        join_kernel,
+        in_specs=[VMEM] * len(arrays),
+        out_specs=VMEM,
+        out_shape=jax.ShapeDtypeStruct((rows,) + arrays[0].shape[1:], arrays[0].dtype),
+        compiler_params=params(4),
+    )(*arrays)
+
+
 def unpack_tokens(x_ref, piece_ref, cols, chunks):
     blocks, br, _ = piece_ref.shape
     tail = br // chunks
@@ -162,55 +181,36 @@
         x_ref[pl.ds(blocks * br, blocks * tail), pl.ds(c * cw, cw)] = dot(pick, folded).astype(BF16)
 
 
-def load_kernel(n_src, spans, *refs):
-    srcs, outs, sem = refs[:n_src], refs[n_src + 1 : -1], refs[-1]
-    copies = [
-        pltpu.make_async_copy(srcs[i].at[pl.ds(first, n)], outs[j], sem.at[j])
-        for j, (i, first, n) in enumerate(spans)
-    ]
-    for cp in copies:
-        cp.start()
-    for cp in copies:
-        cp.wait()
-
-
-def first_half_kernel(
-    chunks, place_ref, piece_ref, ga_ref, gb_ref, ua_ref, up_hbm, g_ref, u_ref, ub_ref, x_ref, sem
-):
-    n, width, _ = ga_ref.shape
+def first_half_kernel(chunks, piece_ref, gate_ref, up_ref, g_ref, u_ref, x_ref):
+    n, width, _ = gate_ref.shape
     cols = width // 2
-    rest = [pltpu.make_async_copy(up_hbm.at[n + e], ub_ref.at[e], sem.at[e]) for e in range(n)]
-    for cp in rest:
-        cp.start()
     unpack_tokens(x_ref, piece_ref, cols, chunks)
-    at = pl.ds(pl.multiple_of(place_ref[0] * cols, cols), cols)
+    at = pl.ds(pl.multiple_of(lax.axis_index("sub") * cols, cols), cols)
     for e in range(n):
-        g_ref[e] = dot(x_ref[...], ga_ref[e, at, :])
-        u_ref[e] = dot(x_ref[...], ua_ref[e, at, :])
-        g_ref[n + e] = dot(x_ref[...], gb_ref[e, at, :])
+        g_ref[e] = dot(x_ref[...], gate_ref[e, at, :])
+        u_ref[e] = dot(x_ref[...], up_ref[e, at, :])
+
+
+def second_half_kernel(chunks, oth_ref, g_ref, u_ref, gate_ref, up_ref, hid_ref, x_ref):
+    n, width, _ = gate_ref.shape
+    cols = width // 2
+    unpack_tokens(x_ref, oth_ref, cols, chunks)
+    at = pl.ds(pl.multiple_of((1 - lax.axis_index("sub")) * cols, cols), cols)
     for e in range(n):
-        rest[e].wait()
-        u_ref[n + e] = dot(x_ref[...], ub_ref[e, at, :])
-
-
-def second_half_kernel(
-    chunks, place_ref, own_ref, oth_ref, g_ref, u_ref, ga_ref, gb_ref, ua_ref, ub_ref, down_hbm,
-    keep_ref, send_ref, x_ref, acc_ref, comb_ref, hid_ref, down_ref, sem,
-):
+        gate = g_ref[e] + dot(x_ref[...], gate_ref[e, at, :])
+        up = u_ref[e] + dot(x_ref[...], up_ref[e, at, :])
+        hid_ref[e] = (gate / (1.0 + jnp.exp(-gate)) * up).astype(BF16)
+
+
+def third_kernel(chunks, own_ref, oth_ref, hid_ref, down_ref, keep_ref, send_ref, acc_ref, comb_ref):
     n, _, width = down_ref.shape
-    downs = [pltpu.make_async_copy(down_hbm.at[e], down_ref.at[e], sem.at[e]) for e in range(n)]
-    for cp in downs:
-        cp.start()
     cols = width // 2
     blocks, br, wide = oth_ref.shape
     cw = cols // chunks
     experts = (wide - cols - cw) // 2
     tail = br // chunks
-    sub = place_ref[0]
+    sub = lax.axis_index("sub")
     s0 = sub == 0
-    unpack_tokens(x_ref, oth_ref, cols, chunks)
-    at = pl.ds(pl.multiple_of((1 - sub) * cols, cols), cols)
-
     mine = own_ref[:, :, pl.ds(cols + cw, 2 * experts)]
     other = oth_ref[:, :, pl.ds(cols + cw, 2 * experts)]
     c0 = jnp.where(s0, mine, other)
@@ -227,18 +227,11 @@
         pick0, c0.reshape(blocks * br, 2 * experts)
     ) + dot(pick1, c1.reshape(blocks * br, 2 * experts))
     lane = lax.broadcasted_iota(jnp.int32, comb_ref.shape, 1)
-    first_expert = (2 * place_ref[1] + sub) * n
+    first_expert = (2 * lax.axis_index("ep") + sub) * n
     comb = comb_ref[...]
-    part = n // 2
-    for e in range(n):
-        gate_ref, up_ref, i = (ga_ref, ua_ref, e) if e < part else (gb_ref, ub_ref, e - part)
-        gate = g_ref[e] + dot(x_ref[...], gate_ref[i, at, :])
-        up = u_ref[e] + dot(x_ref[...], up_ref[i, at, :])
-        hid_ref[e] = (gate / (1.0 + jnp.exp(-gate)) * up).astype(BF16)
     for e in range(n):
         mine_e = (lane == first_expert + e) | (lane == first_expert + e + experts)
         weight = jnp.sum(jnp.where(mine_e, comb, 0.0), -1, keepdims=True)
-        downs[e].wait()
         y = dot(hid_ref[e], down_ref[e]).astype(BF16).astype(F32) * weight
         acc_ref[...] = y if e == 0 else acc_ref[...] + y
 
@@ -279,7 +272,9 @@
 ):
     rows, heads, hd = queries.shape
     in_hbm = functools.partial(pltpu.with_memory_space_constraint, memory_space=pltpu.HBM)
-    gate_proj, up_proj, down_proj = map(in_hbm, (gate_proj, up_proj, down_proj))
+    raw = (gate_proj, up_proj, down_proj)
+    in_vmem = functools.partial(pltpu.with_memory_space_constraint, memory_space=pltpu.VMEM)
+    gate_proj, up_proj, down_proj = map(in_vmem, (gate_proj, up_proj, down_proj))
     win = cache_keys.shape[2]
     width = residual.shape[1]
     dev_rows = residual.shape[0]
@@ -292,9 +287,8 @@
     chunks = SUBL // tail
     cw = cols // chunks
     br = 2 * SUBL
-    n_chunks = 4
+    n_chunks = 2
     tokens = n_ep * rows
-    place = jnp.stack([lax.axis_index("sub"), lax.axis_index("ep")]).astype(jnp.int32)
     swap = [(0, 1), (1, 0)]
 
     def to(x, m):
@@ -302,7 +296,7 @@
 
     partial = pl.pallas_call(
         functools.partial(attention_kernel, n_chunks),
-        in_specs=[SMEM] + [HBM] * 8,
+        in_specs=[HBM] * 8,
         out_specs=VMEM,
         out_shape=jax.ShapeDtypeStruct((rows, width), F32),
         scratch_shapes=[
@@ -326,7 +320,6 @@
         compiler_params=params(14),
         name="attention",
     )(
-        place,
         *map(
             in_hbm,
             (
@@ -339,29 +332,16 @@
     from_sibling = lax.ppermute(partial, "sub", swap)
     payload, stream = pl.pallas_call(
         functools.partial(norm_kernel, experts),
-        in_specs=[SMEM] + [VMEM] * 5,
+        in_specs=[VMEM] * 5 + [HBM] * 3,
         out_specs=(VMEM, VMEM),
         out_shape=(
             jax.ShapeDtypeStruct((br, cols + cw + 2 * experts), BF16),
             jax.ShapeDtypeStruct((dev_rows, width), F32),
         ),
         scratch_shapes=[pltpu.VMEM((rows, cols), F32)],
-        compiler_params=params(6),
+        compiler_params=params(4),
         name="norm",
-    )(place, partial, from_sibling, norm_gain.reshape(1, width), routing, route_weights)
-
-    part = n_exp // 2
-    part_shape = pltpu.VMEM((part, width, ff), BF16)
-
-    def load(srcs, spans, after):
-        return pl.pallas_call(
-            functools.partial(load_kernel, len(srcs), spans),
-            in_specs=[HBM] * (len(srcs) + 1),
-            out_specs=(VMEM,) * len(spans),
-            out_shape=(part_shape,) * len(spans),
-            scratch_shapes=[pltpu.SemaphoreType.DMA((len(spans),))],
-            compiler_params=params(17),
-        )(*srcs, after)
+    )(partial, from_sibling, norm_gain.reshape(1, width), routing, route_weights, *map(in_hbm, raw))
 
     pieces = payload[None]
     far = []
@@ -369,48 +349,49 @@
     while m >= 4:
         far.append(m)
         got = to(pieces, m)
-        pieces = jnp.concatenate([pieces, got], 0)
+        pieces = join([pieces, got])
         m //= 2
     near = list(range(1, min(4, n_ep)))
-    (gate_a,) = load((gate_proj,), ((0, 0, part),), payload)
-    gate_b, up_a = load((gate_proj, up_proj), ((0, part, part), (1, 0, part)), pieces)
     got = []
     for m in near:
         got.append(to(pieces, m))
-    pieces = jnp.concatenate([pieces] + got, 0)
+    pieces = join([pieces] + got)
     others = lax.ppermute(pieces, "sub", swap)
 
     half_shape = jax.ShapeDtypeStruct((n_exp, tokens, ff), F32)
-    gate_half, up_half, up_b = pl.pallas_call(
+    gate_half, up_half = pl.pallas_call(
         functools.partial(first_half_kernel, chunks),
-        in_specs=[SMEM, VMEM, VMEM, VMEM, VMEM, HBM],
-        out_specs=(VMEM,) * 3,
-        out_shape=(half_shape, half_shape, part_shape),
-        scratch_shapes=[pltpu.VMEM((tokens, cols), BF16), pltpu.SemaphoreType.DMA((part,))],
-        compiler_params=params(17),
+        in_specs=[VMEM] * 3,
+        out_specs=(VMEM,) * 2,
+        out_shape=(half_shape, half_shape),
+        scratch_shapes=[pltpu.VMEM((tokens, cols), BF16)],
+        compiler_params=params(4),
         name="experts_first",
-    )(place, pieces, gate_a, gate_b, up_a, up_proj)
+    )(pieces, gate_proj, up_proj)
+
+    hidden = pl.pallas_call(
+        functools.partial(second_half_kernel, chunks),
+        in_specs=[VMEM] * 5,
+        out_specs=VMEM,
+        out_shape=jax.ShapeDtypeStruct((n_exp, tokens, ff), BF16),
+        scratch_shapes=[pltpu.VMEM((tokens, cols), BF16)],
+        compiler_params=params(4),
+        name="experts_second",
+    )(others, gate_half, up_half, gate_proj, up_proj)
 
     ow = width // chunks
     keep, send = pl.pallas_call(
-        functools.partial(second_half_kernel, chunks),
-        in_specs=[SMEM] + [VMEM] * 8 + [HBM],
+        functools.partial(third_kernel, chunks),
+        in_specs=[VMEM] * 4,
         out_specs=(VMEM, VMEM),
         out_shape=(
             jax.ShapeDtypeStruct((n_ep, SUBL, width + ow), F32),
             jax.ShapeDtypeStruct((n_ep, SUBL, width + ow), BF16),
         ),
-        scratch_shapes=[
-            pltpu.VMEM((tokens, cols), BF16),
-            pltpu.VMEM((tokens, width), F32),
-            pltpu.VMEM((tokens, 2 * experts), F32),
-            pltpu.VMEM((n_exp, tokens, ff), BF16),
-            pltpu.VMEM(down_proj.shape, BF16),
-            pltpu.SemaphoreType.DMA((n_exp,)),
-        ],
-        compiler_params=params(17),
-        name="experts_second",
-    )(place, pieces, others, gate_half, up_half, gate_a, gate_b, up_a, up_b, down_proj)
+        scratch_shapes=[pltpu.VMEM((tokens, width), F32), pltpu.VMEM((tokens, 2 * experts), F32)],
+        compiler_params=params(4),
+        name="experts_third",
+    )(pieces, others, hidden, down_proj)
 
     sums = keep + lax.ppermute(send, "sub", swap).astype(F32)
     size = n_ep // (len(near) + 1)

time: 57.5 us -> 44.2 us (0.77)
  Pallas kernels: 26.3 us -> 12.8 us
    pallas_call x6 -> x7, Pallas kernels: 25.7 us -> 12.1 us  [the longest x1 4.85 us: layer(): pl.pallas_call(functools.partial(attention_kernel, n_chunks), in_specs=[H...]
  transfers between devices with their start and end apart: 11 -> 11, of which waited for: 8 -> 10; matrix products, arithmetic and copies ran while one was open for 0% -> 0% of each run, Pallas kernels for 20% -> 5%
where the time goes in v3:
time: 44.2 us; the launch traced here: 44 us
  waiting for transfers between devices  15.4 us (35%)
  starting transfers between devices  15.1 us (34%)
  Pallas kernels  12.8 us (29%)
  local copies, waits for them, and re-layouts  0.45 us (1%)
    ppermute x8, starting transfers between devices, to(): return lax.ppermute(x, 'ep', [(i, i ^ m) for i in range(n_ep)])  13.9 us
    ppermute x8, waiting for transfers between devices, to(): return lax.ppermute(x, 'ep', [(i, i ^ m) for i in range(n_ep)])  13.2 us
    pallas_call x1, Pallas kernels, layer(): pl.pallas_call(functools.partial(attention_kernel, n_chunks), in_specs=[H...  4.85 us
    pallas_call x1, Pallas kernels, layer(): pl.pallas_call(functools.partial(third_kernel, chunks), in_specs=[VMEM] *...  2.48 us
    pallas_call x1, Pallas kernels, layer(): pl.pallas_call(functools.partial(second_half_kernel, chunks), in_specs=[V...  2.33 us
    pallas_call x1, Pallas kernels, layer(): pl.pallas_call(functools.partial(first_half_kernel, chunks), in_specs=[VM...  2.28 us
    ppermute x1, waiting for transfers between devices, layer(): sums = keep + lax.ppermute(send, 'sub', swap).astype(F32)  1.26 us
    ppermute x1, waiting for transfers between devices, layer(): from_sibling = lax.ppermute(partial, 'sub', swap)  0.9 us
  transfers between devices with their start and end apart: 11, of which 10 were waited for; matrix products, arithmetic and copies ran while one was open for 0% of the time, Pallas kernels for 5%

profile of v3, /device:TPU:0, one launch (start us, length us, event | category | flops | bytes accessed | tf_op | source)
XLA Modules:
  0.0 44.0 jit_solution(2460283781252322706)
XLA Ops:
  0.0 4.8 %attention.1.a_ref = f32[20,2048]{1,0:T(8,128)S(1)} custom-call(s32[20]{0:T(128)} %len_hbm.1, bf16[20,8,128]{2,1,0:T(8,128)(2,1)} %q_hbm.1, bf16[20,128]{1,0:T(8,128)(2,1)} %bitcast.17, bf16[20,128]{1,0:T(8,128)(2,1)} %bitcast.18, bf16[10,2048]{1,0:T(8,128)(2,1)} %res_hbm.1, bf16[20,1,384,128]{3,2,1,0:T(8,128)(2,1)} %k_hbm.1, ...), custom_call_target="tpu_custom_call" | custom-call | tf_op jit(solution)/shard_map/attention/pallas_call | solution.py:297
  4.9 0.6 %collective-permute-start = (f32[20,2048]{1,0:T(8,128)S(1)}, f32[20,2048]{1,0:T(8,128)S(1)}, u32[]{:S(2)}, u32[]{:S(2)}) collective-permute-start(f32[20,2048]{1,0:T(8,128)S(1)} %attention.1.a_ref), channel_id=1, source_target_pairs={{0,1},{1,0},{2,3},{3,2},{4,5},{5,4},{6,7},{7,6},{8,9},{9,8},{10,11... | collective-permute-start | bytes 491528 | tf_op jit(solution)/shard_map/ppermute | solution.py:332
  5.4 0.1 copy.15.route_ref
  5.5 0.1 copy.16.rw_ref
  5.6 0.9 %collective-permute-done.b_ref = f32[20,2048]{1,0:T(8,128)S(1)} collective-permute-done((f32[20,2048]{1,0:T(8,128)S(1)}, f32[20,2048]{1,0:T(8,128)S(1)}, u32[]{:S(2)}, u32[]{:S(2)}) %collective-permute-start) | collective-permute-done | bytes 163872 | tf_op jit(solution)/shard_map/ppermute | solution.py:332
  6.5 0.2 norm.1
  6.7 4.0 %collective-permute-start.1 = (bf16[1,16,1408]{2,1,0:T(8,128)(2,1)S(1)}, bf16[1,16,1408]{2,1,0:T(8,128)(2,1)S(1)}, u32[]{:S(2)}, u32[]{:S(2)}) collective-permute-start(bf16[1,16,1408]{2,1,0:T(8,128)(2,1)S(1)} %bitcast.13), channel_id=1, source_target_pairs={{0,8},{2,10},{4,12},{6,14},{8,0},{10,2},{12,4},{14,6},{1,9},{3,11}... | collective-permute-start | bytes 135176 | tf_op jit(solution)/shard_map/ppermute | solution.py:295
  10.7 2.0 %collective-permute-done.1.refs_1_ = bf16[1,16,1408]{2,1,0:T(8,128)(2,1)S(1)} collective-permute-done((bf16[1,16,1408]{2,1,0:T(8,128)(2,1)S(1)}, bf16[1,16,1408]{2,1,0:T(8,128)(2,1)S(1)}, u32[]{:S(2)}, u32[]{:S(2)}) %collective-permute-start.1) | collective-permute-done | bytes 45088 | tf_op jit(solution)/shard_map/ppermute | solution.py:295
  12.7 2.9 %collective-permute-start.4 = (bf16[2,16,1408]{2,1,0:T(8,128)(2,1)S(1)}, bf16[2,16,1408]{2,1,0:T(8,128)(2,1)S(1)}, u32[]{:S(2)}, u32[]{:S(2)}) collective-permute-start(bf16[2,16,1408]{2,1,0:T(8,128)(2,1)S(1)} %shard_map.136.refs_0_), channel_id=1, source_target_pairs={{0,6},{2,4},{4,2},{6,0},{8,14},{10,12},{12,10},{14,8},{1,7},{3,5},... | collective-permute-start | bytes 270344 | tf_op jit(solution)/shard_map/ppermute | solution.py:295
  15.7 0.9 %collective-permute-start.3 = (bf16[2,16,1408]{2,1,0:T(8,128)(2,1)S(1)}, bf16[2,16,1408]{2,1,0:T(8,128)(2,1)S(1)}, u32[]{:S(2)}, u32[]{:S(2)}) collective-permute-start(bf16[2,16,1408]{2,1,0:T(8,128)(2,1)S(1)} %shard_map.136.refs_0_), channel_id=1, source_target_pairs={{0,4},{2,6},{4,0},{6,2},{8,12},{10,14},{12,8},{14,10},{1,5},{3,7},... | collective-permute-start | bytes 270344 | tf_op jit(solution)/shard_map/ppermute | solution.py:295
  16.6 2.3 %collective-permute-done.4.refs_3_ = bf16[2,16,1408]{2,1,0:T(8,128)(2,1)S(1)} collective-permute-done((bf16[2,16,1408]{2,1,0:T(8,128)(2,1)S(1)}, bf16[2,16,1408]{2,1,0:T(8,128)(2,1)S(1)}, u32[]{:S(2)}, u32[]{:S(2)}) %collective-permute-start.4) | collective-permute-done | bytes 90144 | tf_op jit(solution)/shard_map/ppermute | solution.py:295
  18.9 1.3 %collective-permute-done.3.refs_2_ = bf16[2,16,1408]{2,1,0:T(8,128)(2,1)S(1)} collective-permute-done((bf16[2,16,1408]{2,1,0:T(8,128)(2,1)S(1)}, bf16[2,16,1408]{2,1,0:T(8,128)(2,1)S(1)}, u32[]{:S(2)}, u32[]{:S(2)}) %collective-permute-start.3) | collective-permute-done | bytes 90144 | tf_op jit(solution)/shard_map/ppermute | solution.py:295
  20.2 0.9 %collective-permute-done.2.refs_1_ = bf16[2,16,1408]{2,1,0:T(8,128)(2,1)S(1)} collective-permute-done((bf16[2,16,1408]{2,1,0:T(8,128)(2,1)S(1)}, bf16[2,16,1408]{2,1,0:T(8,128)(2,1)S(1)}, u32[]{:S(2)}, u32[]{:S(2)}) %collective-permute-start.2) | collective-permute-done | bytes 90144 | tf_op jit(solution)/shard_map/ppermute | solution.py:295
  21.2 0.1 collective-permute-start.5
  21.3 0.0 slice-start.6
  21.3 2.3 %experts_first.1 = (f32[4,160,768]{2,1,0:T(8,128)S(1)}, f32[4,160,768]{2,1,0:T(8,128)S(1)}) custom-call(bf16[8,16,1408]{2,1,0:T(8,128)(2,1)S(1)} %shard_map.137.piece_ref.own_ref, bf16[4,2048,768]{2,1,0:T(8,128)(2,1)S(1)} %bitcast.8, bf16[4,2048,768]{2,1,0:T(8,128)(2,1)S(1)} %bitcast.10), custom_call_target="tpu_custom_call" | custom-call | tf_op jit(solution)/shard_map/experts_first/pallas_call | solution.py:362
  23.6 0.0 slice-start.8
  23.7 2.3 %experts_second.1.hid_ref = bf16[4,160,768]{2,1,0:T(8,128)(2,1)S(1)} custom-call(bf16[8,16,1408]{2,1,0:T(8,128)(2,1)S(1)} %collective-permute-done.5.oth_ref, f32[4,160,768]{2,1,0:T(8,128)S(1)} %get-tuple-element.13.g_ref, f32[4,160,768]{2,1,0:T(8,128)S(1)} %get-tuple-element.14.u_ref, bf16[4,2048,768]{2,1,0:T(8,128)(2,1)S(1)} %bitcast.8, ...), custom_call_target="tpu_custom_call" | custom-call | tf_op jit(solution)/shard_map/experts_second/pallas_call | solution.py:372
  26.0 0.2 slice-done.8
  26.2 2.5 %experts_third.1 = (f32[8,8,2560]{2,1,0:T(8,128)S(1)}, bf16[8,8,2560]{2,1,0:T(8,128)(2,1)S(1)}) custom-call(bf16[8,16,1408]{2,1,0:T(8,128)(2,1)S(1)} %shard_map.137.piece_ref.own_ref, bf16[8,16,1408]{2,1,0:T(8,128)(2,1)S(1)} %collective-permute-done.5.oth_ref, bf16[4,160,768]{2,1,0:T(8,128)(2,1)S(1)} %experts_second.1.hid_ref, bf16[4,768,2048]{2,1,0:T(8,128)(2,1)S(1)} %bitcast.12), custom_call_target="tpu_custom_call" | custom-call | tf_op jit(solution)/shard_map/experts_third/pallas_call | solution.py:383
  28.7 0.6 %collective-permute-start.6 = (bf16[8,8,2560]{2,1,0:T(8,128)(2,1)S(1)}, bf16[8,8,2560]{2,1,0:T(8,128)(2,1)S(1)}, u32[]{:S(2)}, u32[]{:S(2)}) collective-permute-start(bf16[8,8,2560]{2,1,0:T(8,128)(2,1)S(1)} %get-tuple-element.16), channel_id=1, source_target_pairs={{0,1},{1,0},{2,3},{3,2},{4,5},{5,4},{6,7},{7,6},{8,9},{9,8},{10,11... | collective-permute-start | bytes 983048 | tf_op jit(solution)/shard_map/ppermute | solution.py:396
  29.3 1.3 %collective-permute-done.6 = bf16[8,8,2560]{2,1,0:T(8,128)(2,1)S(1)} collective-permute-done((bf16[8,8,2560]{2,1,0:T(8,128)(2,1)S(1)}, bf16[8,8,2560]{2,1,0:T(8,128)(2,1)S(1)}, u32[]{:S(2)}, u32[]{:S(2)}) %collective-permute-start.6) | collective-permute-done | bytes 327712 | tf_op jit(solution)/shard_map/ppermute | solution.py:396
  30.5 0.1 fusion.2
  30.6 0.5 %collective-permute-start.7 = (bf16[2,8,2560]{2,1,0:T(8,128)(2,1)S(1)}, bf16[2,8,2560]{2,1,0:T(8,128)(2,1)S(1)}, u32[]{:S(2)}, u32[]{:S(2)}) collective-permute-start(bf16[2,8,2560]{2,1,0:T(8,128)(2,1)S(1)} %get-tuple-element.19), channel_id=1, source_target_pairs={{0,2},{2,0},{4,6},{6,4},{8,10},{10,8},{12,14},{14,12},{1,3},{3,1},... | collective-permute-start | bytes 245768 | tf_op jit(solution)/shard_map/ppermute | solution.py:295
  31.1 2.1 %collective-permute-start.9 = (bf16[2,8,2560]{2,1,0:T(8,128)(2,1)S(1)}, bf16[2,8,2560]{2,1,0:T(8,128)(2,1)S(1)}, u32[]{:S(2)}, u32[]{:S(2)}) collective-permute-start(bf16[2,8,2560]{2,1,0:T(8,128)(2,1)S(1)} %get-tuple-element.20), channel_id=1, source_target_pairs={{0,6},{2,4},{4,2},{6,0},{8,14},{10,12},{12,10},{14,8},{1,7},{3,5},... | collective-permute-start | bytes 245768 | tf_op jit(solution)/shard_map/ppermute | solution.py:295
  33.2 0.9 %collective-permute-start.8 = (bf16[2,8,2560]{2,1,0:T(8,128)(2,1)S(1)}, bf16[2,8,2560]{2,1,0:T(8,128)(2,1)S(1)}, u32[]{:S(2)}, u32[]{:S(2)}) collective-permute-start(bf16[2,8,2560]{2,1,0:T(8,128)(2,1)S(1)} %get-tuple-element.21), channel_id=1, source_target_pairs={{0,4},{2,6},{4,0},{6,2},{8,12},{10,14},{12,8},{14,10},{1,5},{3,7},... | collective-permute-start | bytes 245768 | tf_op jit(solution)/shard_map/ppermute | solution.py:295
  34.2 2.9 %collective-permute-done.7 = bf16[2,8,2560]{2,1,0:T(8,128)(2,1)S(1)} collective-permute-done((bf16[2,8,2560]{2,1,0:T(8,128)(2,1)S(1)}, bf16[2,8,2560]{2,1,0:T(8,128)(2,1)S(1)}, u32[]{:S(2)}, u32[]{:S(2)}) %collective-permute-start.7) | collective-permute-done | bytes 81952 | tf_op jit(solution)/shard_map/ppermute | solution.py:295
  37.0 0.2 collective-permute-done.9
  37.3 1.1 %collective-permute-done.8 = bf16[2,8,2560]{2,1,0:T(8,128)(2,1)S(1)} collective-permute-done((bf16[2,8,2560]{2,1,0:T(8,128)(2,1)S(1)}, bf16[2,8,2560]{2,1,0:T(8,128)(2,1)S(1)}, u32[]{:S(2)}, u32[]{:S(2)}) %collective-permute-start.8) | collective-permute-done | bytes 81952 | tf_op jit(solution)/shard_map/ppermute | solution.py:295
  38.4 2.5 %collective-permute-start.10 = (bf16[1,8,2560]{2,1,0:T(8,128)(2,1)S(1)}, bf16[1,8,2560]{2,1,0:T(8,128)(2,1)S(1)}, u32[]{:S(2)}, u32[]{:S(2)}) collective-permute-start(bf16[1,8,2560]{2,1,0:T(8,128)(2,1)S(1)} %slice.41), channel_id=1, source_target_pairs={{0,8},{2,10},{4,12},{6,14},{8,0},{10,2},{12,4},{14,6},{1,9},{3,11}... | collective-permute-start | bytes 122888 | tf_op jit(solution)/shard_map/ppermute | solution.py:295
  40.9 2.5 %collective-permute-done.10 = bf16[1,8,2560]{2,1,0:T(8,128)(2,1)S(1)} collective-permute-done((bf16[1,8,2560]{2,1,0:T(8,128)(2,1)S(1)}, bf16[1,8,2560]{2,1,0:T(8,128)(2,1)S(1)}, u32[]{:S(2)}, u32[]{:S(2)}) %collective-permute-start.10) | collective-permute-done | bytes 40992 | tf_op jit(solution)/shard_map/ppermute | solution.py:295
  43.4 0.7 %finish.1 = bf16[10,2048]{1,0:T(8,128)(2,1)} custom-call(f32[10,2048]{1,0:T(8,128)S(1)} %get-tuple-element.11.stream_ref, f32[8,2560]{1,0:T(8,128)S(1)} %slice_bitcast_fusion.a_ref, bf16[8,2560]{1,0:T(8,128)(2,1)S(1)} %bitcast.15), custom_call_target="tpu_custom_call" | custom-call | tf_op jit(solution)/shard_map/finish/pallas_call | solution.py:412
  (32 shorter events, 0.2 us)
Async XLA Ops:
  0.0 5.4 %copy-start.1 = (s32[10,8]{0,1:T(8,128)S(1)}, s32[10,8]{0,1:T(8,128)}, u32[]{:S(2)}) copy-start(s32[10,8]{0,1:T(8,128)} %param.26) | copy-start | bytes 964
  0.0 5.5 %copy-start.2 = (f32[10,8]{0,1:T(8,128)S(1)}, f32[10,8]{0,1:T(8,128)}, u32[]{:S(2)}) copy-start(f32[10,8]{0,1:T(8,128)} %param.27) | copy-start | bytes 964
  0.0 6.5 %copy-start = (f32[2048]{0:T(1024)S(1)}, f32[2048]{0:T(1024)}, u32[]{:S(2)}) copy-start(f32[2048]{0:T(1024)} %param.22) | copy-start | bytes 24580
  4.9 1.6 %collective-permute-start = (f32[20,2048]{1,0:T(8,128)S(1)}, f32[20,2048]{1,0:T(8,128)S(1)}, u32[]{:S(2)}, u32[]{:S(2)}) collective-permute-start(f32[20,2048]{1,0:T(8,128)S(1)} %attention.1.a_ref), channel_id=1, source_target_pairs={{0,1},{1,0},{2,3},{3,2},{4,5},{5,4},{6,7},{7,6},{8,9},{9,8},{10,11... | collective-permute-start | bytes 491528 | tf_op jit(solution)/shard_map/ppermute | solution.py:332
  6.5 14.7 %slice-start = ((s8[12582912]{0:T(1024)(128)(4,1)}), s8[4194304]{0:T(1024)(128)(4,1)S(1)}, s32[]{:S(2)}) async-start(s8[12582912]{0:T(1024)(128)(4,1)} %bitcast.7), calls=%async_computation | async-start | bytes 8388608
  6.5 14.8 %slice-start.3 = ((s8[12582912]{0:T(1024)(128)(4,1)}), s8[4194304]{0:T(1024)(128)(4,1)S(1)}, s32[]{:S(2)}) async-start(s8[12582912]{0:T(1024)(128)(4,1)} %bitcast.9), calls=%async_computation.3 | async-start | bytes 8388608
  6.5 14.8 %slice-start.1 = ((s8[12582912]{0:T(1024)(128)(4,1)}), s8[4194304]{0:T(1024)(128)(4,1)S(1)}, s32[]{:S(2)}) async-start(s8[12582912]{0:T(1024)(128)(4,1)} %bitcast.7), calls=%async_computation.1 | async-start | bytes 8388608
  6.5 14.8 %slice-start.2 = ((s8[12582912]{0:T(1024)(128)(4,1)}), s8[4194304]{0:T(1024)(128)(4,1)S(1)}, s32[]{:S(2)}) async-start(s8[12582912]{0:T(1024)(128)(4,1)} %bitcast.7), calls=%async_computation.2 | async-start | bytes 8388608
  6.5 14.8 %slice-start.4 = ((s8[12582912]{0:T(1024)(128)(4,1)}), s8[4194304]{0:T(1024)(128)(4,1)S(1)}, s32[]{:S(2)}) async-start(s8[12582912]{0:T(1024)(128)(4,1)} %bitcast.9), calls=%async_computation.4 | async-start | bytes 8388608
  6.5 14.8 %slice-start.5 = ((s8[12582912]{0:T(1024)(128)(4,1)}), s8[4194304]{0:T(1024)(128)(4,1)S(1)}, s32[]{:S(2)}) async-start(s8[12582912]{0:T(1024)(128)(4,1)} %bitcast.9), calls=%async_computation.5 | async-start | bytes 8388608
  6.7 6.0 %collective-permute-start.1 = (bf16[1,16,1408]{2,1,0:T(8,128)(2,1)S(1)}, bf16[1,16,1408]{2,1,0:T(8,128)(2,1)S(1)}, u32[]{:S(2)}, u32[]{:S(2)}) collective-permute-start(bf16[1,16,1408]{2,1,0:T(8,128)(2,1)S(1)} %bitcast.13), channel_id=1, source_target_pairs={{0,8},{2,10},{4,12},{6,14},{8,0},{10,2},{12,4},{14,6},{1,9},{3,11}... | collective-permute-start | bytes 135176 | tf_op jit(solution)/shard_map/ppermute | solution.py:295
  12.7 6.2 %collective-permute-start.4 = (bf16[2,16,1408]{2,1,0:T(8,128)(2,1)S(1)}, bf16[2,16,1408]{2,1,0:T(8,128)(2,1)S(1)}, u32[]{:S(2)}, u32[]{:S(2)}) collective-permute-start(bf16[2,16,1408]{2,1,0:T(8,128)(2,1)S(1)} %shard_map.136.refs_0_), channel_id=1, source_target_pairs={{0,6},{2,4},{4,2},{6,0},{8,14},{10,12},{12,10},{14,8},{1,7},{3,5},... | collective-permute-start | bytes 270344 | tf_op jit(solution)/shard_map/ppermute | solution.py:295
  15.7 4.5 %collective-permute-start.3 = (bf16[2,16,1408]{2,1,0:T(8,128)(2,1)S(1)}, bf16[2,16,1408]{2,1,0:T(8,128)(2,1)S(1)}, u32[]{:S(2)}, u32[]{:S(2)}) collective-permute-start(bf16[2,16,1408]{2,1,0:T(8,128)(2,1)S(1)} %shard_map.136.refs_0_), channel_id=1, source_target_pairs={{0,4},{2,6},{4,0},{6,2},{8,12},{10,14},{12,8},{14,10},{1,5},{3,7},... | collective-permute-start | bytes 270344 | tf_op jit(solution)/shard_map/ppermute | solution.py:295
  16.6 4.5 %collective-permute-start.2 = (bf16[2,16,1408]{2,1,0:T(8,128)(2,1)S(1)}, bf16[2,16,1408]{2,1,0:T(8,128)(2,1)S(1)}, u32[]{:S(2)}, u32[]{:S(2)}) collective-permute-start(bf16[2,16,1408]{2,1,0:T(8,128)(2,1)S(1)} %shard_map.136.refs_0_), channel_id=1, source_target_pairs={{0,2},{2,0},{4,6},{6,4},{8,10},{10,8},{12,14},{14,12},{1,3},{3,1},... | collective-permute-start | bytes 270344 | tf_op jit(solution)/shard_map/ppermute | solution.py:295
  21.2 2.5 %collective-permute-start.5 = (bf16[8,16,1408]{2,1,0:T(8,128)(2,1)S(1)}, bf16[8,16,1408]{2,1,0:T(8,128)(2,1)S(1)}, u32[]{:S(2)}, u32[]{:S(2)}) collective-permute-start(bf16[8,16,1408]{2,1,0:T(8,128)(2,1)S(1)} %shard_map.137.piece_ref.own_ref), channel_id=1, source_target_pairs={{0,1},{1,0},{2,3},{3,2},{4,5},{5,4},{6,7},{7,6},{8,9},{9,8},{10,11... | collective-permute-start | bytes 1081352 | tf_op jit(solution)/shard_map/ppermute | solution.py:359
  21.3 4.7 %slice-start.6 = ((s8[12582912]{0:T(1024)(128)(4,1)}), s8[4194304]{0:T(1024)(128)(4,1)S(1)}, s32[]{:S(2)}) async-start(s8[12582912]{0:T(1024)(128)(4,1)} %bitcast.11), calls=%async_computation.6 | async-start | bytes 8388608
  21.3 4.7 %slice-start.7 = ((s8[12582912]{0:T(1024)(128)(4,1)}), s8[4194304]{0:T(1024)(128)(4,1)S(1)}, s32[]{:S(2)}) async-start(s8[12582912]{0:T(1024)(128)(4,1)} %bitcast.11), calls=%async_computation.7 | async-start | bytes 8388608
  23.6 2.6 %slice-start.8 = ((s8[12582912]{0:T(1024)(128)(4,1)}), s8[4194304]{0:T(1024)(128)(4,1)S(1)}, s32[]{:S(2)}) async-start(s8[12582912]{0:T(1024)(128)(4,1)} %bitcast.11), calls=%async_computation.8 | async-start | bytes 8388608
  28.7 1.8 %collective-permute-start.6 = (bf16[8,8,2560]{2,1,0:T(8,128)(2,1)S(1)}, bf16[8,8,2560]{2,1,0:T(8,128)(2,1)S(1)}, u32[]{:S(2)}, u32[]{:S(2)}) collective-permute-start(bf16[8,8,2560]{2,1,0:T(8,128)(2,1)S(1)} %get-tuple-element.16), channel_id=1, source_target_pairs={{0,1},{1,0},{2,3},{3,2},{4,5},{5,4},{6,7},{7,6},{8,9},{9,8},{10,11... | collective-permute-start | bytes 983048 | tf_op jit(solution)/shard_map/ppermute | solution.py:396
  30.6 6.4 %collective-permute-start.7 = (bf16[2,8,2560]{2,1,0:T(8,128)(2,1)S(1)}, bf16[2,8,2560]{2,1,0:T(8,128)(2,1)S(1)}, u32[]{:S(2)}, u32[]{:S(2)}) collective-permute-start(bf16[2,8,2560]{2,1,0:T(8,128)(2,1)S(1)} %get-tuple-element.19), channel_id=1, source_target_pairs={{0,2},{2,0},{4,6},{6,4},{8,10},{10,8},{12,14},{14,12},{1,3},{3,1},... | collective-permute-start | bytes 245768 | tf_op jit(solution)/shard_map/ppermute | solution.py:295
  31.1 6.2 %collective-permute-start.9 = (bf16[2,8,2560]{2,1,0:T(8,128)(2,1)S(1)}, bf16[2,8,2560]{2,1,0:T(8,128)(2,1)S(1)}, u32[]{:S(2)}, u32[]{:S(2)}) collective-permute-start(bf16[2,8,2560]{2,1,0:T(8,128)(2,1)S(1)} %get-tuple-element.20), channel_id=1, source_target_pairs={{0,6},{2,4},{4,2},{6,0},{8,14},{10,12},{12,10},{14,8},{1,7},{3,5},... | collective-permute-start | bytes 245768 | tf_op jit(solution)/shard_map/ppermute | solution.py:295
  33.2 5.1 %collective-permute-start.8 = (bf16[2,8,2560]{2,1,0:T(8,128)(2,1)S(1)}, bf16[2,8,2560]{2,1,0:T(8,128)(2,1)S(1)}, u32[]{:S(2)}, u32[]{:S(2)}) collective-permute-start(bf16[2,8,2560]{2,1,0:T(8,128)(2,1)S(1)} %get-tuple-element.21), channel_id=1, source_target_pairs={{0,4},{2,6},{4,0},{6,2},{8,12},{10,14},{12,8},{14,10},{1,5},{3,7},... | collective-permute-start | bytes 245768 | tf_op jit(solution)/shard_map/ppermute | solution.py:295
  38.4 5.0 %collective-permute-start.10 = (bf16[1,8,2560]{2,1,0:T(8,128)(2,1)S(1)}, bf16[1,8,2560]{2,1,0:T(8,128)(2,1)S(1)}, u32[]{:S(2)}, u32[]{:S(2)}) collective-permute-start(bf16[1,8,2560]{2,1,0:T(8,128)(2,1)S(1)} %slice.41), channel_id=1, source_target_pairs={{0,8},{2,10},{4,12},{6,14},{8,0},{10,2},{12,4},{14,6},{1,9},{3,11}... | collective-permute-start | bytes 122888 | tf_op jit(solution)/shard_map/ppermute | solution.py:295

commit v4 on v3

--- a/solution.py
+++ b/solution.py
@@ -9,6 +9,7 @@
 from jax.sharding import PartitionSpec as P
 
 
+K_PARTS, V_PARTS, W_PARTS = 2, 1, 1
 F32 = jnp.float32
 BF16 = jnp.bfloat16
 SUBL = 8
@@ -37,26 +38,28 @@
     win = kbuf.shape[1]
     per = rows // n_chunks
     scale = 1.0 / math.sqrt(hd)
-    half = wobuf.shape[0] // 2
-    kcp = [
-        pltpu.make_async_copy(k_hbm.at[pl.ds(c * per, per), 0], kbuf.at[pl.ds(c * per, per)], ksem.at[c])
-        for c in range(n_chunks)
-    ]
-    vcp = [
-        pltpu.make_async_copy(v_hbm.at[pl.ds(c * per, per), 0], vbuf.at[pl.ds(c * per, per)], vsem.at[c])
-        for c in range(n_chunks)
-    ]
-    wcp = [
-        pltpu.make_async_copy(wo_hbm.at[pl.ds(c * half, half)], wobuf.at[pl.ds(c * half, half)], wsem.at[c])
-        for c in range(2)
-    ]
+
+    def split(src, dst, first, n, parts, sems):
+        step = n // parts
+        return [
+            pltpu.make_async_copy(
+                src.at[pl.ds(first + i * step, step)], dst.at[pl.ds(first + i * step, step)], sems.at[i]
+            )
+            for i in range(parts)
+        ]
+
+    kcp = [split(k_hbm.at[:, 0], kbuf, c * per, per, K_PARTS, ksem.at[c]) for c in range(n_chunks)]
+    vcp = [split(v_hbm.at[:, 0], vbuf, c * per, per, V_PARTS, vsem.at[c]) for c in range(n_chunks)]
+    n_w = W_PARTS
+    step_w = wobuf.shape[0] // n_w
+    wcp = split(wo_hbm, wobuf, 0, wobuf.shape[0], n_w, wsem)
     small = [
         pltpu.make_async_copy(src, dst, ssem.at[i])
         for i, (src, dst) in enumerate(
             ((q_hbm, q_ref), (len_hbm, len_ref), (nk_hbm, nk_ref), (nv_hbm, nv_ref), (res_hbm, res_ref))
         )
     ]
-    for cp in small + kcp + vcp + wcp:
+    for cp in small + sum(kcp, []) + sum(vcp, []) + wcp:
         cp.start()
     for cp in small:
         cp.wait()
@@ -66,7 +69,8 @@
     new_v = nv_ref[...].astype(F32)
     slot = lax.broadcasted_iota(jnp.int32, (heads, win), 1)
     for c in range(n_chunks):
-        kcp[c].wait()
+        for cp in kcp[c]:
+            cp.wait()
         for b in range(c * per, (c + 1) * per):
             s = lax.dot_general(q_ref[b], kbuf[b], (((1,), (1,)), ((), ())), preferred_element_type=F32)
             sc_ref[b] = jnp.where(slot < len_ref[b], s * scale, -1e30)
@@ -80,7 +84,8 @@
         den = jnp.sum(w, -1, keepdims=True) + ow
         w_ref[r] = w.astype(BF16)
         owv = ow.astype(BF16).astype(F32) * new_v[c * per : (c + 1) * per, None, :]
-        vcp[c].wait()
+        for cp in vcp[c]:
+            cp.wait()
         for b in range(c * per, (c + 1) * per):
             i = b - c * per
             mix_ref[pl.ds(b * heads, heads)] = (dot(w_ref[b], vbuf[b]) + owv[i]) / den[i]
@@ -95,10 +100,12 @@
             ho_ref[pl.ds(at, n), pl.ds(h * hd, hd)] = piece
             at += n
     ho = ho_ref[...].astype(BF16)
-    wcp[0].wait()
-    acc = dot(ho[:, :half], wobuf[:half])
-    wcp[1].wait()
-    out_ref[...] = acc + dot(ho[:, half:], wobuf[half:])
+    acc = None
+    for i in range(n_w):
+        wcp[i].wait()
+        piece = dot(ho[:, i * step_w : (i + 1) * step_w], wobuf[pl.ds(i * step_w, step_w)])
+        acc = piece if acc is None else acc + piece
+    out_ref[...] = acc
     sub = lax.axis_index("sub")
     res = res_ref[...].astype(F32)
 
@@ -313,9 +320,9 @@
             pltpu.VMEM((rows * heads, hd), F32),
             pltpu.VMEM((rows, heads * hd), F32),
             pltpu.SemaphoreType.DMA((5,)),
-            pltpu.SemaphoreType.DMA((n_chunks,)),
-            pltpu.SemaphoreType.DMA((n_chunks,)),
-            pltpu.SemaphoreType.DMA((2,)),
+            pltpu.SemaphoreType.DMA((n_chunks, K_PARTS)),
+            pltpu.SemaphoreType.DMA((n_chunks, V_PARTS)),
+            pltpu.SemaphoreType.DMA((W_PARTS,)),
         ],
         compiler_params=params(14),
         name="attention",

time: 44.2 us -> 43.8 us (level)
  no operation moved by 1% of the time
where the time goes in v4:
time: 43.8 us; the launch traced here: 43.6 us
  waiting for transfers between devices  15.4 us (35%)
  starting transfers between devices  15.1 us (34%)
  Pallas kernels  12.4 us (28%)
  local copies, waits for them, and re-layouts  0.46 us (1%)
    ppermute x8, starting transfers between devices, to(): return lax.ppermute(x, 'ep', [(i, i ^ m) for i in range(n_ep)])  13.9 us
    ppermute x8, waiting for transfers between devices, to(): return lax.ppermute(x, 'ep', [(i, i ^ m) for i in range(n_ep)])  13.2 us
    pallas_call x1, Pallas kernels, layer(): pl.pallas_call(functools.partial(attention_kernel, n_chunks), in_specs=[H...  4.45 us
    pallas_call x1, Pallas kernels, layer(): pl.pallas_call(functools.partial(third_kernel, chunks), in_specs=[VMEM] *...  2.49 us
    pallas_call x1, Pallas kernels, layer(): pl.pallas_call(functools.partial(second_half_kernel, chunks), in_specs=[V...  2.33 us
    pallas_call x1, Pallas kernels, layer(): pl.pallas_call(functools.partial(first_half_kernel, chunks), in_specs=[VM...  2.28 us
    ppermute x1, waiting for transfers between devices, layer(): sums = keep + lax.ppermute(send, 'sub', swap).astype(F32)  1.26 us
    ppermute x1, waiting for transfers between devices, layer(): from_sibling = lax.ppermute(partial, 'sub', swap)  0.9 us
  transfers between devices with their start and end apart: 11, of which 10 were waited for; matrix products, arithmetic and copies ran while one was open for 0% of the time, Pallas kernels for 5%

profile of v4, /device:TPU:0, one launch (start us, length us, event | category | flops | bytes accessed | tf_op | source)
XLA Modules:
  0.0 43.6 jit_solution(7786352875045008117)
XLA Ops:
  0.0 4.5 %attention.1.a_ref = f32[20,2048]{1,0:T(8,128)S(1)} custom-call(s32[20]{0:T(128)} %len_hbm.1, bf16[20,8,128]{2,1,0:T(8,128)(2,1)} %q_hbm.1, bf16[20,128]{1,0:T(8,128)(2,1)} %bitcast.17, bf16[20,128]{1,0:T(8,128)(2,1)} %bitcast.18, bf16[10,2048]{1,0:T(8,128)(2,1)} %res_hbm.1, bf16[20,1,384,128]{3,2,1,0:T(8,128)(2,1)} %k_hbm.1, ...), custom_call_target="tpu_custom_call" | custom-call | tf_op jit(solution)/shard_map/attention/pallas_call | solution.py:304
  4.5 0.6 %collective-permute-start = (f32[20,2048]{1,0:T(8,128)S(1)}, f32[20,2048]{1,0:T(8,128)S(1)}, u32[]{:S(2)}, u32[]{:S(2)}) collective-permute-start(f32[20,2048]{1,0:T(8,128)S(1)} %attention.1.a_ref), channel_id=1, source_target_pairs={{0,1},{1,0},{2,3},{3,2},{4,5},{5,4},{6,7},{7,6},{8,9},{9,8},{10,11... | collective-permute-start | bytes 491528 | tf_op jit(solution)/shard_map/ppermute | solution.py:339
  5.0 0.1 copy.15.route_ref
  5.1 0.1 copy.16.rw_ref
  5.2 0.9 %collective-permute-done.b_ref = f32[20,2048]{1,0:T(8,128)S(1)} collective-permute-done((f32[20,2048]{1,0:T(8,128)S(1)}, f32[20,2048]{1,0:T(8,128)S(1)}, u32[]{:S(2)}, u32[]{:S(2)}) %collective-permute-start) | collective-permute-done | bytes 163872 | tf_op jit(solution)/shard_map/ppermute | solution.py:339
  6.1 0.2 norm.1
  6.3 4.0 %collective-permute-start.1 = (bf16[1,16,1408]{2,1,0:T(8,128)(2,1)S(1)}, bf16[1,16,1408]{2,1,0:T(8,128)(2,1)S(1)}, u32[]{:S(2)}, u32[]{:S(2)}) collective-permute-start(bf16[1,16,1408]{2,1,0:T(8,128)(2,1)S(1)} %bitcast.13), channel_id=1, source_target_pairs={{0,8},{2,10},{4,12},{6,14},{8,0},{10,2},{12,4},{14,6},{1,9},{3,11}... | collective-permute-start | bytes 135176 | tf_op jit(solution)/shard_map/ppermute | solution.py:302
  10.3 2.0 %collective-permute-done.1.refs_1_ = bf16[1,16,1408]{2,1,0:T(8,128)(2,1)S(1)} collective-permute-done((bf16[1,16,1408]{2,1,0:T(8,128)(2,1)S(1)}, bf16[1,16,1408]{2,1,0:T(8,128)(2,1)S(1)}, u32[]{:S(2)}, u32[]{:S(2)}) %collective-permute-start.1) | collective-permute-done | bytes 45088 | tf_op jit(solution)/shard_map/ppermute | solution.py:302
  12.4 2.9 %collective-permute-start.4 = (bf16[2,16,1408]{2,1,0:T(8,128)(2,1)S(1)}, bf16[2,16,1408]{2,1,0:T(8,128)(2,1)S(1)}, u32[]{:S(2)}, u32[]{:S(2)}) collective-permute-start(bf16[2,16,1408]{2,1,0:T(8,128)(2,1)S(1)} %shard_map.136.refs_0_), channel_id=1, source_target_pairs={{0,6},{2,4},{4,2},{6,0},{8,14},{10,12},{12,10},{14,8},{1,7},{3,5},... | collective-permute-start | bytes 270344 | tf_op jit(solution)/shard_map/ppermute | solution.py:302
  15.3 0.9 %collective-permute-start.3 = (bf16[2,16,1408]{2,1,0:T(8,128)(2,1)S(1)}, bf16[2,16,1408]{2,1,0:T(8,128)(2,1)S(1)}, u32[]{:S(2)}, u32[]{:S(2)}) collective-permute-start(bf16[2,16,1408]{2,1,0:T(8,128)(2,1)S(1)} %shard_map.136.refs_0_), channel_id=1, source_target_pairs={{0,4},{2,6},{4,0},{6,2},{8,12},{10,14},{12,8},{14,10},{1,5},{3,7},... | collective-permute-start | bytes 270344 | tf_op jit(solution)/shard_map/ppermute | solution.py:302
  16.2 2.3 %collective-permute-done.4.refs_3_ = bf16[2,16,1408]{2,1,0:T(8,128)(2,1)S(1)} collective-permute-done((bf16[2,16,1408]{2,1,0:T(8,128)(2,1)S(1)}, bf16[2,16,1408]{2,1,0:T(8,128)(2,1)S(1)}, u32[]{:S(2)}, u32[]{:S(2)}) %collective-permute-start.4) | collective-permute-done | bytes 90144 | tf_op jit(solution)/shard_map/ppermute | solution.py:302
  18.6 1.3 %collective-permute-done.3.refs_2_ = bf16[2,16,1408]{2,1,0:T(8,128)(2,1)S(1)} collective-permute-done((bf16[2,16,1408]{2,1,0:T(8,128)(2,1)S(1)}, bf16[2,16,1408]{2,1,0:T(8,128)(2,1)S(1)}, u32[]{:S(2)}, u32[]{:S(2)}) %collective-permute-start.3) | collective-permute-done | bytes 90144 | tf_op jit(solution)/shard_map/ppermute | solution.py:302
  19.8 0.9 %collective-permute-done.2.refs_1_ = bf16[2,16,1408]{2,1,0:T(8,128)(2,1)S(1)} collective-permute-done((bf16[2,16,1408]{2,1,0:T(8,128)(2,1)S(1)}, bf16[2,16,1408]{2,1,0:T(8,128)(2,1)S(1)}, u32[]{:S(2)}, u32[]{:S(2)}) %collective-permute-start.2) | collective-permute-done | bytes 90144 | tf_op jit(solution)/shard_map/ppermute | solution.py:302
  20.8 0.1 collective-permute-start.5
  20.9 0.0 slice-start.6
  21.0 2.3 %experts_first.1 = (f32[4,160,768]{2,1,0:T(8,128)S(1)}, f32[4,160,768]{2,1,0:T(8,128)S(1)}) custom-call(bf16[8,16,1408]{2,1,0:T(8,128)(2,1)S(1)} %shard_map.137.piece_ref.own_ref, bf16[4,2048,768]{2,1,0:T(8,128)(2,1)S(1)} %bitcast.8, bf16[4,2048,768]{2,1,0:T(8,128)(2,1)S(1)} %bitcast.10), custom_call_target="tpu_custom_call" | custom-call | tf_op jit(solution)/shard_map/experts_first/pallas_call | solution.py:369
  23.2 0.0 slice-start.8
  23.3 2.3 %experts_second.1.hid_ref = bf16[4,160,768]{2,1,0:T(8,128)(2,1)S(1)} custom-call(bf16[8,16,1408]{2,1,0:T(8,128)(2,1)S(1)} %collective-permute-done.5.oth_ref, f32[4,160,768]{2,1,0:T(8,128)S(1)} %get-tuple-element.13.g_ref, f32[4,160,768]{2,1,0:T(8,128)S(1)} %get-tuple-element.14.u_ref, bf16[4,2048,768]{2,1,0:T(8,128)(2,1)S(1)} %bitcast.8, ...), custom_call_target="tpu_custom_call" | custom-call | tf_op jit(solution)/shard_map/experts_second/pallas_call | solution.py:379
  25.6 0.2 slice-done.8
  25.8 2.5 %experts_third.1 = (f32[8,8,2560]{2,1,0:T(8,128)S(1)}, bf16[8,8,2560]{2,1,0:T(8,128)(2,1)S(1)}) custom-call(bf16[8,16,1408]{2,1,0:T(8,128)(2,1)S(1)} %shard_map.137.piece_ref.own_ref, bf16[8,16,1408]{2,1,0:T(8,128)(2,1)S(1)} %collective-permute-done.5.oth_ref, bf16[4,160,768]{2,1,0:T(8,128)(2,1)S(1)} %experts_second.1.hid_ref, bf16[4,768,2048]{2,1,0:T(8,128)(2,1)S(1)} %bitcast.12), custom_call_target="tpu_custom_call" | custom-call | tf_op jit(solution)/shard_map/experts_third/pallas_call | solution.py:390
  28.3 0.5 %collective-permute-start.6 = (bf16[8,8,2560]{2,1,0:T(8,128)(2,1)S(1)}, bf16[8,8,2560]{2,1,0:T(8,128)(2,1)S(1)}, u32[]{:S(2)}, u32[]{:S(2)}) collective-permute-start(bf16[8,8,2560]{2,1,0:T(8,128)(2,1)S(1)} %get-tuple-element.16), channel_id=1, source_target_pairs={{0,1},{1,0},{2,3},{3,2},{4,5},{5,4},{6,7},{7,6},{8,9},{9,8},{10,11... | collective-permute-start | bytes 983048 | tf_op jit(solution)/shard_map/ppermute | solution.py:403
  28.9 1.3 %collective-permute-done.6 = bf16[8,8,2560]{2,1,0:T(8,128)(2,1)S(1)} collective-permute-done((bf16[8,8,2560]{2,1,0:T(8,128)(2,1)S(1)}, bf16[8,8,2560]{2,1,0:T(8,128)(2,1)S(1)}, u32[]{:S(2)}, u32[]{:S(2)}) %collective-permute-start.6) | collective-permute-done | bytes 327712 | tf_op jit(solution)/shard_map/ppermute | solution.py:403
  30.1 0.1 fusion.2
  30.2 0.5 %collective-permute-start.7 = (bf16[2,8,2560]{2,1,0:T(8,128)(2,1)S(1)}, bf16[2,8,2560]{2,1,0:T(8,128)(2,1)S(1)}, u32[]{:S(2)}, u32[]{:S(2)}) collective-permute-start(bf16[2,8,2560]{2,1,0:T(8,128)(2,1)S(1)} %get-tuple-element.19), channel_id=1, source_target_pairs={{0,2},{2,0},{4,6},{6,4},{8,10},{10,8},{12,14},{14,12},{1,3},{3,1},... | collective-permute-start | bytes 245768 | tf_op jit(solution)/shard_map/ppermute | solution.py:302
  30.7 2.2 %collective-permute-start.9 = (bf16[2,8,2560]{2,1,0:T(8,128)(2,1)S(1)}, bf16[2,8,2560]{2,1,0:T(8,128)(2,1)S(1)}, u32[]{:S(2)}, u32[]{:S(2)}) collective-permute-start(bf16[2,8,2560]{2,1,0:T(8,128)(2,1)S(1)} %get-tuple-element.20), channel_id=1, source_target_pairs={{0,6},{2,4},{4,2},{6,0},{8,14},{10,12},{12,10},{14,8},{1,7},{3,5},... | collective-permute-start | bytes 245768 | tf_op jit(solution)/shard_map/ppermute | solution.py:302
  32.8 0.9 %collective-permute-start.8 = (bf16[2,8,2560]{2,1,0:T(8,128)(2,1)S(1)}, bf16[2,8,2560]{2,1,0:T(8,128)(2,1)S(1)}, u32[]{:S(2)}, u32[]{:S(2)}) collective-permute-start(bf16[2,8,2560]{2,1,0:T(8,128)(2,1)S(1)} %get-tuple-element.21), channel_id=1, source_target_pairs={{0,4},{2,6},{4,0},{6,2},{8,12},{10,14},{12,8},{14,10},{1,5},{3,7},... | collective-permute-start | bytes 245768 | tf_op jit(solution)/shard_map/ppermute | solution.py:302
  33.8 2.9 %collective-permute-done.7 = bf16[2,8,2560]{2,1,0:T(8,128)(2,1)S(1)} collective-permute-done((bf16[2,8,2560]{2,1,0:T(8,128)(2,1)S(1)}, bf16[2,8,2560]{2,1,0:T(8,128)(2,1)S(1)}, u32[]{:S(2)}, u32[]{:S(2)}) %collective-permute-start.7) | collective-permute-done | bytes 81952 | tf_op jit(solution)/shard_map/ppermute | solution.py:302
  36.7 0.2 collective-permute-done.9
  36.9 1.1 %collective-permute-done.8 = bf16[2,8,2560]{2,1,0:T(8,128)(2,1)S(1)} collective-permute-done((bf16[2,8,2560]{2,1,0:T(8,128)(2,1)S(1)}, bf16[2,8,2560]{2,1,0:T(8,128)(2,1)S(1)}, u32[]{:S(2)}, u32[]{:S(2)}) %collective-permute-start.8) | collective-permute-done | bytes 81952 | tf_op jit(solution)/shard_map/ppermute | solution.py:302
  38.0 2.5 %collective-permute-start.10 = (bf16[1,8,2560]{2,1,0:T(8,128)(2,1)S(1)}, bf16[1,8,2560]{2,1,0:T(8,128)(2,1)S(1)}, u32[]{:S(2)}, u32[]{:S(2)}) collective-permute-start(bf16[1,8,2560]{2,1,0:T(8,128)(2,1)S(1)} %slice.41), channel_id=1, source_target_pairs={{0,8},{2,10},{4,12},{6,14},{8,0},{10,2},{12,4},{14,6},{1,9},{3,11}... | collective-permute-start | bytes 122888 | tf_op jit(solution)/shard_map/ppermute | solution.py:302
  40.5 2.5 %collective-permute-done.10 = bf16[1,8,2560]{2,1,0:T(8,128)(2,1)S(1)} collective-permute-done((bf16[1,8,2560]{2,1,0:T(8,128)(2,1)S(1)}, bf16[1,8,2560]{2,1,0:T(8,128)(2,1)S(1)}, u32[]{:S(2)}, u32[]{:S(2)}) %collective-permute-start.10) | collective-permute-done | bytes 40992 | tf_op jit(solution)/shard_map/ppermute | solution.py:302
  43.0 0.7 %finish.1 = bf16[10,2048]{1,0:T(8,128)(2,1)} custom-call(f32[10,2048]{1,0:T(8,128)S(1)} %get-tuple-element.11.stream_ref, f32[8,2560]{1,0:T(8,128)S(1)} %slice_bitcast_fusion.a_ref, bf16[8,2560]{1,0:T(8,128)(2,1)S(1)} %bitcast.15), custom_call_target="tpu_custom_call" | custom-call | tf_op jit(solution)/shard_map/finish/pallas_call | solution.py:419
  (32 shorter events, 0.2 us)
Async XLA Ops:
  0.0 5.0 %copy-start.1 = (s32[10,8]{0,1:T(8,128)S(1)}, s32[10,8]{0,1:T(8,128)}, u32[]{:S(2)}) copy-start(s32[10,8]{0,1:T(8,128)} %param.26) | copy-start | bytes 964
  0.0 5.1 %copy-start.2 = (f32[10,8]{0,1:T(8,128)S(1)}, f32[10,8]{0,1:T(8,128)}, u32[]{:S(2)}) copy-start(f32[10,8]{0,1:T(8,128)} %param.27) | copy-start | bytes 964
  0.0 6.1 %copy-start = (f32[2048]{0:T(1024)S(1)}, f32[2048]{0:T(1024)}, u32[]{:S(2)}) copy-start(f32[2048]{0:T(1024)} %param.22) | copy-start | bytes 24580
  4.5 1.6 %collective-permute-start = (f32[20,2048]{1,0:T(8,128)S(1)}, f32[20,2048]{1,0:T(8,128)S(1)}, u32[]{:S(2)}, u32[]{:S(2)}) collective-permute-start(f32[20,2048]{1,0:T(8,128)S(1)} %attention.1.a_ref), channel_id=1, source_target_pairs={{0,1},{1,0},{2,3},{3,2},{4,5},{5,4},{6,7},{7,6},{8,9},{9,8},{10,11... | collective-permute-start | bytes 491528 | tf_op jit(solution)/shard_map/ppermute | solution.py:339
  6.1 14.7 %slice-start = ((s8[12582912]{0:T(1024)(128)(4,1)}), s8[4194304]{0:T(1024)(128)(4,1)S(1)}, s32[]{:S(2)}) async-start(s8[12582912]{0:T(1024)(128)(4,1)} %bitcast.7), calls=%async_computation | async-start | bytes 8388608
  6.1 14.8 %slice-start.3 = ((s8[12582912]{0:T(1024)(128)(4,1)}), s8[4194304]{0:T(1024)(128)(4,1)S(1)}, s32[]{:S(2)}) async-start(s8[12582912]{0:T(1024)(128)(4,1)} %bitcast.9), calls=%async_computation.3 | async-start | bytes 8388608
  6.1 14.8 %slice-start.1 = ((s8[12582912]{0:T(1024)(128)(4,1)}), s8[4194304]{0:T(1024)(128)(4,1)S(1)}, s32[]{:S(2)}) async-start(s8[12582912]{0:T(1024)(128)(4,1)} %bitcast.7), calls=%async_computation.1 | async-start | bytes 8388608
  6.1 14.8 %slice-start.2 = ((s8[12582912]{0:T(1024)(128)(4,1)}), s8[4194304]{0:T(1024)(128)(4,1)S(1)}, s32[]{:S(2)}) async-start(s8[12582912]{0:T(1024)(128)(4,1)} %bitcast.7), calls=%async_computation.2 | async-start | bytes 8388608
  6.1 14.8 %slice-start.4 = ((s8[12582912]{0:T(1024)(128)(4,1)}), s8[4194304]{0:T(1024)(128)(4,1)S(1)}, s32[]{:S(2)}) async-start(s8[12582912]{0:T(1024)(128)(4,1)} %bitcast.9), calls=%async_computation.4 | async-start | bytes 8388608
  6.1 14.8 %slice-start.5 = ((s8[12582912]{0:T(1024)(128)(4,1)}), s8[4194304]{0:T(1024)(128)(4,1)S(1)}, s32[]{:S(2)}) async-start(s8[12582912]{0:T(1024)(128)(4,1)} %bitcast.9), calls=%async_computation.5 | async-start | bytes 8388608
  6.3 6.0 %collective-permute-start.1 = (bf16[1,16,1408]{2,1,0:T(8,128)(2,1)S(1)}, bf16[1,16,1408]{2,1,0:T(8,128)(2,1)S(1)}, u32[]{:S(2)}, u32[]{:S(2)}) collective-permute-start(bf16[1,16,1408]{2,1,0:T(8,128)(2,1)S(1)} %bitcast.13), channel_id=1, source_target_pairs={{0,8},{2,10},{4,12},{6,14},{8,0},{10,2},{12,4},{14,6},{1,9},{3,11}... | collective-permute-start | bytes 135176 | tf_op jit(solution)/shard_map/ppermute | solution.py:302
  12.4 6.2 %collective-permute-start.4 = (bf16[2,16,1408]{2,1,0:T(8,128)(2,1)S(1)}, bf16[2,16,1408]{2,1,0:T(8,128)(2,1)S(1)}, u32[]{:S(2)}, u32[]{:S(2)}) collective-permute-start(bf16[2,16,1408]{2,1,0:T(8,128)(2,1)S(1)} %shard_map.136.refs_0_), channel_id=1, source_target_pairs={{0,6},{2,4},{4,2},{6,0},{8,14},{10,12},{12,10},{14,8},{1,7},{3,5},... | collective-permute-start | bytes 270344 | tf_op jit(solution)/shard_map/ppermute | solution.py:302
  15.3 4.5 %collective-permute-start.3 = (bf16[2,16,1408]{2,1,0:T(8,128)(2,1)S(1)}, bf16[2,16,1408]{2,1,0:T(8,128)(2,1)S(1)}, u32[]{:S(2)}, u32[]{:S(2)}) collective-permute-start(bf16[2,16,1408]{2,1,0:T(8,128)(2,1)S(1)} %shard_map.136.refs_0_), channel_id=1, source_target_pairs={{0,4},{2,6},{4,0},{6,2},{8,12},{10,14},{12,8},{14,10},{1,5},{3,7},... | collective-permute-start | bytes 270344 | tf_op jit(solution)/shard_map/ppermute | solution.py:302
  16.2 4.5 %collective-permute-start.2 = (bf16[2,16,1408]{2,1,0:T(8,128)(2,1)S(1)}, bf16[2,16,1408]{2,1,0:T(8,128)(2,1)S(1)}, u32[]{:S(2)}, u32[]{:S(2)}) collective-permute-start(bf16[2,16,1408]{2,1,0:T(8,128)(2,1)S(1)} %shard_map.136.refs_0_), channel_id=1, source_target_pairs={{0,2},{2,0},{4,6},{6,4},{8,10},{10,8},{12,14},{14,12},{1,3},{3,1},... | collective-permute-start | bytes 270344 | tf_op jit(solution)/shard_map/ppermute | solution.py:302
  20.8 2.5 %collective-permute-start.5 = (bf16[8,16,1408]{2,1,0:T(8,128)(2,1)S(1)}, bf16[8,16,1408]{2,1,0:T(8,128)(2,1)S(1)}, u32[]{:S(2)}, u32[]{:S(2)}) collective-permute-start(bf16[8,16,1408]{2,1,0:T(8,128)(2,1)S(1)} %shard_map.137.piece_ref.own_ref), channel_id=1, source_target_pairs={{0,1},{1,0},{2,3},{3,2},{4,5},{5,4},{6,7},{7,6},{8,9},{9,8},{10,11... | collective-permute-start | bytes 1081352 | tf_op jit(solution)/shard_map/ppermute | solution.py:366
  20.9 4.7 %slice-start.6 = ((s8[12582912]{0:T(1024)(128)(4,1)}), s8[4194304]{0:T(1024)(128)(4,1)S(1)}, s32[]{:S(2)}) async-start(s8[12582912]{0:T(1024)(128)(4,1)} %bitcast.11), calls=%async_computation.6 | async-start | bytes 8388608
  20.9 4.7 %slice-start.7 = ((s8[12582912]{0:T(1024)(128)(4,1)}), s8[4194304]{0:T(1024)(128)(4,1)S(1)}, s32[]{:S(2)}) async-start(s8[12582912]{0:T(1024)(128)(4,1)} %bitcast.11), calls=%async_computation.7 | async-start | bytes 8388608
  23.2 2.6 %slice-start.8 = ((s8[12582912]{0:T(1024)(128)(4,1)}), s8[4194304]{0:T(1024)(128)(4,1)S(1)}, s32[]{:S(2)}) async-start(s8[12582912]{0:T(1024)(128)(4,1)} %bitcast.11), calls=%async_computation.8 | async-start | bytes 8388608
  28.3 1.8 %collective-permute-start.6 = (bf16[8,8,2560]{2,1,0:T(8,128)(2,1)S(1)}, bf16[8,8,2560]{2,1,0:T(8,128)(2,1)S(1)}, u32[]{:S(2)}, u32[]{:S(2)}) collective-permute-start(bf16[8,8,2560]{2,1,0:T(8,128)(2,1)S(1)} %get-tuple-element.16), channel_id=1, source_target_pairs={{0,1},{1,0},{2,3},{3,2},{4,5},{5,4},{6,7},{7,6},{8,9},{9,8},{10,11... | collective-permute-start | bytes 983048 | tf_op jit(solution)/shard_map/ppermute | solution.py:403
  30.2 6.4 %collective-permute-start.7 = (bf16[2,8,2560]{2,1,0:T(8,128)(2,1)S(1)}, bf16[2,8,2560]{2,1,0:T(8,128)(2,1)S(1)}, u32[]{:S(2)}, u32[]{:S(2)}) collective-permute-start(bf16[2,8,2560]{2,1,0:T(8,128)(2,1)S(1)} %get-tuple-element.19), channel_id=1, source_target_pairs={{0,2},{2,0},{4,6},{6,4},{8,10},{10,8},{12,14},{14,12},{1,3},{3,1},... | collective-permute-start | bytes 245768 | tf_op jit(solution)/shard_map/ppermute | solution.py:302
  30.7 6.2 %collective-permute-start.9 = (bf16[2,8,2560]{2,1,0:T(8,128)(2,1)S(1)}, bf16[2,8,2560]{2,1,0:T(8,128)(2,1)S(1)}, u32[]{:S(2)}, u32[]{:S(2)}) collective-permute-start(bf16[2,8,2560]{2,1,0:T(8,128)(2,1)S(1)} %get-tuple-element.20), channel_id=1, source_target_pairs={{0,6},{2,4},{4,2},{6,0},{8,14},{10,12},{12,10},{14,8},{1,7},{3,5},... | collective-permute-start | bytes 245768 | tf_op jit(solution)/shard_map/ppermute | solution.py:302
  32.8 5.1 %collective-permute-start.8 = (bf16[2,8,2560]{2,1,0:T(8,128)(2,1)S(1)}, bf16[2,8,2560]{2,1,0:T(8,128)(2,1)S(1)}, u32[]{:S(2)}, u32[]{:S(2)}) collective-permute-start(bf16[2,8,2560]{2,1,0:T(8,128)(2,1)S(1)} %get-tuple-element.21), channel_id=1, source_target_pairs={{0,4},{2,6},{4,0},{6,2},{8,12},{10,14},{12,8},{14,10},{1,5},{3,7},... | collective-permute-start | bytes 245768 | tf_op jit(solution)/shard_map/ppermute | solution.py:302
  38.0 5.0 %collective-permute-start.10 = (bf16[1,8,2560]{2,1,0:T(8,128)(2,1)S(1)}, bf16[1,8,2560]{2,1,0:T(8,128)(2,1)S(1)}, u32[]{:S(2)}, u32[]{:S(2)}) collective-permute-start(bf16[1,8,2560]{2,1,0:T(8,128)(2,1)S(1)} %slice.41), channel_id=1, source_target_pairs={{0,8},{2,10},{4,12},{6,14},{8,0},{10,2},{12,4},{14,6},{1,9},{3,11}... | collective-permute-start | bytes 122888 | tf_op jit(solution)/shard_map/ppermute | solution.py:302

commit v5 on v4

--- a/solution.py
+++ b/solution.py
@@ -174,8 +174,10 @@
     )(*arrays)
 
 
-def unpack_tokens(x_ref, piece_ref, cols, chunks):
-    blocks, br, _ = piece_ref.shape
+def unpack_tokens(x_ref, piece_ref, cols, chunks, skip=0):
+    br = piece_ref.shape[1]
+    blocks = piece_ref.shape[0] - skip
+    piece_ref = piece_ref.at[pl.ds(skip, blocks)]
     tail = br // chunks
     cw = cols // chunks
     x_ref[pl.ds(0, blocks * br)] = piece_ref[:, :, pl.ds(0, cols)].reshape(blocks * br, cols)
@@ -188,24 +190,32 @@
         x_ref[pl.ds(blocks * br, blocks * tail), pl.ds(c * cw, cw)] = dot(pick, folded).astype(BF16)
 
 
-def first_half_kernel(chunks, piece_ref, gate_ref, up_ref, g_ref, u_ref, x_ref):
+def first_half_kernel(chunks, skip, piece_ref, gate_ref, up_ref, g_ref, u_ref, x_ref):
     n, width, _ = gate_ref.shape
     cols = width // 2
-    unpack_tokens(x_ref, piece_ref, cols, chunks)
+    unpack_tokens(x_ref, piece_ref, cols, chunks, skip)
     at = pl.ds(pl.multiple_of(lax.axis_index("sub") * cols, cols), cols)
     for e in range(n):
         g_ref[e] = dot(x_ref[...], gate_ref[e, at, :])
         u_ref[e] = dot(x_ref[...], up_ref[e, at, :])
 
 
-def second_half_kernel(chunks, oth_ref, g_ref, u_ref, gate_ref, up_ref, hid_ref, x_ref):
+def second_half_kernel(
+    chunks, oth_ref, ga_ref, ua_ref, gb_ref, ub_ref, gate_ref, up_ref, hid_ref, x_ref
+):
     n, width, _ = gate_ref.shape
     cols = width // 2
+    early = ga_ref.shape[1] * chunks // (chunks + 1)
+    late = gb_ref.shape[1] * chunks // (chunks + 1)
+
+    def whole(a, b):
+        return jnp.concatenate([a[:early], b[:late], a[early:], b[late:]], 0)
+
     unpack_tokens(x_ref, oth_ref, cols, chunks)
     at = pl.ds(pl.multiple_of((1 - lax.axis_index("sub")) * cols, cols), cols)
     for e in range(n):
-        gate = g_ref[e] + dot(x_ref[...], gate_ref[e, at, :])
-        up = u_ref[e] + dot(x_ref[...], up_ref[e, at, :])
+        gate = whole(ga_ref[e], gb_ref[e]) + dot(x_ref[...], gate_ref[e, at, :])
+        up = whole(ua_ref[e], ub_ref[e]) + dot(x_ref[...], up_ref[e, at, :])
         hid_ref[e] = (gate / (1.0 + jnp.exp(-gate)) * up).astype(BF16)
 
 
@@ -359,32 +369,37 @@
         pieces = join([pieces, got])
         m //= 2
     near = list(range(1, min(4, n_ep)))
+    early = pieces
     got = []
     for m in near:
         got.append(to(pieces, m))
     pieces = join([pieces] + got)
     others = lax.ppermute(pieces, "sub", swap)
 
-    half_shape = jax.ShapeDtypeStruct((n_exp, tokens, ff), F32)
-    gate_half, up_half = pl.pallas_call(
-        functools.partial(first_half_kernel, chunks),
-        in_specs=[VMEM] * 3,
-        out_specs=(VMEM,) * 2,
-        out_shape=(half_shape, half_shape),
-        scratch_shapes=[pltpu.VMEM((tokens, cols), BF16)],
-        compiler_params=params(4),
-        name="experts_first",
-    )(pieces, gate_proj, up_proj)
+    def first_half(x, skip):
+        n_rows = (x.shape[0] - skip) * rows
+        shape = jax.ShapeDtypeStruct((n_exp, n_rows, ff), F32)
+        return pl.pallas_call(
+            functools.partial(first_half_kernel, chunks, skip),
+            in_specs=[VMEM] * 3,
+            out_specs=(VMEM,) * 2,
+            out_shape=(shape, shape),
+            scratch_shapes=[pltpu.VMEM((n_rows, cols), BF16)],
+            compiler_params=params(4),
+        )(x, gate_proj, up_proj)
+
+    gate_early, up_early = first_half(early, 0)
+    gate_late, up_late = first_half(pieces, early.shape[0])
 
     hidden = pl.pallas_call(
         functools.partial(second_half_kernel, chunks),
-        in_specs=[VMEM] * 5,
+        in_specs=[VMEM] * 7,
         out_specs=VMEM,
         out_shape=jax.ShapeDtypeStruct((n_exp, tokens, ff), BF16),
         scratch_shapes=[pltpu.VMEM((tokens, cols), BF16)],
         compiler_params=params(4),
         name="experts_second",
-    )(others, gate_half, up_half, gate_proj, up_proj)
+    )(others, gate_early, up_early, gate_late, up_late, gate_proj, up_proj)
 
     ow = width // chunks
     keep, send = pl.pallas_call(
@@ -402,7 +417,9 @@
 
     sums = keep + lax.ppermute(send, "sub", swap).astype(F32)
     size = n_ep // (len(near) + 1)
-    arrived = [to(sums[i * size : (i + 1) * size].astype(BF16), m) for i, m in enumerate(near, 1)]
+    arrived = []
+    for i, m in enumerate(near, 1):
+        arrived.append(to(sums[i * size : (i + 1) * size].astype(BF16), m))
     sums = sums[:size]
     for x in arrived:
         sums = sums + x.astype(F32)

time: 43.8 us -> 46.1 us (1.053)
  Pallas kernels: 12.4 us -> 14.3 us
    pallas_call x1 -> x2, Pallas kernels: 2.28 us -> 4.22 us  [first_half(): pl.pallas_call(functools.partial(first_half_kernel, chunks, skip), in_spe...]
  transfers between devices with their start and end apart: 11 -> 11, of which waited for: 10 -> 10; matrix products, arithmetic and copies ran while one was open for 0% -> 0% of each run, Pallas kernels for 5% -> 9%
where the time goes in v5:
time: 46.1 us; the launch traced here: 46 us
  waiting for transfers between devices  15.4 us (33%)
  starting transfers between devices  15.1 us (33%)
  Pallas kernels  14.3 us (31%)
  local copies, waits for them, and re-layouts  0.83 us (2%)
    ppermute x8, starting transfers between devices, to(): return lax.ppermute(x, 'ep', [(i, i ^ m) for i in range(n_ep)])  13.9 us
    ppermute x8, waiting for transfers between devices, to(): return lax.ppermute(x, 'ep', [(i, i ^ m) for i in range(n_ep)])  13.2 us
    pallas_call x1, Pallas kernels, layer(): pl.pallas_call(functools.partial(attention_kernel, n_chunks), in_specs=[H...  4.45 us
    pallas_call x2, Pallas kernels, first_half(): pl.pallas_call(functools.partial(first_half_kernel, chunks, skip), in_spe...  4.22 us
    pallas_call x1, Pallas kernels, layer(): pl.pallas_call(functools.partial(third_kernel, chunks), in_specs=[VMEM] *...  2.48 us
    pallas_call x1, Pallas kernels, layer(): pl.pallas_call(functools.partial(second_half_kernel, chunks), in_specs=[V...  2.35 us
    ppermute x1, waiting for transfers between devices, layer(): sums = keep + lax.ppermute(send, 'sub', swap).astype(F32)  1.26 us
  transfers between devices with their start and end apart: 11, of which 10 were waited for; matrix products, arithmetic and copies ran while one was open for 0% of the time, Pallas kernels for 9%

profile of v5, /device:TPU:0, one launch (start us, length us, event | category | flops | bytes accessed | tf_op | source)
XLA Modules:
  0.0 46.0 jit_solution(2460273600390530516)
XLA Ops:
  0.0 4.5 %attention.1.a_ref = f32[20,2048]{1,0:T(8,128)S(1)} custom-call(s32[20]{0:T(128)} %len_hbm.1, bf16[20,8,128]{2,1,0:T(8,128)(2,1)} %q_hbm.1, bf16[20,128]{1,0:T(8,128)(2,1)} %bitcast.17, bf16[20,128]{1,0:T(8,128)(2,1)} %bitcast.18, bf16[10,2048]{1,0:T(8,128)(2,1)} %res_hbm.1, bf16[20,1,384,128]{3,2,1,0:T(8,128)(2,1)} %k_hbm.1, ...), custom_call_target="tpu_custom_call" | custom-call | tf_op jit(solution)/shard_map/attention/pallas_call | solution.py:314
  4.5 0.6 %collective-permute-start = (f32[20,2048]{1,0:T(8,128)S(1)}, f32[20,2048]{1,0:T(8,128)S(1)}, u32[]{:S(2)}, u32[]{:S(2)}) collective-permute-start(f32[20,2048]{1,0:T(8,128)S(1)} %attention.1.a_ref), channel_id=1, source_target_pairs={{0,1},{1,0},{2,3},{3,2},{4,5},{5,4},{6,7},{7,6},{8,9},{9,8},{10,11... | collective-permute-start | bytes 491528 | tf_op jit(solution)/shard_map/ppermute | solution.py:349
  5.0 0.1 copy.15.route_ref
  5.1 0.1 copy.16.rw_ref
  5.2 0.9 %collective-permute-done.b_ref = f32[20,2048]{1,0:T(8,128)S(1)} collective-permute-done((f32[20,2048]{1,0:T(8,128)S(1)}, f32[20,2048]{1,0:T(8,128)S(1)}, u32[]{:S(2)}, u32[]{:S(2)}) %collective-permute-start) | collective-permute-done | bytes 163872 | tf_op jit(solution)/shard_map/ppermute | solution.py:349
  6.1 0.2 norm.1
  6.3 4.0 %collective-permute-start.1 = (bf16[1,16,1408]{2,1,0:T(8,128)(2,1)S(1)}, bf16[1,16,1408]{2,1,0:T(8,128)(2,1)S(1)}, u32[]{:S(2)}, u32[]{:S(2)}) collective-permute-start(bf16[1,16,1408]{2,1,0:T(8,128)(2,1)S(1)} %bitcast.13), channel_id=1, source_target_pairs={{0,8},{2,10},{4,12},{6,14},{8,0},{10,2},{12,4},{14,6},{1,9},{3,11}... | collective-permute-start | bytes 135176 | tf_op jit(solution)/shard_map/ppermute | solution.py:312
  10.3 2.0 %collective-permute-done.1.refs_1_ = bf16[1,16,1408]{2,1,0:T(8,128)(2,1)S(1)} collective-permute-done((bf16[1,16,1408]{2,1,0:T(8,128)(2,1)S(1)}, bf16[1,16,1408]{2,1,0:T(8,128)(2,1)S(1)}, u32[]{:S(2)}, u32[]{:S(2)}) %collective-permute-start.1) | collective-permute-done | bytes 45088 | tf_op jit(solution)/shard_map/ppermute | solution.py:312
  12.4 2.9 %collective-permute-start.4 = (bf16[2,16,1408]{2,1,0:T(8,128)(2,1)S(1)}, bf16[2,16,1408]{2,1,0:T(8,128)(2,1)S(1)}, u32[]{:S(2)}, u32[]{:S(2)}) collective-permute-start(bf16[2,16,1408]{2,1,0:T(8,128)(2,1)S(1)} %shard_map.136.refs_0_.piece_ref), channel_id=1, source_target_pairs={{0,6},{2,4},{4,2},{6,0},{8,14},{10,12},{12,10},{14,8},{1,7},{3,5},... | collective-permute-start | bytes 270344 | tf_op jit(solution)/shard_map/ppermute | solution.py:312
  15.3 0.9 %collective-permute-start.3 = (bf16[2,16,1408]{2,1,0:T(8,128)(2,1)S(1)}, bf16[2,16,1408]{2,1,0:T(8,128)(2,1)S(1)}, u32[]{:S(2)}, u32[]{:S(2)}) collective-permute-start(bf16[2,16,1408]{2,1,0:T(8,128)(2,1)S(1)} %shard_map.136.refs_0_.piece_ref), channel_id=1, source_target_pairs={{0,4},{2,6},{4,0},{6,2},{8,12},{10,14},{12,8},{14,10},{1,5},{3,7},... | collective-permute-start | bytes 270344 | tf_op jit(solution)/shard_map/ppermute | solution.py:312
  16.2 2.3 %collective-permute-done.4.refs_3_ = bf16[2,16,1408]{2,1,0:T(8,128)(2,1)S(1)} collective-permute-done((bf16[2,16,1408]{2,1,0:T(8,128)(2,1)S(1)}, bf16[2,16,1408]{2,1,0:T(8,128)(2,1)S(1)}, u32[]{:S(2)}, u32[]{:S(2)}) %collective-permute-start.4) | collective-permute-done | bytes 90144 | tf_op jit(solution)/shard_map/ppermute | solution.py:312
  18.6 1.3 %collective-permute-done.3.refs_2_ = bf16[2,16,1408]{2,1,0:T(8,128)(2,1)S(1)} collective-permute-done((bf16[2,16,1408]{2,1,0:T(8,128)(2,1)S(1)}, bf16[2,16,1408]{2,1,0:T(8,128)(2,1)S(1)}, u32[]{:S(2)}, u32[]{:S(2)}) %collective-permute-start.3) | collective-permute-done | bytes 90144 | tf_op jit(solution)/shard_map/ppermute | solution.py:312
  19.8 0.9 %collective-permute-done.2.refs_1_ = bf16[2,16,1408]{2,1,0:T(8,128)(2,1)S(1)} collective-permute-done((bf16[2,16,1408]{2,1,0:T(8,128)(2,1)S(1)}, bf16[2,16,1408]{2,1,0:T(8,128)(2,1)S(1)}, u32[]{:S(2)}, u32[]{:S(2)}) %collective-permute-start.2) | collective-permute-done | bytes 90144 | tf_op jit(solution)/shard_map/ppermute | solution.py:312
  20.8 0.1 collective-permute-start.5
  20.9 2.3 %shard_map.138 = (f32[4,40,768]{2,1,0:T(8,128)S(1)}, f32[4,40,768]{2,1,0:T(8,128)S(1)}) custom-call(bf16[2,16,1408]{2,1,0:T(8,128)(2,1)S(1)} %shard_map.136.refs_0_.piece_ref, bf16[4,2048,768]{2,1,0:T(8,128)(2,1)S(1)} %bitcast.8, bf16[4,2048,768]{2,1,0:T(8,128)(2,1)S(1)} %bitcast.10), custom_call_target="tpu_custom_call" | custom-call | tf_op jit(solution)/shard_map/pallas_call | solution.py:382
  23.3 0.0 slice-start.6
  23.3 1.9 %shard_map.139 = (f32[4,120,768]{2,1,0:T(8,128)S(1)}, f32[4,120,768]{2,1,0:T(8,128)S(1)}) custom-call(bf16[8,16,1408]{2,1,0:T(8,128)(2,1)S(1)} %shard_map.137.piece_ref.own_ref, bf16[4,2048,768]{2,1,0:T(8,128)(2,1)S(1)} %bitcast.8, bf16[4,2048,768]{2,1,0:T(8,128)(2,1)S(1)} %bitcast.10), custom_call_target="tpu_custom_call" | custom-call | tf_op jit(solution)/shard_map/pallas_call | solution.py:382
  25.2 2.3 %experts_second.1.hid_ref = bf16[4,160,768]{2,1,0:T(8,128)(2,1)S(1)} custom-call(bf16[8,16,1408]{2,1,0:T(8,128)(2,1)S(1)} %collective-permute-done.5.oth_ref, f32[4,40,768]{2,1,0:T(8,128)S(1)} %get-tuple-element.15.ga_ref, f32[4,40,768]{2,1,0:T(8,128)S(1)} %get-tuple-element.16.ua_ref, f32[4,120,768]{2,1,0:T(8,128)S(1)} %get-tuple-element.17.gb_ref, ...), custom_call_target="tpu_custom_call" | custom-call | tf_op jit(solution)/shard_map/experts_second/pallas_call | solution.py:394
  27.6 0.6 %slice-done.8 = s8[4194304]{0:T(1024)(128)(4,1)S(1)} async-done(((s8[12582912]{0:T(1024)(128)(4,1)}), s8[4194304]{0:T(1024)(128)(4,1)S(1)}, s32[]{:S(2)}) %slice-start.8) | async-done | bytes 4194328
  28.2 2.5 %experts_third.1 = (f32[8,8,2560]{2,1,0:T(8,128)S(1)}, bf16[8,8,2560]{2,1,0:T(8,128)(2,1)S(1)}) custom-call(bf16[8,16,1408]{2,1,0:T(8,128)(2,1)S(1)} %shard_map.137.piece_ref.own_ref, bf16[8,16,1408]{2,1,0:T(8,128)(2,1)S(1)} %collective-permute-done.5.oth_ref, bf16[4,160,768]{2,1,0:T(8,128)(2,1)S(1)} %experts_second.1.hid_ref, bf16[4,768,2048]{2,1,0:T(8,128)(2,1)S(1)} %bitcast.12), custom_call_target="tpu_custom_call" | custom-call | tf_op jit(solution)/shard_map/experts_third/pallas_call | solution.py:405
  30.6 0.6 %collective-permute-start.6 = (bf16[8,8,2560]{2,1,0:T(8,128)(2,1)S(1)}, bf16[8,8,2560]{2,1,0:T(8,128)(2,1)S(1)}, u32[]{:S(2)}, u32[]{:S(2)}) collective-permute-start(bf16[8,8,2560]{2,1,0:T(8,128)(2,1)S(1)} %get-tuple-element.20), channel_id=1, source_target_pairs={{0,1},{1,0},{2,3},{3,2},{4,5},{5,4},{6,7},{7,6},{8,9},{9,8},{10,11... | collective-permute-start | bytes 983048 | tf_op jit(solution)/shard_map/ppermute | solution.py:418
  31.2 1.3 %collective-permute-done.6 = bf16[8,8,2560]{2,1,0:T(8,128)(2,1)S(1)} collective-permute-done((bf16[8,8,2560]{2,1,0:T(8,128)(2,1)S(1)}, bf16[8,8,2560]{2,1,0:T(8,128)(2,1)S(1)}, u32[]{:S(2)}, u32[]{:S(2)}) %collective-permute-start.6) | collective-permute-done | bytes 327712 | tf_op jit(solution)/shard_map/ppermute | solution.py:418
  32.4 0.1 fusion.2
  32.6 0.5 collective-permute-start.7
  33.0 2.2 %collective-permute-start.9 = (bf16[2,8,2560]{2,1,0:T(8,128)(2,1)S(1)}, bf16[2,8,2560]{2,1,0:T(8,128)(2,1)S(1)}, u32[]{:S(2)}, u32[]{:S(2)}) collective-permute-start(bf16[2,8,2560]{2,1,0:T(8,128)(2,1)S(1)} %get-tuple-element.24), channel_id=1, source_target_pairs={{0,6},{2,4},{4,2},{6,0},{8,14},{10,12},{12,10},{14,8},{1,7},{3,5},... | collective-permute-start | bytes 245768 | tf_op jit(solution)/shard_map/ppermute | solution.py:312
  35.2 0.9 %collective-permute-start.8 = (bf16[2,8,2560]{2,1,0:T(8,128)(2,1)S(1)}, bf16[2,8,2560]{2,1,0:T(8,128)(2,1)S(1)}, u32[]{:S(2)}, u32[]{:S(2)}) collective-permute-start(bf16[2,8,2560]{2,1,0:T(8,128)(2,1)S(1)} %get-tuple-element.25), channel_id=1, source_target_pairs={{0,4},{2,6},{4,0},{6,2},{8,12},{10,14},{12,8},{14,10},{1,5},{3,7},... | collective-permute-start | bytes 245768 | tf_op jit(solution)/shard_map/ppermute | solution.py:312
  36.1 2.9 %collective-permute-done.7 = bf16[2,8,2560]{2,1,0:T(8,128)(2,1)S(1)} collective-permute-done((bf16[2,8,2560]{2,1,0:T(8,128)(2,1)S(1)}, bf16[2,8,2560]{2,1,0:T(8,128)(2,1)S(1)}, u32[]{:S(2)}, u32[]{:S(2)}) %collective-permute-start.7) | collective-permute-done | bytes 81952 | tf_op jit(solution)/shard_map/ppermute | solution.py:312
  39.0 0.2 collective-permute-done.9
  39.2 1.1 %collective-permute-done.8 = bf16[2,8,2560]{2,1,0:T(8,128)(2,1)S(1)} collective-permute-done((bf16[2,8,2560]{2,1,0:T(8,128)(2,1)S(1)}, bf16[2,8,2560]{2,1,0:T(8,128)(2,1)S(1)}, u32[]{:S(2)}, u32[]{:S(2)}) %collective-permute-start.8) | collective-permute-done | bytes 81952 | tf_op jit(solution)/shard_map/ppermute | solution.py:312
  40.3 2.5 %collective-permute-start.10 = (bf16[1,8,2560]{2,1,0:T(8,128)(2,1)S(1)}, bf16[1,8,2560]{2,1,0:T(8,128)(2,1)S(1)}, u32[]{:S(2)}, u32[]{:S(2)}) collective-permute-start(bf16[1,8,2560]{2,1,0:T(8,128)(2,1)S(1)} %slice.41), channel_id=1, source_target_pairs={{0,8},{2,10},{4,12},{6,14},{8,0},{10,2},{12,4},{14,6},{1,9},{3,11}... | collective-permute-start | bytes 122888 | tf_op jit(solution)/shard_map/ppermute | solution.py:312
  42.8 2.5 %collective-permute-done.10 = bf16[1,8,2560]{2,1,0:T(8,128)(2,1)S(1)} collective-permute-done((bf16[1,8,2560]{2,1,0:T(8,128)(2,1)S(1)}, bf16[1,8,2560]{2,1,0:T(8,128)(2,1)S(1)}, u32[]{:S(2)}, u32[]{:S(2)}) %collective-permute-start.10) | collective-permute-done | bytes 40992 | tf_op jit(solution)/shard_map/ppermute | solution.py:312
  45.3 0.7 %finish.1 = bf16[10,2048]{1,0:T(8,128)(2,1)} custom-call(f32[10,2048]{1,0:T(8,128)S(1)} %get-tuple-element.13.stream_ref, f32[8,2560]{1,0:T(8,128)S(1)} %slice_bitcast_fusion.a_ref, bf16[8,2560]{1,0:T(8,128)(2,1)S(1)} %bitcast.15), custom_call_target="tpu_custom_call" | custom-call | tf_op jit(solution)/shard_map/finish/pallas_call | solution.py:436
  (33 shorter events, 0.2 us)
Async XLA Ops:
  0.0 5.0 %copy-start.1 = (s32[10,8]{0,1:T(8,128)S(1)}, s32[10,8]{0,1:T(8,128)}, u32[]{:S(2)}) copy-start(s32[10,8]{0,1:T(8,128)} %param.26) | copy-start | bytes 964
  0.0 5.1 %copy-start.2 = (f32[10,8]{0,1:T(8,128)S(1)}, f32[10,8]{0,1:T(8,128)}, u32[]{:S(2)}) copy-start(f32[10,8]{0,1:T(8,128)} %param.27) | copy-start | bytes 964
  0.0 6.1 %copy-start = (f32[2048]{0:T(1024)S(1)}, f32[2048]{0:T(1024)}, u32[]{:S(2)}) copy-start(f32[2048]{0:T(1024)} %param.22) | copy-start | bytes 24580
  4.5 1.6 %collective-permute-start = (f32[20,2048]{1,0:T(8,128)S(1)}, f32[20,2048]{1,0:T(8,128)S(1)}, u32[]{:S(2)}, u32[]{:S(2)}) collective-permute-start(f32[20,2048]{1,0:T(8,128)S(1)} %attention.1.a_ref), channel_id=1, source_target_pairs={{0,1},{1,0},{2,3},{3,2},{4,5},{5,4},{6,7},{7,6},{8,9},{9,8},{10,11... | collective-permute-start | bytes 491528 | tf_op jit(solution)/shard_map/ppermute | solution.py:349
  6.1 14.7 %slice-start = ((s8[12582912]{0:T(1024)(128)(4,1)}), s8[4194304]{0:T(1024)(128)(4,1)S(1)}, s32[]{:S(2)}) async-start(s8[12582912]{0:T(1024)(128)(4,1)} %bitcast.7), calls=%async_computation | async-start | bytes 8388608
  6.1 14.8 %slice-start.3 = ((s8[12582912]{0:T(1024)(128)(4,1)}), s8[4194304]{0:T(1024)(128)(4,1)S(1)}, s32[]{:S(2)}) async-start(s8[12582912]{0:T(1024)(128)(4,1)} %bitcast.9), calls=%async_computation.3 | async-start | bytes 8388608
  6.1 14.8 %slice-start.1 = ((s8[12582912]{0:T(1024)(128)(4,1)}), s8[4194304]{0:T(1024)(128)(4,1)S(1)}, s32[]{:S(2)}) async-start(s8[12582912]{0:T(1024)(128)(4,1)} %bitcast.7), calls=%async_computation.1 | async-start | bytes 8388608
  6.1 14.8 %slice-start.2 = ((s8[12582912]{0:T(1024)(128)(4,1)}), s8[4194304]{0:T(1024)(128)(4,1)S(1)}, s32[]{:S(2)}) async-start(s8[12582912]{0:T(1024)(128)(4,1)} %bitcast.7), calls=%async_computation.2 | async-start | bytes 8388608
  6.1 14.8 %slice-start.4 = ((s8[12582912]{0:T(1024)(128)(4,1)}), s8[4194304]{0:T(1024)(128)(4,1)S(1)}, s32[]{:S(2)}) async-start(s8[12582912]{0:T(1024)(128)(4,1)} %bitcast.9), calls=%async_computation.4 | async-start | bytes 8388608
  6.1 14.8 %slice-start.5 = ((s8[12582912]{0:T(1024)(128)(4,1)}), s8[4194304]{0:T(1024)(128)(4,1)S(1)}, s32[]{:S(2)}) async-start(s8[12582912]{0:T(1024)(128)(4,1)} %bitcast.9), calls=%async_computation.5 | async-start | bytes 8388608
  6.3 6.0 %collective-permute-start.1 = (bf16[1,16,1408]{2,1,0:T(8,128)(2,1)S(1)}, bf16[1,16,1408]{2,1,0:T(8,128)(2,1)S(1)}, u32[]{:S(2)}, u32[]{:S(2)}) collective-permute-start(bf16[1,16,1408]{2,1,0:T(8,128)(2,1)S(1)} %bitcast.13), channel_id=1, source_target_pairs={{0,8},{2,10},{4,12},{6,14},{8,0},{10,2},{12,4},{14,6},{1,9},{3,11}... | collective-permute-start | bytes 135176 | tf_op jit(solution)/shard_map/ppermute | solution.py:312
  12.4 6.2 %collective-permute-start.4 = (bf16[2,16,1408]{2,1,0:T(8,128)(2,1)S(1)}, bf16[2,16,1408]{2,1,0:T(8,128)(2,1)S(1)}, u32[]{:S(2)}, u32[]{:S(2)}) collective-permute-start(bf16[2,16,1408]{2,1,0:T(8,128)(2,1)S(1)} %shard_map.136.refs_0_.piece_ref), channel_id=1, source_target_pairs={{0,6},{2,4},{4,2},{6,0},{8,14},{10,12},{12,10},{14,8},{1,7},{3,5},... | collective-permute-start | bytes 270344 | tf_op jit(solution)/shard_map/ppermute | solution.py:312
  15.3 4.5 %collective-permute-start.3 = (bf16[2,16,1408]{2,1,0:T(8,128)(2,1)S(1)}, bf16[2,16,1408]{2,1,0:T(8,128)(2,1)S(1)}, u32[]{:S(2)}, u32[]{:S(2)}) collective-permute-start(bf16[2,16,1408]{2,1,0:T(8,128)(2,1)S(1)} %shard_map.136.refs_0_.piece_ref), channel_id=1, source_target_pairs={{0,4},{2,6},{4,0},{6,2},{8,12},{10,14},{12,8},{14,10},{1,5},{3,7},... | collective-permute-start | bytes 270344 | tf_op jit(solution)/shard_map/ppermute | solution.py:312
  16.2 4.5 %collective-permute-start.2 = (bf16[2,16,1408]{2,1,0:T(8,128)(2,1)S(1)}, bf16[2,16,1408]{2,1,0:T(8,128)(2,1)S(1)}, u32[]{:S(2)}, u32[]{:S(2)}) collective-permute-start(bf16[2,16,1408]{2,1,0:T(8,128)(2,1)S(1)} %shard_map.136.refs_0_.piece_ref), channel_id=1, source_target_pairs={{0,2},{2,0},{4,6},{6,4},{8,10},{10,8},{12,14},{14,12},{1,3},{3,1},... | collective-permute-start | bytes 270344 | tf_op jit(solution)/shard_map/ppermute | solution.py:312
  20.8 4.4 %collective-permute-start.5 = (bf16[8,16,1408]{2,1,0:T(8,128)(2,1)S(1)}, bf16[8,16,1408]{2,1,0:T(8,128)(2,1)S(1)}, u32[]{:S(2)}, u32[]{:S(2)}) collective-permute-start(bf16[8,16,1408]{2,1,0:T(8,128)(2,1)S(1)} %shard_map.137.piece_ref.own_ref), channel_id=1, source_target_pairs={{0,1},{1,0},{2,3},{3,2},{4,5},{5,4},{6,7},{7,6},{8,9},{9,8},{10,11... | collective-permute-start | bytes 1081352 | tf_op jit(solution)/shard_map/ppermute | solution.py:377
  23.3 4.3 %slice-start.6 = ((s8[12582912]{0:T(1024)(128)(4,1)}), s8[4194304]{0:T(1024)(128)(4,1)S(1)}, s32[]{:S(2)}) async-start(s8[12582912]{0:T(1024)(128)(4,1)} %bitcast.11), calls=%async_computation.6 | async-start | bytes 8388608
  23.3 4.3 %slice-start.7 = ((s8[12582912]{0:T(1024)(128)(4,1)}), s8[4194304]{0:T(1024)(128)(4,1)S(1)}, s32[]{:S(2)}) async-start(s8[12582912]{0:T(1024)(128)(4,1)} %bitcast.11), calls=%async_computation.7 | async-start | bytes 8388608
  25.2 3.0 %slice-start.8 = ((s8[12582912]{0:T(1024)(128)(4,1)}), s8[4194304]{0:T(1024)(128)(4,1)S(1)}, s32[]{:S(2)}) async-start(s8[12582912]{0:T(1024)(128)(4,1)} %bitcast.11), calls=%async_computation.8 | async-start | bytes 8388608
  30.6 1.8 %collective-permute-start.6 = (bf16[8,8,2560]{2,1,0:T(8,128)(2,1)S(1)}, bf16[8,8,2560]{2,1,0:T(8,128)(2,1)S(1)}, u32[]{:S(2)}, u32[]{:S(2)}) collective-permute-start(bf16[8,8,2560]{2,1,0:T(8,128)(2,1)S(1)} %get-tuple-element.20), channel_id=1, source_target_pairs={{0,1},{1,0},{2,3},{3,2},{4,5},{5,4},{6,7},{7,6},{8,9},{9,8},{10,11... | collective-permute-start | bytes 983048 | tf_op jit(solution)/shard_map/ppermute | solution.py:418
  32.6 6.4 %collective-permute-start.7 = (bf16[2,8,2560]{2,1,0:T(8,128)(2,1)S(1)}, bf16[2,8,2560]{2,1,0:T(8,128)(2,1)S(1)}, u32[]{:S(2)}, u32[]{:S(2)}) collective-permute-start(bf16[2,8,2560]{2,1,0:T(8,128)(2,1)S(1)} %get-tuple-element.23), channel_id=1, source_target_pairs={{0,2},{2,0},{4,6},{6,4},{8,10},{10,8},{12,14},{14,12},{1,3},{3,1},... | collective-permute-start | bytes 245768 | tf_op jit(solution)/shard_map/ppermute | solution.py:312
  33.0 6.2 %collective-permute-start.9 = (bf16[2,8,2560]{2,1,0:T(8,128)(2,1)S(1)}, bf16[2,8,2560]{2,1,0:T(8,128)(2,1)S(1)}, u32[]{:S(2)}, u32[]{:S(2)}) collective-permute-start(bf16[2,8,2560]{2,1,0:T(8,128)(2,1)S(1)} %get-tuple-element.24), channel_id=1, source_target_pairs={{0,6},{2,4},{4,2},{6,0},{8,14},{10,12},{12,10},{14,8},{1,7},{3,5},... | collective-permute-start | bytes 245768 | tf_op jit(solution)/shard_map/ppermute | solution.py:312
  35.2 5.1 %collective-permute-start.8 = (bf16[2,8,2560]{2,1,0:T(8,128)(2,1)S(1)}, bf16[2,8,2560]{2,1,0:T(8,128)(2,1)S(1)}, u32[]{:S(2)}, u32[]{:S(2)}) collective-permute-start(bf16[2,8,2560]{2,1,0:T(8,128)(2,1)S(1)} %get-tuple-element.25), channel_id=1, source_target_pairs={{0,4},{2,6},{4,0},{6,2},{8,12},{10,14},{12,8},{14,10},{1,5},{3,7},... | collective-permute-start | bytes 245768 | tf_op jit(solution)/shard_map/ppermute | solution.py:312
  40.3 5.0 %collective-permute-start.10 = (bf16[1,8,2560]{2,1,0:T(8,128)(2,1)S(1)}, bf16[1,8,2560]{2,1,0:T(8,128)(2,1)S(1)}, u32[]{:S(2)}, u32[]{:S(2)}) collective-permute-start(bf16[1,8,2560]{2,1,0:T(8,128)(2,1)S(1)} %slice.41), channel_id=1, source_target_pairs={{0,8},{2,10},{4,12},{6,14},{8,0},{10,2},{12,4},{14,6},{1,9},{3,11}... | collective-permute-start | bytes 122888 | tf_op jit(solution)/shard_map/ppermute | solution.py:312

commit v6 on v5

--- a/solution.py
+++ b/solution.py
@@ -255,7 +255,7 @@
     ow = width // (SUBL // ht)
     main = acc_ref[pl.ds(0, blocks * br)].reshape(blocks, 2, SUBL, width)
     m0, m1 = main[:, 0], main[:, 1]
-    keep_ref[:, :, pl.ds(0, width)] = jnp.where(s0, m0, m1)
+    keep_ref[:, :, pl.ds(0, width)] = jnp.where(s0, m0, m1).astype(BF16)
     send_ref[:, :, pl.ds(0, width)] = jnp.where(s0, m1, m0).astype(BF16)
     rest = acc_ref[pl.ds(blocks * br, blocks * tail)].astype(BF16)
     for ref, side in ((keep_ref, sub), (send_ref, 1 - sub)):
@@ -407,7 +407,7 @@
         in_specs=[VMEM] * 4,
         out_specs=(VMEM, VMEM),
         out_shape=(
-            jax.ShapeDtypeStruct((n_ep, SUBL, width + ow), F32),
+            jax.ShapeDtypeStruct((n_ep, SUBL, width + ow), BF16),
             jax.ShapeDtypeStruct((n_ep, SUBL, width + ow), BF16),
         ),
         scratch_shapes=[pltpu.VMEM((tokens, width), F32), pltpu.VMEM((tokens, 2 * experts), F32)],
@@ -415,7 +415,7 @@
         name="experts_third",
     )(pieces, others, hidden, down_proj)
 
-    sums = keep + lax.ppermute(send, "sub", swap).astype(F32)
+    sums = keep.astype(F32) + lax.ppermute(send, "sub", swap).astype(F32)
     size = n_ep // (len(near) + 1)
     arrived = []
     for i, m in enumerate(near, 1):

time: 46.1 us -> 46.1 us (level)
  no operation moved by 1% of the time
where the time goes in v6:
time: 46.1 us; the launch traced here: 46 us
  waiting for transfers between devices  15.4 us (33%)
  starting transfers between devices  15.1 us (33%)
  Pallas kernels  14.3 us (31%)
  local copies, waits for them, and re-layouts  0.83 us (2%)
    ppermute x8, starting transfers between devices, to(): return lax.ppermute(x, 'ep', [(i, i ^ m) for i in range(n_ep)])  13.9 us
    ppermute x8, waiting for transfers between devices, to(): return lax.ppermute(x, 'ep', [(i, i ^ m) for i in range(n_ep)])  13.2 us
    pallas_call x1, Pallas kernels, layer(): pl.pallas_call(functools.partial(attention_kernel, n_chunks), in_specs=[H...  4.45 us
    pallas_call x2, Pallas kernels, first_half(): pl.pallas_call(functools.partial(first_half_kernel, chunks, skip), in_spe...  4.22 us
    pallas_call x1, Pallas kernels, layer(): pl.pallas_call(functools.partial(third_kernel, chunks), in_specs=[VMEM] *...  2.48 us
    pallas_call x1, Pallas kernels, layer(): pl.pallas_call(functools.partial(second_half_kernel, chunks), in_specs=[V...  2.35 us
    ppermute x1, waiting for transfers between devices, layer(): sums = keep.astype(F32) + lax.ppermute(send, 'sub', swap).astype(F32)  1.26 us
  transfers between devices with their start and end apart: 11, of which 10 were waited for; matrix products, arithmetic and copies ran while one was open for 0% of the time, Pallas kernels for 9%

profile of v6, /device:TPU:0, one launch (start us, length us, event | category | flops | bytes accessed | tf_op | source)
XLA Modules:
  0.0 46.0 jit_solution(475314497928645035)
XLA Ops:
  0.0 4.5 %attention.1.a_ref = f32[20,2048]{1,0:T(8,128)S(1)} custom-call(s32[20]{0:T(128)} %len_hbm.1, bf16[20,8,128]{2,1,0:T(8,128)(2,1)} %q_hbm.1, bf16[20,128]{1,0:T(8,128)(2,1)} %bitcast.17, bf16[20,128]{1,0:T(8,128)(2,1)} %bitcast.18, bf16[10,2048]{1,0:T(8,128)(2,1)} %res_hbm.1, bf16[20,1,384,128]{3,2,1,0:T(8,128)(2,1)} %k_hbm.1, ...), custom_call_target="tpu_custom_call" | custom-call | tf_op jit(solution)/shard_map/attention/pallas_call | solution.py:314
  4.5 0.6 %collective-permute-start = (f32[20,2048]{1,0:T(8,128)S(1)}, f32[20,2048]{1,0:T(8,128)S(1)}, u32[]{:S(2)}, u32[]{:S(2)}) collective-permute-start(f32[20,2048]{1,0:T(8,128)S(1)} %attention.1.a_ref), channel_id=1, source_target_pairs={{0,1},{1,0},{2,3},{3,2},{4,5},{5,4},{6,7},{7,6},{8,9},{9,8},{10,11... | collective-permute-start | bytes 491528 | tf_op jit(solution)/shard_map/ppermute | solution.py:349
  5.0 0.1 copy.15.route_ref
  5.1 0.1 copy.16.rw_ref
  5.2 0.9 %collective-permute-done.b_ref = f32[20,2048]{1,0:T(8,128)S(1)} collective-permute-done((f32[20,2048]{1,0:T(8,128)S(1)}, f32[20,2048]{1,0:T(8,128)S(1)}, u32[]{:S(2)}, u32[]{:S(2)}) %collective-permute-start) | collective-permute-done | bytes 163872 | tf_op jit(solution)/shard_map/ppermute | solution.py:349
  6.1 0.2 norm.1
  6.3 4.0 %collective-permute-start.1 = (bf16[1,16,1408]{2,1,0:T(8,128)(2,1)S(1)}, bf16[1,16,1408]{2,1,0:T(8,128)(2,1)S(1)}, u32[]{:S(2)}, u32[]{:S(2)}) collective-permute-start(bf16[1,16,1408]{2,1,0:T(8,128)(2,1)S(1)} %bitcast.13), channel_id=1, source_target_pairs={{0,8},{2,10},{4,12},{6,14},{8,0},{10,2},{12,4},{14,6},{1,9},{3,11}... | collective-permute-start | bytes 135176 | tf_op jit(solution)/shard_map/ppermute | solution.py:312
  10.3 2.0 %collective-permute-done.1.refs_1_ = bf16[1,16,1408]{2,1,0:T(8,128)(2,1)S(1)} collective-permute-done((bf16[1,16,1408]{2,1,0:T(8,128)(2,1)S(1)}, bf16[1,16,1408]{2,1,0:T(8,128)(2,1)S(1)}, u32[]{:S(2)}, u32[]{:S(2)}) %collective-permute-start.1) | collective-permute-done | bytes 45088 | tf_op jit(solution)/shard_map/ppermute | solution.py:312
  12.4 2.9 %collective-permute-start.4 = (bf16[2,16,1408]{2,1,0:T(8,128)(2,1)S(1)}, bf16[2,16,1408]{2,1,0:T(8,128)(2,1)S(1)}, u32[]{:S(2)}, u32[]{:S(2)}) collective-permute-start(bf16[2,16,1408]{2,1,0:T(8,128)(2,1)S(1)} %shard_map.136.refs_0_.piece_ref), channel_id=1, source_target_pairs={{0,6},{2,4},{4,2},{6,0},{8,14},{10,12},{12,10},{14,8},{1,7},{3,5},... | collective-permute-start | bytes 270344 | tf_op jit(solution)/shard_map/ppermute | solution.py:312
  15.3 0.9 %collective-permute-start.3 = (bf16[2,16,1408]{2,1,0:T(8,128)(2,1)S(1)}, bf16[2,16,1408]{2,1,0:T(8,128)(2,1)S(1)}, u32[]{:S(2)}, u32[]{:S(2)}) collective-permute-start(bf16[2,16,1408]{2,1,0:T(8,128)(2,1)S(1)} %shard_map.136.refs_0_.piece_ref), channel_id=1, source_target_pairs={{0,4},{2,6},{4,0},{6,2},{8,12},{10,14},{12,8},{14,10},{1,5},{3,7},... | collective-permute-start | bytes 270344 | tf_op jit(solution)/shard_map/ppermute | solution.py:312
  16.2 2.3 %collective-permute-done.4.refs_3_ = bf16[2,16,1408]{2,1,0:T(8,128)(2,1)S(1)} collective-permute-done((bf16[2,16,1408]{2,1,0:T(8,128)(2,1)S(1)}, bf16[2,16,1408]{2,1,0:T(8,128)(2,1)S(1)}, u32[]{:S(2)}, u32[]{:S(2)}) %collective-permute-start.4) | collective-permute-done | bytes 90144 | tf_op jit(solution)/shard_map/ppermute | solution.py:312
  18.6 1.3 %collective-permute-done.3.refs_2_ = bf16[2,16,1408]{2,1,0:T(8,128)(2,1)S(1)} collective-permute-done((bf16[2,16,1408]{2,1,0:T(8,128)(2,1)S(1)}, bf16[2,16,1408]{2,1,0:T(8,128)(2,1)S(1)}, u32[]{:S(2)}, u32[]{:S(2)}) %collective-permute-start.3) | collective-permute-done | bytes 90144 | tf_op jit(solution)/shard_map/ppermute | solution.py:312
  19.8 0.9 %collective-permute-done.2.refs_1_ = bf16[2,16,1408]{2,1,0:T(8,128)(2,1)S(1)} collective-permute-done((bf16[2,16,1408]{2,1,0:T(8,128)(2,1)S(1)}, bf16[2,16,1408]{2,1,0:T(8,128)(2,1)S(1)}, u32[]{:S(2)}, u32[]{:S(2)}) %collective-permute-start.2) | collective-permute-done | bytes 90144 | tf_op jit(solution)/shard_map/ppermute | solution.py:312
  20.8 0.1 collective-permute-start.5
  20.9 2.3 %shard_map.138 = (f32[4,40,768]{2,1,0:T(8,128)S(1)}, f32[4,40,768]{2,1,0:T(8,128)S(1)}) custom-call(bf16[2,16,1408]{2,1,0:T(8,128)(2,1)S(1)} %shard_map.136.refs_0_.piece_ref, bf16[4,2048,768]{2,1,0:T(8,128)(2,1)S(1)} %bitcast.8, bf16[4,2048,768]{2,1,0:T(8,128)(2,1)S(1)} %bitcast.10), custom_call_target="tpu_custom_call" | custom-call | tf_op jit(solution)/shard_map/pallas_call | solution.py:382
  23.3 0.0 slice-start.6
  23.3 1.9 %shard_map.139 = (f32[4,120,768]{2,1,0:T(8,128)S(1)}, f32[4,120,768]{2,1,0:T(8,128)S(1)}) custom-call(bf16[8,16,1408]{2,1,0:T(8,128)(2,1)S(1)} %shard_map.137.piece_ref.own_ref, bf16[4,2048,768]{2,1,0:T(8,128)(2,1)S(1)} %bitcast.8, bf16[4,2048,768]{2,1,0:T(8,128)(2,1)S(1)} %bitcast.10), custom_call_target="tpu_custom_call" | custom-call | tf_op jit(solution)/shard_map/pallas_call | solution.py:382
  25.2 2.3 %experts_second.1.hid_ref = bf16[4,160,768]{2,1,0:T(8,128)(2,1)S(1)} custom-call(bf16[8,16,1408]{2,1,0:T(8,128)(2,1)S(1)} %collective-permute-done.5.oth_ref, f32[4,40,768]{2,1,0:T(8,128)S(1)} %get-tuple-element.15.ga_ref, f32[4,40,768]{2,1,0:T(8,128)S(1)} %get-tuple-element.16.ua_ref, f32[4,120,768]{2,1,0:T(8,128)S(1)} %get-tuple-element.17.gb_ref, ...), custom_call_target="tpu_custom_call" | custom-call | tf_op jit(solution)/shard_map/experts_second/pallas_call | solution.py:394
  27.6 0.6 %slice-done.8 = s8[4194304]{0:T(1024)(128)(4,1)S(1)} async-done(((s8[12582912]{0:T(1024)(128)(4,1)}), s8[4194304]{0:T(1024)(128)(4,1)S(1)}, s32[]{:S(2)}) %slice-start.8) | async-done | bytes 4194328
  28.2 2.5 %experts_third.1 = (bf16[8,8,2560]{2,1,0:T(8,128)(2,1)S(1)}, bf16[8,8,2560]{2,1,0:T(8,128)(2,1)S(1)}) custom-call(bf16[8,16,1408]{2,1,0:T(8,128)(2,1)S(1)} %shard_map.137.piece_ref.own_ref, bf16[8,16,1408]{2,1,0:T(8,128)(2,1)S(1)} %collective-permute-done.5.oth_ref, bf16[4,160,768]{2,1,0:T(8,128)(2,1)S(1)} %experts_second.1.hid_ref, ...), custom_call_target="tpu_custom_call" | custom-call | tf_op jit(solution)/shard_map/experts_third/pallas_call | solution.py:405
  30.6 0.5 %collective-permute-start.6 = (bf16[8,8,2560]{2,1,0:T(8,128)(2,1)S(1)}, bf16[8,8,2560]{2,1,0:T(8,128)(2,1)S(1)}, u32[]{:S(2)}, u32[]{:S(2)}) collective-permute-start(bf16[8,8,2560]{2,1,0:T(8,128)(2,1)S(1)} %get-tuple-element.20), channel_id=1, source_target_pairs={{0,1},{1,0},{2,3},{3,2},{4,5},{5,4},{6,7},{7,6},{8,9},{9,8},{10,11... | collective-permute-start | bytes 983048 | tf_op jit(solution)/shard_map/ppermute | solution.py:418
  31.2 1.3 %collective-permute-done.6 = bf16[8,8,2560]{2,1,0:T(8,128)(2,1)S(1)} collective-permute-done((bf16[8,8,2560]{2,1,0:T(8,128)(2,1)S(1)}, bf16[8,8,2560]{2,1,0:T(8,128)(2,1)S(1)}, u32[]{:S(2)}, u32[]{:S(2)}) %collective-permute-start.6) | collective-permute-done | bytes 327712 | tf_op jit(solution)/shard_map/ppermute | solution.py:418
  32.4 0.1 fusion.2
  32.6 0.5 collective-permute-start.7
  33.0 2.2 %collective-permute-start.9 = (bf16[2,8,2560]{2,1,0:T(8,128)(2,1)S(1)}, bf16[2,8,2560]{2,1,0:T(8,128)(2,1)S(1)}, u32[]{:S(2)}, u32[]{:S(2)}) collective-permute-start(bf16[2,8,2560]{2,1,0:T(8,128)(2,1)S(1)} %get-tuple-element.24), channel_id=1, source_target_pairs={{0,6},{2,4},{4,2},{6,0},{8,14},{10,12},{12,10},{14,8},{1,7},{3,5},... | collective-permute-start | bytes 245768 | tf_op jit(solution)/shard_map/ppermute | solution.py:312
  35.2 0.9 %collective-permute-start.8 = (bf16[2,8,2560]{2,1,0:T(8,128)(2,1)S(1)}, bf16[2,8,2560]{2,1,0:T(8,128)(2,1)S(1)}, u32[]{:S(2)}, u32[]{:S(2)}) collective-permute-start(bf16[2,8,2560]{2,1,0:T(8,128)(2,1)S(1)} %get-tuple-element.25), channel_id=1, source_target_pairs={{0,4},{2,6},{4,0},{6,2},{8,12},{10,14},{12,8},{14,10},{1,5},{3,7},... | collective-permute-start | bytes 245768 | tf_op jit(solution)/shard_map/ppermute | solution.py:312
  36.1 2.9 %collective-permute-done.7 = bf16[2,8,2560]{2,1,0:T(8,128)(2,1)S(1)} collective-permute-done((bf16[2,8,2560]{2,1,0:T(8,128)(2,1)S(1)}, bf16[2,8,2560]{2,1,0:T(8,128)(2,1)S(1)}, u32[]{:S(2)}, u32[]{:S(2)}) %collective-permute-start.7) | collective-permute-done | bytes 81952 | tf_op jit(solution)/shard_map/ppermute | solution.py:312
  39.0 0.2 collective-permute-done.9
  39.2 1.1 %collective-permute-done.8 = bf16[2,8,2560]{2,1,0:T(8,128)(2,1)S(1)} collective-permute-done((bf16[2,8,2560]{2,1,0:T(8,128)(2,1)S(1)}, bf16[2,8,2560]{2,1,0:T(8,128)(2,1)S(1)}, u32[]{:S(2)}, u32[]{:S(2)}) %collective-permute-start.8) | collective-permute-done | bytes 81952 | tf_op jit(solution)/shard_map/ppermute | solution.py:312
  40.3 2.5 %collective-permute-start.10 = (bf16[1,8,2560]{2,1,0:T(8,128)(2,1)S(1)}, bf16[1,8,2560]{2,1,0:T(8,128)(2,1)S(1)}, u32[]{:S(2)}, u32[]{:S(2)}) collective-permute-start(bf16[1,8,2560]{2,1,0:T(8,128)(2,1)S(1)} %slice.41), channel_id=1, source_target_pairs={{0,8},{2,10},{4,12},{6,14},{8,0},{10,2},{12,4},{14,6},{1,9},{3,11}... | collective-permute-start | bytes 122888 | tf_op jit(solution)/shard_map/ppermute | solution.py:312
  42.8 2.5 %collective-permute-done.10 = bf16[1,8,2560]{2,1,0:T(8,128)(2,1)S(1)} collective-permute-done((bf16[1,8,2560]{2,1,0:T(8,128)(2,1)S(1)}, bf16[1,8,2560]{2,1,0:T(8,128)(2,1)S(1)}, u32[]{:S(2)}, u32[]{:S(2)}) %collective-permute-start.10) | collective-permute-done | bytes 40992 | tf_op jit(solution)/shard_map/ppermute | solution.py:312
  45.3 0.7 %finish.1 = bf16[10,2048]{1,0:T(8,128)(2,1)} custom-call(f32[10,2048]{1,0:T(8,128)S(1)} %get-tuple-element.13.stream_ref, f32[8,2560]{1,0:T(8,128)S(1)} %slice_bitcast_fusion.a_ref, bf16[8,2560]{1,0:T(8,128)(2,1)S(1)} %bitcast.15), custom_call_target="tpu_custom_call" | custom-call | tf_op jit(solution)/shard_map/finish/pallas_call | solution.py:436
  (33 shorter events, 0.2 us)
Async XLA Ops:
  0.0 5.0 %copy-start.1 = (s32[10,8]{0,1:T(8,128)S(1)}, s32[10,8]{0,1:T(8,128)}, u32[]{:S(2)}) copy-start(s32[10,8]{0,1:T(8,128)} %param.26) | copy-start | bytes 964
  0.0 5.1 %copy-start.2 = (f32[10,8]{0,1:T(8,128)S(1)}, f32[10,8]{0,1:T(8,128)}, u32[]{:S(2)}) copy-start(f32[10,8]{0,1:T(8,128)} %param.27) | copy-start | bytes 964
  0.0 6.1 %copy-start = (f32[2048]{0:T(1024)S(1)}, f32[2048]{0:T(1024)}, u32[]{:S(2)}) copy-start(f32[2048]{0:T(1024)} %param.22) | copy-start | bytes 24580
  4.5 1.6 %collective-permute-start = (f32[20,2048]{1,0:T(8,128)S(1)}, f32[20,2048]{1,0:T(8,128)S(1)}, u32[]{:S(2)}, u32[]{:S(2)}) collective-permute-start(f32[20,2048]{1,0:T(8,128)S(1)} %attention.1.a_ref), channel_id=1, source_target_pairs={{0,1},{1,0},{2,3},{3,2},{4,5},{5,4},{6,7},{7,6},{8,9},{9,8},{10,11... | collective-permute-start | bytes 491528 | tf_op jit(solution)/shard_map/ppermute | solution.py:349
  6.1 14.7 %slice-start = ((s8[12582912]{0:T(1024)(128)(4,1)}), s8[4194304]{0:T(1024)(128)(4,1)S(1)}, s32[]{:S(2)}) async-start(s8[12582912]{0:T(1024)(128)(4,1)} %bitcast.7), calls=%async_computation | async-start | bytes 8388608
  6.1 14.8 %slice-start.3 = ((s8[12582912]{0:T(1024)(128)(4,1)}), s8[4194304]{0:T(1024)(128)(4,1)S(1)}, s32[]{:S(2)}) async-start(s8[12582912]{0:T(1024)(128)(4,1)} %bitcast.9), calls=%async_computation.3 | async-start | bytes 8388608
  6.1 14.8 %slice-start.1 = ((s8[12582912]{0:T(1024)(128)(4,1)}), s8[4194304]{0:T(1024)(128)(4,1)S(1)}, s32[]{:S(2)}) async-start(s8[12582912]{0:T(1024)(128)(4,1)} %bitcast.7), calls=%async_computation.1 | async-start | bytes 8388608
  6.1 14.8 %slice-start.2 = ((s8[12582912]{0:T(1024)(128)(4,1)}), s8[4194304]{0:T(1024)(128)(4,1)S(1)}, s32[]{:S(2)}) async-start(s8[12582912]{0:T(1024)(128)(4,1)} %bitcast.7), calls=%async_computation.2 | async-start | bytes 8388608
  6.1 14.8 %slice-start.4 = ((s8[12582912]{0:T(1024)(128)(4,1)}), s8[4194304]{0:T(1024)(128)(4,1)S(1)}, s32[]{:S(2)}) async-start(s8[12582912]{0:T(1024)(128)(4,1)} %bitcast.9), calls=%async_computation.4 | async-start | bytes 8388608
  6.1 14.8 %slice-start.5 = ((s8[12582912]{0:T(1024)(128)(4,1)}), s8[4194304]{0:T(1024)(128)(4,1)S(1)}, s32[]{:S(2)}) async-start(s8[12582912]{0:T(1024)(128)(4,1)} %bitcast.9), calls=%async_computation.5 | async-start | bytes 8388608
  6.3 6.0 %collective-permute-start.1 = (bf16[1,16,1408]{2,1,0:T(8,128)(2,1)S(1)}, bf16[1,16,1408]{2,1,0:T(8,128)(2,1)S(1)}, u32[]{:S(2)}, u32[]{:S(2)}) collective-permute-start(bf16[1,16,1408]{2,1,0:T(8,128)(2,1)S(1)} %bitcast.13), channel_id=1, source_target_pairs={{0,8},{2,10},{4,12},{6,14},{8,0},{10,2},{12,4},{14,6},{1,9},{3,11}... | collective-permute-start | bytes 135176 | tf_op jit(solution)/shard_map/ppermute | solution.py:312
  12.4 6.2 %collective-permute-start.4 = (bf16[2,16,1408]{2,1,0:T(8,128)(2,1)S(1)}, bf16[2,16,1408]{2,1,0:T(8,128)(2,1)S(1)}, u32[]{:S(2)}, u32[]{:S(2)}) collective-permute-start(bf16[2,16,1408]{2,1,0:T(8,128)(2,1)S(1)} %shard_map.136.refs_0_.piece_ref), channel_id=1, source_target_pairs={{0,6},{2,4},{4,2},{6,0},{8,14},{10,12},{12,10},{14,8},{1,7},{3,5},... | collective-permute-start | bytes 270344 | tf_op jit(solution)/shard_map/ppermute | solution.py:312
  15.3 4.5 %collective-permute-start.3 = (bf16[2,16,1408]{2,1,0:T(8,128)(2,1)S(1)}, bf16[2,16,1408]{2,1,0:T(8,128)(2,1)S(1)}, u32[]{:S(2)}, u32[]{:S(2)}) collective-permute-start(bf16[2,16,1408]{2,1,0:T(8,128)(2,1)S(1)} %shard_map.136.refs_0_.piece_ref), channel_id=1, source_target_pairs={{0,4},{2,6},{4,0},{6,2},{8,12},{10,14},{12,8},{14,10},{1,5},{3,7},... | collective-permute-start | bytes 270344 | tf_op jit(solution)/shard_map/ppermute | solution.py:312
  16.2 4.5 %collective-permute-start.2 = (bf16[2,16,1408]{2,1,0:T(8,128)(2,1)S(1)}, bf16[2,16,1408]{2,1,0:T(8,128)(2,1)S(1)}, u32[]{:S(2)}, u32[]{:S(2)}) collective-permute-start(bf16[2,16,1408]{2,1,0:T(8,128)(2,1)S(1)} %shard_map.136.refs_0_.piece_ref), channel_id=1, source_target_pairs={{0,2},{2,0},{4,6},{6,4},{8,10},{10,8},{12,14},{14,12},{1,3},{3,1},... | collective-permute-start | bytes 270344 | tf_op jit(solution)/shard_map/ppermute | solution.py:312
  20.8 4.4 %collective-permute-start.5 = (bf16[8,16,1408]{2,1,0:T(8,128)(2,1)S(1)}, bf16[8,16,1408]{2,1,0:T(8,128)(2,1)S(1)}, u32[]{:S(2)}, u32[]{:S(2)}) collective-permute-start(bf16[8,16,1408]{2,1,0:T(8,128)(2,1)S(1)} %shard_map.137.piece_ref.own_ref), channel_id=1, source_target_pairs={{0,1},{1,0},{2,3},{3,2},{4,5},{5,4},{6,7},{7,6},{8,9},{9,8},{10,11... | collective-permute-start | bytes 1081352 | tf_op jit(solution)/shard_map/ppermute | solution.py:377
  23.3 4.3 %slice-start.6 = ((s8[12582912]{0:T(1024)(128)(4,1)}), s8[4194304]{0:T(1024)(128)(4,1)S(1)}, s32[]{:S(2)}) async-start(s8[12582912]{0:T(1024)(128)(4,1)} %bitcast.11), calls=%async_computation.6 | async-start | bytes 8388608
  23.3 4.3 %slice-start.7 = ((s8[12582912]{0:T(1024)(128)(4,1)}), s8[4194304]{0:T(1024)(128)(4,1)S(1)}, s32[]{:S(2)}) async-start(s8[12582912]{0:T(1024)(128)(4,1)} %bitcast.11), calls=%async_computation.7 | async-start | bytes 8388608
  25.2 3.0 %slice-start.8 = ((s8[12582912]{0:T(1024)(128)(4,1)}), s8[4194304]{0:T(1024)(128)(4,1)S(1)}, s32[]{:S(2)}) async-start(s8[12582912]{0:T(1024)(128)(4,1)} %bitcast.11), calls=%async_computation.8 | async-start | bytes 8388608
  30.6 1.8 %collective-permute-start.6 = (bf16[8,8,2560]{2,1,0:T(8,128)(2,1)S(1)}, bf16[8,8,2560]{2,1,0:T(8,128)(2,1)S(1)}, u32[]{:S(2)}, u32[]{:S(2)}) collective-permute-start(bf16[8,8,2560]{2,1,0:T(8,128)(2,1)S(1)} %get-tuple-element.20), channel_id=1, source_target_pairs={{0,1},{1,0},{2,3},{3,2},{4,5},{5,4},{6,7},{7,6},{8,9},{9,8},{10,11... | collective-permute-start | bytes 983048 | tf_op jit(solution)/shard_map/ppermute | solution.py:418
  32.6 6.4 %collective-permute-start.7 = (bf16[2,8,2560]{2,1,0:T(8,128)(2,1)S(1)}, bf16[2,8,2560]{2,1,0:T(8,128)(2,1)S(1)}, u32[]{:S(2)}, u32[]{:S(2)}) collective-permute-start(bf16[2,8,2560]{2,1,0:T(8,128)(2,1)S(1)} %get-tuple-element.23), channel_id=1, source_target_pairs={{0,2},{2,0},{4,6},{6,4},{8,10},{10,8},{12,14},{14,12},{1,3},{3,1},... | collective-permute-start | bytes 245768 | tf_op jit(solution)/shard_map/ppermute | solution.py:312
  33.0 6.2 %collective-permute-start.9 = (bf16[2,8,2560]{2,1,0:T(8,128)(2,1)S(1)}, bf16[2,8,2560]{2,1,0:T(8,128)(2,1)S(1)}, u32[]{:S(2)}, u32[]{:S(2)}) collective-permute-start(bf16[2,8,2560]{2,1,0:T(8,128)(2,1)S(1)} %get-tuple-element.24), channel_id=1, source_target_pairs={{0,6},{2,4},{4,2},{6,0},{8,14},{10,12},{12,10},{14,8},{1,7},{3,5},... | collective-permute-start | bytes 245768 | tf_op jit(solution)/shard_map/ppermute | solution.py:312
  35.2 5.1 %collective-permute-start.8 = (bf16[2,8,2560]{2,1,0:T(8,128)(2,1)S(1)}, bf16[2,8,2560]{2,1,0:T(8,128)(2,1)S(1)}, u32[]{:S(2)}, u32[]{:S(2)}) collective-permute-start(bf16[2,8,2560]{2,1,0:T(8,128)(2,1)S(1)} %get-tuple-element.25), channel_id=1, source_target_pairs={{0,4},{2,6},{4,0},{6,2},{8,12},{10,14},{12,8},{14,10},{1,5},{3,7},... | collective-permute-start | bytes 245768 | tf_op jit(solution)/shard_map/ppermute | solution.py:312
  40.3 5.0 %collective-permute-start.10 = (bf16[1,8,2560]{2,1,0:T(8,128)(2,1)S(1)}, bf16[1,8,2560]{2,1,0:T(8,128)(2,1)S(1)}, u32[]{:S(2)}, u32[]{:S(2)}) collective-permute-start(bf16[1,8,2560]{2,1,0:T(8,128)(2,1)S(1)} %slice.41), channel_id=1, source_target_pairs={{0,8},{2,10},{4,12},{6,14},{8,0},{10,2},{12,4},{14,6},{1,9},{3,11}... | collective-permute-start | bytes 122888 | tf_op jit(solution)/shard_map/ppermute | solution.py:312
